TPU v7x, 32 devices: a whole 2x2x4 slice. The times are simulated.
32 devices in a mesh: grp: 4 (over y, x), wide: 8 (over z, core).
Axes of the slice: x: 2, y: 2, z: 4, core: 2. Of those that a mesh axis runs over, the one named last changes fastest.
Arguments:
- fine_pop: float32 [64, 19, 4096], P(('grp', 'wide')), may hold values from 0 to 1, as said below
- coarse_pop: float32 [19, 32, 8, 1024], P(None, 'grp', None, 'wide'), may hold values from 0 to 1, as said below
- new_slot: int32 [64], replicated, may hold values from 0 to 63, each once
Outputs:
- fine_out: float32 [64, 19, 4096], P(('grp', 'wide'))
- coarse_out: float32 [19, 32, 8, 1024], P(None, 'grp', None, 'wide')
Inputs may be any that keep to these rules, and one draw needn't show every extreme that they name: A permutation: fine block b moves to slot new_slot[b]. `fine_pop`: positive populations near equilibrium, densities of order one, speeds under 0.25. `coarse_pop`: positive populations near equilibrium, densities of order one, speeds under 0.25.
All inputs are finite; a program needn't handle non-finite values.
Results may differ from a plain program's by a relative error of at most 0.00002.
Values sent between devices are 32-bit elements; how exact they have to be, the bound alone decides.
No kernel may reach another device: no remote copies, remote signals or barrier semaphores. Data moves between devices by JAX's collectives and lax.ppermute only.
A program may use at most 128 MiB of HBM per device.

v0:
```python
import functools

import jax
import jax.numpy as jnp
from jax import lax
from jax.experimental import pallas as pl
from jax.experimental.pallas import tpu as pltpu
from jax.sharding import PartitionSpec as P

B = 16
LANES = 128
SUB = 8
HALO = 4
PAD = 8

VELOCITIES = (
    (0, 0, 0),
    (1, 0, 0),
    (-1, 0, 0),
    (0, 1, 0),
    (0, -1, 0),
    (0, 0, 1),
    (0, 0, -1),
    (1, 1, 0),
    (-1, -1, 0),
    (1, -1, 0),
    (-1, 1, 0),
    (1, 0, 1),
    (-1, 0, -1),
    (1, 0, -1),
    (-1, 0, 1),
    (0, 1, 1),
    (0, -1, -1),
    (0, 1, -1),
    (0, -1, 1),
)
Q = len(VELOCITIES)
WEIGHTS = (1.0 / 3.0,) + (1.0 / 18.0,) * 6 + (1.0 / 36.0,) * 12
W_AXIS = WEIGHTS[1]
W_DIAG = WEIGHTS[7]
COUPLING = -5.0
FINE_TAU = 1.1
COARSE_TAU = 0.8
TO_COARSE = 2.0 * COARSE_TAU / FINE_TAU
TO_FINE = FINE_TAU / (2.0 * COARSE_TAU)
UP = tuple(i for i in range(Q) if VELOCITIES[i][1] == 1)
DOWN = tuple(i for i in range(Q) if VELOCITIES[i][1] == -1)
NG = len(UP) + 1

VMEM = pl.BlockSpec(memory_space=pltpu.VMEM)
SMEM = pl.BlockSpec(memory_space=pltpu.SMEM)


def call(body, outs, specs, scratch=(), flops=10**6, moved=10**6):
    return pl.pallas_call(
        body,
        out_shape=outs,
        in_specs=specs,
        out_specs=jax.tree.map(lambda _: VMEM, outs),
        scratch_shapes=list(scratch),
        cost_estimate=pl.CostEstimate(flops=flops, bytes_accessed=moved, transcendentals=0),
    )


def f32(*shape):
    return jax.ShapeDtypeStruct(shape, jnp.float32)


def moments(f):
    density = f[0]
    momentum = [None, None, None]
    for i in range(1, Q, 2):
        density = density + (f[i] + f[i + 1])
        odd = f[i] - f[i + 1]
        for j in range(3):
            c = VELOCITIES[i][j]
            if c:
                term = odd if c > 0 else -odd
                if momentum[j] is None:
                    momentum[j] = term
                else:
                    momentum[j] = momentum[j] + odd if c > 0 else momentum[j] - odd
    return density, momentum


def balances(density, u, scale):
    base = 1.0 - 1.5 * (u[0] * u[0] + u[1] * u[1] + u[2] * u[2])
    scaled = {w: density * (w * scale) for w in set(WEIGHTS)}
    yield 0, scaled[WEIGHTS[0]] * base
    for i in range(1, Q, 2):
        along = None
        for j in range(3):
            c = VELOCITIES[i][j]
            if c:
                if along is None:
                    along = u[j] if c > 0 else -u[j]
                else:
                    along = along + u[j] if c > 0 else along - u[j]
        weight = scaled[WEIGHTS[i]]
        even = weight * (base + 4.5 * (along * along))
        odd = weight * (3.0 * along)
        yield i, even + odd
        yield i + 1, even - odd


def rescaled(f, factor, wanted):
    density, momentum = moments(f)
    inverse = 1.0 / density
    u = [m * inverse for m in momentum]
    found = {}
    for i, balance in balances(density, u, 1.0):
        if i in wanted:
            found[i] = balance + factor * (f[i] - balance)
    return 1.0 - jnp.exp(-density), found


def gradient_parts(p, shift_y, shift_z):
    above = shift_y(p, -1, "p")
    below = shift_y(p, 1, "p")
    front = shift_z(p, -1)
    back = shift_z(p, 1)
    n = range(len(p))
    dy = [above[q] - below[q] for q in n]
    sy = [above[q] + below[q] for q in n]
    dz = [front[q] - back[q] for q in n]
    tx = [W_AXIS * p[q] + W_DIAG * (sy[q] + (front[q] + back[q])) for q in n]
    mixed = [W_AXIS * p[q] + W_DIAG * sy[q] for q in n]
    mixed_front = shift_z(mixed, -1)
    mixed_back = shift_z(mixed, 1)
    dy_front = shift_z(dy, -1)
    dy_back = shift_z(dy, 1)
    gy = [W_AXIS * dy[q] + W_DIAG * (dy_front[q] + dy_back[q]) for q in n]
    gz = [mixed_front[q] - mixed_back[q] for q in n]
    return tx, [W_DIAG * v for v in dy], [W_DIAG * v for v in dz], gy, gz


def velocity_of(density, momentum, potential, pull, tau):
    inverse = 1.0 / density
    force = (-tau * COUPLING) * potential
    return [(momentum[j] + force * pull[j]) * inverse for j in range(3)]


def regroup_body(blocks, k_blocks, rows, slot_ref, in_ref, out_ref):
    def step(b, carry):
        s = slot_ref[b]
        source = (b // k_blocks) * (rows * k_blocks) + b % k_blocks
        target = (s // k_blocks) * (rows * k_blocks) + s % k_blocks
        out_ref[pl.ds(target, rows, stride=k_blocks), :] = in_ref[
            pl.ds(source, rows, stride=k_blocks), :
        ]
        return carry

    lax.fori_loop(0, blocks, step, 0, unroll=4)


def lane_ids():
    lane = lax.broadcasted_iota(jnp.int32, (SUB, LANES), 1)
    return lane % B, lane // B


def fine_shifts(ch_count, k_count, ghost):
    y, z = lane_ids()
    first_y, last_y = y == 0, y == B - 1
    first_z, last_z = z == 0, z == LANES // B - 1

    def shift_y(v, c, which):
        out = []
        for ch in range(ch_count):
            for k in range(k_count):
                q = ch * k_count + k
                if c > 0:
                    own = pltpu.roll(v[q], 1, 1)
                    carry = (
                        ghost(0, which, ch) if k == 0 else pltpu.roll(v[q - 1], LANES - (B - 1), 1)
                    )
                    out.append(jnp.where(first_y, carry, own))
                else:
                    own = pltpu.roll(v[q], LANES - 1, 1)
                    carry = (
                        ghost(1, which, ch)
                        if k == k_count - 1
                        else pltpu.roll(v[q + 1], B - 1, 1)
                    )
                    out.append(jnp.where(last_y, carry, own))
        return out

    def shift_z(v, c):
        rolled = [pltpu.roll(x, B if c > 0 else LANES - B, 1) for x in v]
        edge = first_z if c > 0 else last_z
        out = []
        for ch in range(ch_count):
            other = (ch - c) % ch_count
            for k in range(k_count):
                q = ch * k_count + k
                out.append(jnp.where(edge, rolled[other * k_count + k], rolled[q]))
        return out

    return shift_y, shift_z


def fine_step(src, offset, dst, ghosts, parts, ch_count, k_count, chunks):
    nq = ch_count * k_count
    qs = range(nq)
    for chunk in range(chunks):
        r = chunk * SUB
        f = [[src[i, q, pl.ds(offset + r, SUB), :] for i in range(Q)] for q in qs]
        moved = [moments(f[q]) for q in qs]
        p = [1.0 - jnp.exp(-moved[q][0]) for q in qs]

        def ghost(side, which, ch, r=r):
            return ghosts[side, NG - 1, ch, pl.ds(r, SUB), :]

        shift_y, shift_z = fine_shifts(ch_count, k_count, ghost)
        tx, dy, dz, gy, gz = gradient_parts(p, shift_y, shift_z)
        for q in qs:
            values = (tx[q], dy[q], dz[q], gy[q], gz[q], p[q], moved[q][0], *moved[q][1])
            for n, v in enumerate(values):
                parts[n, q, pl.ds(PAD + r, SUB), :] = v
    for chunk in range(chunks):
        r = chunk * SUB

        def ghost(side, which, ch, r=r):
            place = (UP if side == 0 else DOWN).index(which)
            return ghosts[side, place, ch, pl.ds(r, SUB), :]

        shift_y, shift_z = fine_shifts(ch_count, k_count, ghost)
        density, streams = [], []
        for q in qs:
            low = [parts[n, q, pl.ds(PAD + r - 1, SUB), :] for n in range(3)]
            high = [parts[n, q, pl.ds(PAD + r + 1, SUB), :] for n in range(3)]
            gy, gz, p, rho, mx, my, mz = (
                parts[n, q, pl.ds(PAD + r, SUB), :] for n in range(3, 10)
            )
            pull = [high[0] - low[0], gy + (high[1] + low[1]), gz + (high[2] + low[2])]
            u = velocity_of(rho, (mx, my, mz), p, pull, FINE_TAU)
            streams.append(balances(rho, u, 1.0 / FINE_TAU))
        for i in range(Q):
            cx, cy, cz = VELOCITIES[i]
            post = []
            for q in qs:
                _, balance = next(streams[q])
                h = src[i, q, pl.ds(offset + r, SUB), :]
                post.append(h * (1.0 - 1.0 / FINE_TAU) + balance)
            if cy:
                post = shift_y(post, cy, i)
            if cz:
                post = shift_z(post, cz)
            for q in qs:
                dst[i, q, pl.ds(PAD + r + cx, SUB), :] = post[q]


def fine_body(ch_count, k_count, own, left, right, ghosts, out, first, second, third, parts):
    nq = ch_count * k_count

    def gather(i, carry):
        for q in range(nq):
            first[i, q, pl.ds(0, HALO), :] = left[pl.ds(i * (HALO * nq) + q, HALO, stride=nq), :]
            first[i, q, pl.ds(HALO, B), :] = own[pl.ds(i * (B * nq) + q, B, stride=nq), :]
            first[i, q, pl.ds(HALO + B, HALO), :] = right[
                pl.ds(i * (HALO * nq) + q, HALO, stride=nq), :
            ]
        return carry

    lax.fori_loop(0, Q, gather, 0)
    chunks = (B + 2 * HALO) // SUB
    fine_step(first, 0, second, ghosts, parts, ch_count, k_count, chunks)
    fine_step(second, PAD, third, ghosts, parts, ch_count, k_count, chunks)

    def scatter(i, carry):
        for q in range(nq):
            out[pl.ds(i * (B * nq) + q, B, stride=nq), :] = third[i, q, pl.ds(PAD + HALO, B), :]
        return carry

    lax.fori_loop(0, Q, scatter, 0)


def fine_ghost_body(ch_count, rows, layers, spread, out, wide):
    for side in range(2):
        wide[...] = jnp.dot(
            layers[side],
            spread[...],
            precision=lax.Precision.HIGHEST,
            preferred_element_type=jnp.float32,
        )
        wanted = UP if side == 0 else DOWN
        for ch in range(ch_count):
            for r in range(0, rows, SUB):
                f = [
                    wide[pl.ds(i * rows + r, SUB), pl.ds(ch * LANES, LANES)] for i in range(Q)
                ]
                potential, found = rescaled(f, TO_FINE, wanted)
                for n, i in enumerate(wanted):
                    out[side, n, ch, pl.ds(r, SUB), :] = found[i]
                out[side, NG - 1, ch, pl.ds(r, SUB), :] = potential


STRIDE = 32
PER = LANES // STRIDE


def restrict_body(ch_count, k_count, own, left, right, out, buffer):
    nq = ch_count * k_count
    row = lax.broadcasted_iota(jnp.int32, (LANES, LANES), 0)
    col = lax.broadcasted_iota(jnp.int32, (LANES, LANES), 1)
    for side in range(2):
        k = k_count - 1 if side == 0 else 0
        y = row % B
        picked = (y >= B - 2) if side == 0 else (y < 2)
        total = None
        for ch in range(ch_count):
            q = ch * k_count + k

            def gather(i, carry, ch=ch, q=q):
                at = i * STRIDE
                buffer[ch, pl.ds(at, HALO), :] = left[
                    pl.ds(i * (HALO * nq) + q, HALO, stride=nq), :
                ]
                buffer[ch, pl.ds(at + HALO, B), :] = own[pl.ds(i * (B * nq) + q, B, stride=nq), :]
                buffer[ch, pl.ds(at + HALO + B, HALO), :] = right[
                    pl.ds(i * (HALO * nq) + q, HALO, stride=nq), :
                ]
                buffer[ch, pl.ds(at + 2 * HALO + B, STRIDE - 2 * HALO - B), :] = jnp.zeros(
                    (STRIDE - 2 * HALO - B, LANES), jnp.float32
                )
                return carry

            lax.fori_loop(0, Q, gather, 0)
            coarse_z = ch * (LANES // B // 2) + row // (2 * B)
            select = jnp.where(picked & (coarse_z == col), 0.125, 0.0).astype(jnp.float32)
            part = jnp.dot(
                buffer[ch, pl.ds(0, Q * STRIDE), :],
                select,
                precision=lax.Precision.HIGHEST,
                preferred_element_type=jnp.float32,
            )
            total = part if total is None else total + part
        for n in range(pl.cdiv(Q, PER)):
            count = min(PER, Q - n * PER) * STRIDE
            block = total[n * LANES : n * LANES + count]
            if count < LANES:
                block = jnp.concatenate(
                    [block, jnp.zeros((LANES - count, LANES), jnp.float32)], axis=0
                )
            out[side, n] = block.T[:SUB]


def coarse_body(planes, state, low, high, out, ghosts, parts):
    lane = lax.broadcasted_iota(jnp.int32, (SUB, LANES), 1)
    first_y, last_y = lane == 0, lane == LANES - 1

    for side, ref in enumerate((low, high)):
        paired = []
        for n in range(pl.cdiv(Q, PER)):
            v = ref[n]
            paired.append(v + pltpu.roll(v, LANES - 1, 1))
        f = []
        for i in range(Q):
            s = (i % PER) * STRIDE
            f.append(paired[i // PER] if s == 0 else pltpu.roll(paired[i // PER], LANES - s, 1))
        wanted = UP if side == 0 else DOWN
        potential, found = rescaled(f, TO_COARSE, wanted)
        for n, v in enumerate([found[i] for i in wanted] + [potential]):
            for x in range(planes):
                ghosts[side, n, x] = jnp.broadcast_to(v[:, 2 * x : 2 * x + 1], (SUB, LANES))

    def shifts(x):
        def shift_y(v, c, which):
            side = 0 if c > 0 else 1
            place = NG - 1 if which == "p" else (UP if c > 0 else DOWN).index(which)
            carry = ghosts[side, place, x]
            own = pltpu.roll(v[0], 1 if c > 0 else LANES - 1, 1)
            return [jnp.where(first_y if c > 0 else last_y, carry, own)]

        def shift_z(v, c):
            return [pltpu.roll(v[0], 1 if c > 0 else SUB - 1, 0)]

        return shift_y, shift_z

    def prepare(x, carry):
        density, momentum = moments([state[i, x] for i in range(Q)])
        p = 1.0 - jnp.exp(-density)
        values = gradient_parts([p], *shifts(x))
        values = [v[0] for v in values] + [p, density, *momentum]
        for n, v in enumerate(values):
            parts[n, x] = v
        return carry

    lax.fori_loop(0, planes, prepare, 0, unroll=2)

    inner = planes - 2 * (HALO // 2)
    base = HALO // 2

    def update(x, carry):
        shift_y, shift_z = shifts(x)
        lower = [parts[n, x - 1] for n in range(3)]
        upper = [parts[n, x + 1] for n in range(3)]
        gy, gz, p, rho, mx, my, mz = (parts[n, x] for n in range(3, 10))
        pull = [upper[0] - lower[0], gy + (upper[1] + lower[1]), gz + (upper[2] + lower[2])]
        u = velocity_of(rho, (mx, my, mz), p, pull, COARSE_TAU)
        for i, balance in balances(rho, u, 1.0 / COARSE_TAU):
            cx, cy, cz = VELOCITIES[i]
            post = [state[i, x] * (1.0 - 1.0 / COARSE_TAU) + balance]
            if cy:
                post = shift_y(post, cy, i)
            if cz:
                post = shift_z(post, cz)
            out[i, x + cx] = post[0]
        return carry

    lax.fori_loop(base - 1, base + inner + 1, update, 0, unroll=2)


def ring(axis, count, step):
    return [(i, (i + step) % count) for i in range(count)]


def local(fine_pop, coarse_pop, new_slot):
    k_count, q_count, cells = fine_pop.shape
    blocks = new_slot.shape[0]
    devices = blocks // k_count
    tiles = cells // LANES
    ch_count = tiles // B
    nq = ch_count * k_count
    axes = ("grp", "wide")
    n_grp, n_wide = lax.axis_size("grp"), lax.axis_size("wide")
    _, cx, cz, cy = coarse_pop.shape
    planes = cx + HALO
    fine_rows = B + 2 * HALO

    rows = pl.cdiv(Q * tiles, devices)
    pieces = fine_pop.reshape(k_count, Q, tiles, LANES).transpose(1, 2, 0, 3)
    pieces = pieces.reshape(Q * tiles, k_count, LANES)
    if rows * devices != Q * tiles:
        pieces = jnp.pad(pieces, ((0, rows * devices - Q * tiles), (0, 0), (0, 0)))
    pieces = pieces.reshape(devices, rows, k_count, LANES)
    spread = lax.all_to_all(pieces, axes, 0, 0, tiled=True)
    total = devices * rows * k_count
    regroup = call(
        functools.partial(regroup_body, blocks, k_count, rows),
        f32(total, LANES),
        [SMEM, VMEM],
        moved=8 * total * LANES,
    )
    outgoing = regroup(new_slot, spread.reshape(total, LANES))
    arrived = lax.all_to_all(
        outgoing.reshape(devices, rows, k_count, LANES), axes, 0, 0, tiled=True
    )
    own = arrived.reshape(total, LANES)[: Q * tiles * k_count]

    edge = HALO // 2
    coarse_left = lax.ppermute(coarse_pop[:, cx - edge :], "grp", ring("grp", n_grp, 1))
    coarse_right = lax.ppermute(coarse_pop[:, :edge], "grp", ring("grp", n_grp, -1))
    coarse = jnp.concatenate([coarse_left, coarse_pop, coarse_right], axis=1)
    below = lax.ppermute(coarse[..., -1], "wide", ring("wide", n_wide, 1))
    layers = jnp.repeat(jnp.stack([below, coarse[..., 0]]), 2, axis=2)
    layers = layers.reshape(2, Q * fine_rows, cz)
    lane = jnp.arange(ch_count * LANES) // (2 * B)
    one_hot = (jnp.arange(cz)[:, None] == lane[None, :]).astype(jnp.float32)
    fine_ghosts = call(
        functools.partial(fine_ghost_body, ch_count, fine_rows),
        f32(2, NG, ch_count, fine_rows, LANES),
        [VMEM, VMEM],
        [pltpu.VMEM((Q * fine_rows, ch_count * LANES), jnp.float32)],
    )(layers, one_hot)

    by_x = own.reshape(Q, B * nq, LANES)
    width = HALO * nq
    left = lax.ppermute(by_x[:, -width:], "grp", ring("grp", n_grp, 1)).reshape(Q * width, LANES)
    right = lax.ppermute(by_x[:, :width], "grp", ring("grp", n_grp, -1)).reshape(Q * width, LANES)

    groups = pl.cdiv(Q, PER)
    restricted = call(
        functools.partial(restrict_body, ch_count, k_count),
        f32(2, groups, SUB, LANES),
        [VMEM, VMEM, VMEM],
        [pltpu.VMEM((ch_count, Q * STRIDE, LANES), jnp.float32)],
    )(own, left, right)
    high = lax.ppermute(restricted[1], "wide", ring("wide", n_wide, -1))

    padded = PAD + fine_rows + PAD
    fine = call(
        functools.partial(fine_body, ch_count, k_count),
        f32(Q * B * nq, LANES),
        [VMEM] * 4,
        [
            pltpu.VMEM((Q, nq, fine_rows, LANES), jnp.float32),
            pltpu.VMEM((Q, nq, padded, LANES), jnp.float32),
            pltpu.VMEM((Q, nq, padded, LANES), jnp.float32),
            pltpu.VMEM((10, nq, padded, LANES), jnp.float32),
        ],
        flops=10**7,
    )(own, left, right, fine_ghosts)

    coarse_new = call(
        functools.partial(coarse_body, planes),
        f32(Q, planes, cz, cy),
        [VMEM] * 3,
        [
            pltpu.VMEM((2, NG, planes, SUB, LANES), jnp.float32),
            pltpu.VMEM((10, planes, SUB, LANES), jnp.float32),
        ],
        flops=10**7,
    )(coarse, restricted[0], high)
    coarse_out = coarse_new[:, edge : edge + cx]

    fine_out = fine.reshape(Q, tiles, k_count, LANES).transpose(2, 0, 1, 3)
    fine_out = fine_out.reshape(k_count, q_count, cells)
    return fine_out, coarse_out


def solution(mesh):
    return jax.shard_map(
        local,
        mesh=mesh,
        in_specs=(P(("grp", "wide"), None, None), P(None, "grp", None, "wide"), P()),
        out_specs=(P(("grp", "wide"), None, None), P(None, "grp", None, "wide")),
        check_vma=False,
    )
```

profile of v0, /device:TPU:0, one launch (start us, length us, event | category | flops | bytes accessed | tf_op | source)
XLA Modules:
  0.0 84.2 jit_solution(17931130229381071264)
XLA Ops:
  0.6 1.6 %reshape.41 = f32[2,19,32,128]{3,2,0,1:T(8,128)S(1)} reshape(f32[2,19,4096]{2,0,1:T(2,128)} %param.3) | data formatting | bytes 1245184 | tf_op jit(solution)/shard_map/reshape | solution.py:431
  2.2 0.5 copy.12
  2.7 25.6 %all_to_all.10 = f32[32,19,2,128]{3,2,1,0:T(2,128)} all-to-all(f32[32,19,2,128]{3,2,1,0:T(2,128)S(1)} %bitcast.27), channel_id=1, replica_groups=mesh['grp'=4,'wide'=8] {'grp','wide'}, dimensions={0} | all-to-all | bytes 1245184 | tf_op jit(solution)/shard_map/all_to_all | solution.py:436
  28.3 2.8 %shard_map.50 = f32[1216,128]{1,0:T(8,128)} custom-call(s32[64]{0:T(128)} %slot_ref.1, f32[1216,128]{1,0:T(8,128)} %bitcast.28), custom_call_target="tpu_custom_call" | custom-call | flops 1000000 | bytes 1245184 | tf_op jit(solution)/shard_map/pallas_call | solution.py:444
  31.1 2.7 %all-to-all-start.1 = ((f32[32,19,2,128]{3,2,1,0:T(2,128)}), f32[32,19,2,128]{3,2,1,0:T(2,128)S(1)}, u32[]{:S(2)}, u32[]{:S(2)}) async-start(f32[32,19,2,128]{3,2,1,0:T(2,128)} %bitcast.26), calls=%async_computation.1 | async-start | bytes 1245184 | tf_op jit(solution)/shard_map/all_to_all | solution.py:445
  33.9 1.7 %collective-permute-start.2 = (f32[19,2,8,128]{3,2,1,0:T(8,128)S(1)}, f32[19,2,8,128]{3,2,1,0:T(8,128)S(1)}, u32[]{:S(2)}, u32[]{:S(2)}) collective-permute-start(f32[19,2,8,128]{3,2,1,0:T(8,128)S(1)} %get-tuple-element.5), channel_id=1, source_target_pairs={{0,8},{8,16},{16,24},{24,0},{1,9},{9,17},{17,25},{25,1},{2,10},{10... | collective-permute-start | bytes 466952 | tf_op jit(solution)/shard_map/ppermute | solution.py:451
  35.6 1.3 %collective-permute-start.3 = (f32[19,2,8,128]{3,2,1,0:T(8,128)S(1)}, f32[19,2,8,128]{3,2,1,0:T(8,128)S(1)}, u32[]{:S(2)}, u32[]{:S(2)}) collective-permute-start(f32[19,2,8,128]{3,2,1,0:T(8,128)S(1)} %get-tuple-element.4), channel_id=1, source_target_pairs={{0,24},{8,0},{16,8},{24,16},{1,25},{9,1},{17,9},{25,17},{2,26},{10... | collective-permute-start | bytes 466952 | tf_op jit(solution)/shard_map/ppermute | solution.py:452
  36.8 0.6 fusion.spread
  37.4 8.5 %collective-permute-done.2 = f32[19,2,8,128]{3,2,1,0:T(8,128)S(1)} collective-permute-done((f32[19,2,8,128]{3,2,1,0:T(8,128)S(1)}, f32[19,2,8,128]{3,2,1,0:T(8,128)S(1)}, u32[]{:S(2)}, u32[]{:S(2)}) %collective-permute-start.2) | collective-permute-done | bytes 155680 | tf_op jit(solution)/shard_map/ppermute | solution.py:451
  46.0 3.0 %collective-permute-done.3 = f32[19,2,8,128]{3,2,1,0:T(8,128)S(1)} collective-permute-done((f32[19,2,8,128]{3,2,1,0:T(8,128)S(1)}, f32[19,2,8,128]{3,2,1,0:T(8,128)S(1)}, u32[]{:S(2)}, u32[]{:S(2)}) %collective-permute-start.3) | collective-permute-done | bytes 155680 | tf_op jit(solution)/shard_map/ppermute | solution.py:452
  49.1 3.1 %all-to-all-done.1 = f32[32,19,2,128]{3,2,1,0:T(2,128)S(1)} async-done(((f32[32,19,2,128]{3,2,1,0:T(2,128)}), f32[32,19,2,128]{3,2,1,0:T(2,128)S(1)}, u32[]{:S(2)}, u32[]{:S(2)}) %all-to-all-start.1) | async-done | bytes 622624 | tf_op jit(solution)/shard_map/all_to_all | solution.py:445
  52.2 0.8 fusion.3
  53.0 0.0 collective-permute-start
  53.0 2.9 %collective-permute-start.1 = (f32[19,16,128]{2,1,0:T(8,128)}, f32[19,16,128]{2,1,0:T(8,128)}, u32[]{:S(2)}, u32[]{:S(2)}) collective-permute-start(f32[19,16,128]{2,1,0:T(8,128)} %get-tuple-element.6), channel_id=1, source_target_pairs={{0,24},{8,0},{16,8},{24,16},{1,25},{9,1},{17,9},{25,17},{2,26},{10... | collective-permute-start | bytes 466952 | tf_op jit(solution)/shard_map/ppermute | solution.py:469
  55.9 0.3 fusion.1
  56.3 0.7 copy.14
  57.0 0.7 copy.13
  57.7 0.0 collective-permute-start.4
  57.8 3.3 %collective-permute-done = f32[19,16,128]{2,1,0:T(8,128)} collective-permute-done((f32[19,16,128]{2,1,0:T(8,128)}, f32[19,16,128]{2,1,0:T(8,128)}, u32[]{:S(2)}, u32[]{:S(2)}) %collective-permute-start) | collective-permute-done | bytes 155680 | tf_op jit(solution)/shard_map/ppermute | solution.py:468
  61.1 1.9 %collective-permute-done.1 = f32[19,16,128]{2,1,0:T(8,128)} collective-permute-done((f32[19,16,128]{2,1,0:T(8,128)}, f32[19,16,128]{2,1,0:T(8,128)}, u32[]{:S(2)}, u32[]{:S(2)}) %collective-permute-start.1) | collective-permute-done | bytes 155680 | tf_op jit(solution)/shard_map/ppermute | solution.py:469
  63.0 4.7 %shard_map.53 = f32[2,5,8,128]{3,2,1,0:T(8,128)} custom-call(f32[1216,128]{1,0:T(8,128)} %bitcast.24, f32[304,128]{1,0:T(8,128)} %bitcast.6.left, f32[304,128]{1,0:T(8,128)} %bitcast.7.right), custom_call_target="tpu_custom_call" | custom-call | flops 1000000 | bytes 1000000 | tf_op jit(solution)/shard_map/pallas_call | solution.py:472
  67.7 1.3 %slice_bitcast_fusion = (f32[5,8,128]{2,1,0:T(8,128)S(1)}, f32[5,8,128]{2,1,0:T(8,128)}) fusion(f32[2,5,8,128]{3,2,1,0:T(8,128)} %shard_map.53), kind=kLoop, calls=%fused_computation.1 | loop fusion | bytes 81920 | tf_op jit(solution)/shard_map/squeeze | solution.py:478
  69.0 0.0 collective-permute-start.5
  69.0 0.0 collective-permute-done.4
  69.0 0.3 copy.15
  69.3 0.9 %broadcast_in_dim.2 = f32[2,19,12,2,8]{4,3,2,1,0:T(2,128)} broadcast(f32[2,19,12,8]{3,2,1,0:T(8,128)S(1)} %copy.15), dimensions={0,1,2,4} | broadcast | bytes 43776 | tf_op jit(solution)/shard_map/broadcast_in_dim | solution.py:455
  70.3 2.7 %shard_map.51.ghosts = f32[2,6,2,24,128]{4,3,2,1,0:T(8,128)} custom-call(f32[2,456,8]{2,1,0:T(8,128)} %bitcast.30, f32[8,256]{1,0:T(8,128)} %fusion.spread), custom_call_target="tpu_custom_call" | custom-call | flops 1000000 | bytes 1000000 | tf_op jit(solution)/shard_map/pallas_call | solution.py:459
  73.0 4.7 %shard_map.52 = f32[1216,128]{1,0:T(8,128)} custom-call(f32[1216,128]{1,0:T(8,128)} %bitcast.25, f32[304,128]{1,0:T(8,128)} %bitcast.6.left, f32[304,128]{1,0:T(8,128)} %bitcast.7.right, f32[2,6,2,24,128]{4,3,2,1,0:T(8,128)} %shard_map.51.ghosts), custom_call_target="tpu_custom_call" | custom-call | flops 10000000 | bytes 1000000 | tf_op jit(solution)/shard_map/pallas_call | solution.py:481
  77.7 0.0 collective-permute-done.5.high
  77.8 0.6 copy-done.3
  78.4 3.9 %shard_map.54 = f32[19,12,8,128]{3,2,1,0:T(8,128)} custom-call(f32[19,12,8,128]{3,2,1,0:T(8,128)} %copy-done, f32[5,8,128]{2,1,0:T(8,128)} %get-tuple-element.9.low, f32[5,8,128]{2,1,0:T(8,128)} %copy-done.3), custom_call_target="tpu_custom_call" | custom-call | flops 10000000 | bytes 1000000 | tf_op jit(solution)/shard_map/pallas_call | solution.py:494
  82.3 2.0 %slice.42 = f32[19,8,8,128]{3,2,1,0:T(8,128)} slice(f32[19,12,8,128]{3,2,1,0:T(8,128)} %shard_map.54), slice={[0:19], [2:10], [0:8], [0:128]} | slice | bytes 1245184 | tf_op jit(solution)/shard_map/slice | solution.py:504
  (13 shorter events, 0.1 us)
Async XLA Ops:
  31.1 2.8 %copy-start.2 = (f32[19,8,8,128]{3,2,1,0:T(8,128)S(1)}, f32[19,8,8,128]{3,2,1,0:T(8,128)}, u32[]{:S(2)}) copy-start(f32[19,8,8,128]{3,2,1,0:T(8,128)} %param.4) | copy-start | bytes 1867780
  31.1 21.1 %all-to-all-start.1 = ((f32[32,19,2,128]{3,2,1,0:T(2,128)}), f32[32,19,2,128]{3,2,1,0:T(2,128)S(1)}, u32[]{:S(2)}, u32[]{:S(2)}) async-start(f32[32,19,2,128]{3,2,1,0:T(2,128)} %bitcast.26), calls=%async_computation.1 | async-start | bytes 1245184 | tf_op jit(solution)/shard_map/all_to_all | solution.py:445
  33.9 12.1 %collective-permute-start.2 = (f32[19,2,8,128]{3,2,1,0:T(8,128)S(1)}, f32[19,2,8,128]{3,2,1,0:T(8,128)S(1)}, u32[]{:S(2)}, u32[]{:S(2)}) collective-permute-start(f32[19,2,8,128]{3,2,1,0:T(8,128)S(1)} %get-tuple-element.5), channel_id=1, source_target_pairs={{0,8},{8,16},{16,24},{24,0},{1,9},{9,17},{17,25},{25,1},{2,10},{10... | collective-permute-start | bytes 466952 | tf_op jit(solution)/shard_map/ppermute | solution.py:451
  35.6 13.5 %collective-permute-start.3 = (f32[19,2,8,128]{3,2,1,0:T(8,128)S(1)}, f32[19,2,8,128]{3,2,1,0:T(8,128)S(1)}, u32[]{:S(2)}, u32[]{:S(2)}) collective-permute-start(f32[19,2,8,128]{3,2,1,0:T(8,128)S(1)} %get-tuple-element.4), channel_id=1, source_target_pairs={{0,24},{8,0},{16,8},{24,16},{1,25},{9,1},{17,9},{25,17},{2,26},{10... | collective-permute-start | bytes 466952 | tf_op jit(solution)/shard_map/ppermute | solution.py:452
  49.0 7.2 %copy-start = (f32[19,12,8,128]{3,2,1,0:T(8,128)}, f32[19,12,8,128]{3,2,1,0:T(8,128)S(1)}, u32[]{:S(2)}) copy-start(f32[19,12,8,128]{3,2,1,0:T(8,128)S(1)} %constant_dynamic-update-slice_fusion.state) | copy-start | bytes 2801668
  52.2 4.1 %copy-start.1 = (f32[32,19,2,128]{3,2,1,0:T(2,128)}, f32[32,19,2,128]{3,2,1,0:T(2,128)S(1)}, u32[]{:S(2)}) copy-start(f32[32,19,2,128]{3,2,1,0:T(2,128)S(1)} %all-to-all-done.1) | copy-start | bytes 1867780
  53.0 8.1 %collective-permute-start = (f32[19,16,128]{2,1,0:T(8,128)}, f32[19,16,128]{2,1,0:T(8,128)}, u32[]{:S(2)}, u32[]{:S(2)}) collective-permute-start(f32[19,16,128]{2,1,0:T(8,128)} %get-tuple-element.7), channel_id=1, source_target_pairs={{0,8},{8,16},{16,24},{24,0},{1,9},{9,17},{17,25},{25,1},{2,10},{10... | collective-permute-start | bytes 466952 | tf_op jit(solution)/shard_map/ppermute | solution.py:468
  53.0 10.0 %collective-permute-start.1 = (f32[19,16,128]{2,1,0:T(8,128)}, f32[19,16,128]{2,1,0:T(8,128)}, u32[]{:S(2)}, u32[]{:S(2)}) collective-permute-start(f32[19,16,128]{2,1,0:T(8,128)} %get-tuple-element.6), channel_id=1, source_target_pairs={{0,24},{8,0},{16,8},{24,16},{1,25},{9,1},{17,9},{25,17},{2,26},{10... | collective-permute-start | bytes 466952 | tf_op jit(solution)/shard_map/ppermute | solution.py:469
  57.7 11.3 %collective-permute-start.4 = (f32[19,12,8]{0,2,1:T(8,128)S(1)}, f32[19,12,8]{0,2,1:T(8,128)S(1)}, u32[]{:S(2)}, u32[]{:S(2)}) collective-permute-start(f32[19,12,8]{0,2,1:T(8,128)S(1)} %bitcast.34), channel_id=1, source_target_pairs={{0,1},{1,2},{2,3},{3,4},{4,5},{5,6},{6,7},{7,0},{8,9},{9,10},{10,1... | collective-permute-start | bytes 21896 | tf_op jit(solution)/shard_map/ppermute | solution.py:454
  69.0 8.7 %collective-permute-start.5 = (f32[5,8,128]{2,1,0:T(8,128)S(1)}, f32[5,8,128]{2,1,0:T(8,128)S(1)}, u32[]{:S(2)}, u32[]{:S(2)}) collective-permute-start(f32[5,8,128]{2,1,0:T(8,128)S(1)} %get-tuple-element.8), channel_id=1, source_target_pairs={{0,7},{1,0},{2,1},{3,2},{4,3},{5,4},{6,5},{7,6},{8,15},{9,8},{10,9... | collective-permute-start | bytes 61448 | tf_op jit(solution)/shard_map/ppermute | solution.py:478
  77.7 0.6 copy-start.3
where the time goes:
time: 84.7 us; the launch traced here: 84.2 us
  blocking collectives  25.6 us (30%)
  waiting for transfers between devices  19.8 us (23%)
  Pallas kernels  18.8 us (22%)
  local copies, waits for them, and re-layouts  9.96 us (12%)
  starting transfers between devices  8.68 us (10%)
    all_to_all x1, blocking collectives, local(): spread = lax.all_to_all(pieces, axes, 0, 0, tiled=True)  25.6 us
    ppermute x1, waiting for transfers between devices, local(): lax.ppermute(coarse_pop[:, cx - edge:], 'grp', ring('grp', n_grp, 1))  8.51 us
    pallas_call x1, Pallas kernels, local(): call(functools.partial(fine_body, ch_count, k_count), f32(Q * B * nq, LAN...  4.73 us
    pallas_call x1, Pallas kernels, local(): call(functools.partial(restrict_body, ch_count, k_count), f32(2, groups,...  4.71 us
    pallas_call x1, Pallas kernels, local(): call(functools.partial(coarse_body, planes), f32(Q, planes, cz, cy), [VME...  3.89 us
    ppermute x1, waiting for transfers between devices, local(): lax.ppermute(by_x[:, -width:], 'grp', ring('grp', n_grp, 1))  3.34 us
    all_to_all x1, waiting for transfers between devices, local(): lax.all_to_all(outgoing.reshape(devices, rows, k_count, LANES), axes, 0,...  3.11 us
    ppermute x1, waiting for transfers between devices, local(): lax.ppermute(coarse_pop[:, :edge], 'grp', ring('grp', n_grp, -1))  3.01 us
  transfers between devices with their start and end apart: 7, of which 5 were waited for; matrix products, arithmetic and copies ran while one was open for 6% of the time, Pallas kernels for 14%

commit v1 on v0

--- a/solution.py
+++ b/solution.py
@@ -4,6 +4,7 @@
 import jax.numpy as jnp
 from jax import lax
 from jax.experimental import pallas as pl
+from jax.experimental.layout import Layout, with_layout_constraint
 from jax.experimental.pallas import tpu as pltpu
 from jax.sharding import PartitionSpec as P
 
@@ -12,6 +13,7 @@
 SUB = 8
 HALO = 4
 PAD = 8
+GRANT = 24 << 20
 
 VELOCITIES = (
     (0, 0, 0),
@@ -59,6 +61,7 @@
         out_specs=jax.tree.map(lambda _: VMEM, outs),
         scratch_shapes=list(scratch),
         cost_estimate=pl.CostEstimate(flops=flops, bytes_accessed=moved, transcendentals=0),
+        compiler_params=pltpu.CompilerParams(vmem_limit_bytes=GRANT),
     )
 
 
@@ -298,7 +301,7 @@
 PER = LANES // STRIDE
 
 
-def restrict_body(ch_count, k_count, own, left, right, out, buffer):
+def restrict_body(ch_count, k_count, own, left, right, out_low, out_high, buffer):
     nq = ch_count * k_count
     row = lax.broadcasted_iota(jnp.int32, (LANES, LANES), 0)
     col = lax.broadcasted_iota(jnp.int32, (LANES, LANES), 1)
@@ -341,10 +344,10 @@
                 block = jnp.concatenate(
                     [block, jnp.zeros((LANES - count, LANES), jnp.float32)], axis=0
                 )
-            out[side, n] = block.T[:SUB]
-
-
-def coarse_body(planes, state, low, high, out, ghosts, parts):
+            (out_low, out_high)[side][n] = block.T[:SUB]
+
+
+def coarse_body(planes, state, low, high, out, ghosts, parts, out_pad):
     lane = lax.broadcasted_iota(jnp.int32, (SUB, LANES), 1)
     first_y, last_y = lane == 0, lane == LANES - 1
 
@@ -404,10 +407,13 @@
                 post = shift_y(post, cy, i)
             if cz:
                 post = shift_z(post, cz)
-            out[i, x + cx] = post[0]
+            inside = x + cx - base
+            spare = jnp.where((inside >= 0) & (inside < inner), inside, inner)
+            out_pad[i, spare] = post[0]
         return carry
 
     lax.fori_loop(base - 1, base + inner + 1, update, 0, unroll=2)
+    out[...] = out_pad[:, :inner]
 
 
 def ring(axis, count, step):
@@ -428,12 +434,20 @@
     fine_rows = B + 2 * HALO
 
     rows = pl.cdiv(Q * tiles, devices)
-    pieces = fine_pop.reshape(k_count, Q, tiles, LANES).transpose(1, 2, 0, 3)
+    pieces = fine_pop.reshape(k_count, Q, tiles, LANES)
+    pieces = with_layout_constraint(pieces, Layout(major_to_minor=(1, 2, 0, 3)))
+    pieces = pieces.transpose(1, 2, 0, 3)
     pieces = pieces.reshape(Q * tiles, k_count, LANES)
     if rows * devices != Q * tiles:
         pieces = jnp.pad(pieces, ((0, rows * devices - Q * tiles), (0, 0), (0, 0)))
     pieces = pieces.reshape(devices, rows, k_count, LANES)
     spread = lax.all_to_all(pieces, axes, 0, 0, tiled=True)
+    edge = HALO // 2
+    coarse_left = lax.ppermute(coarse_pop[:, cx - edge :], "grp", ring("grp", n_grp, 1))
+    coarse_right = lax.ppermute(coarse_pop[:, :edge], "grp", ring("grp", n_grp, -1))
+    coarse = jnp.concatenate([coarse_left, coarse_pop, coarse_right], axis=1)
+    below = lax.ppermute(coarse[..., -1], "wide", ring("wide", n_wide, 1))
+    spread, coarse, below = lax.optimization_barrier((spread, coarse, below))
     total = devices * rows * k_count
     regroup = call(
         functools.partial(regroup_body, blocks, k_count, rows),
@@ -445,13 +459,6 @@
     arrived = lax.all_to_all(
         outgoing.reshape(devices, rows, k_count, LANES), axes, 0, 0, tiled=True
     )
-    own = arrived.reshape(total, LANES)[: Q * tiles * k_count]
-
-    edge = HALO // 2
-    coarse_left = lax.ppermute(coarse_pop[:, cx - edge :], "grp", ring("grp", n_grp, 1))
-    coarse_right = lax.ppermute(coarse_pop[:, :edge], "grp", ring("grp", n_grp, -1))
-    coarse = jnp.concatenate([coarse_left, coarse_pop, coarse_right], axis=1)
-    below = lax.ppermute(coarse[..., -1], "wide", ring("wide", n_wide, 1))
     layers = jnp.repeat(jnp.stack([below, coarse[..., 0]]), 2, axis=2)
     layers = layers.reshape(2, Q * fine_rows, cz)
     lane = jnp.arange(ch_count * LANES) // (2 * B)
@@ -462,6 +469,8 @@
         [VMEM, VMEM],
         [pltpu.VMEM((Q * fine_rows, ch_count * LANES), jnp.float32)],
     )(layers, one_hot)
+    arrived, fine_ghosts = lax.optimization_barrier((arrived, fine_ghosts))
+    own = arrived.reshape(total, LANES)[: Q * tiles * k_count]
 
     by_x = own.reshape(Q, B * nq, LANES)
     width = HALO * nq
@@ -471,7 +480,7 @@
     groups = pl.cdiv(Q, PER)
     restricted = call(
         functools.partial(restrict_body, ch_count, k_count),
-        f32(2, groups, SUB, LANES),
+        [f32(groups, SUB, LANES)] * 2,
         [VMEM, VMEM, VMEM],
         [pltpu.VMEM((ch_count, Q * STRIDE, LANES), jnp.float32)],
     )(own, left, right)
@@ -491,17 +500,17 @@
         flops=10**7,
     )(own, left, right, fine_ghosts)
 
-    coarse_new = call(
+    coarse_out = call(
         functools.partial(coarse_body, planes),
-        f32(Q, planes, cz, cy),
+        f32(Q, cx, cz, cy),
         [VMEM] * 3,
         [
             pltpu.VMEM((2, NG, planes, SUB, LANES), jnp.float32),
             pltpu.VMEM((10, planes, SUB, LANES), jnp.float32),
+            pltpu.VMEM((Q, cx + 1, SUB, LANES), jnp.float32),
         ],
         flops=10**7,
     )(coarse, restricted[0], high)
-    coarse_out = coarse_new[:, edge : edge + cx]
 
     fine_out = fine.reshape(Q, tiles, k_count, LANES).transpose(2, 0, 1, 3)
     fine_out = fine_out.reshape(k_count, q_count, cells)

time: 84.7 us -> 73 us (0.86)
  blocking collectives: 25.6 us -> 0 us
  waiting for transfers between devices: 19.8 us -> 40.4 us
  starting transfers between devices: 8.68 us -> 17.2 us
  local copies, waits for them, and re-layouts: 9.96 us -> 2.36 us
  Pallas kernels: 18.8 us -> 12.1 us
    all_to_all x1 -> x0, blocking collectives: 25.6 us -> none  [local(): spread = lax.all_to_all(pieces, axes, 0, 0, tiled=True)]
    all_to_all x1, waiting for transfers between devices: 3.11 us -> 16.1 us  [local(): lax.all_to_all(outgoing.reshape(devices, rows, k_count, LANES), axes, 0,...]
    all_to_all x0 -> x1, starting transfers between devices: none -> 7.33 us  [local(): spread = lax.all_to_all(pieces, axes, 0, 0, tiled=True)]
    ppermute x1, waiting for transfers between devices: 0.01 us -> 5.33 us  [local(): below = lax.ppermute(coarse[..., -1], 'wide', ring('wide', n_wide, 1))]
    pallas_call x2, Pallas kernels: 8.61 us -> 5.42 us  [the longest x1 2.88 us: local(): call(functools.partial(restrict_body, ch_count, k_count), [f32(groups, SU...]
    slice x1 -> x0, local copies, waits for them, and re-layouts: 1.96 us -> none  [local(): coarse_out = coarse_new[:, edge:edge + cx]]
    pallas_call x1, Pallas kernels: 2.73 us -> 0.99 us  [local(): call(functools.partial(fine_ghost_body, ch_count, fine_rows), f32(2, NG,...]
    reshape x1 -> x0, local copies, waits for them, and re-layouts: 1.61 us -> none  [local(): pieces = fine_pop.reshape(k_count, Q, tiles, LANES).transpose(1, 2, 0, 3)]
  transfers between devices with their start and end apart: 7 -> 8, of which waited for: 5 -> 6; matrix products, arithmetic and copies ran while one was open for 6% -> 3% of each run, Pallas kernels for 14% -> 6%
where the time goes in v1:
time: 73 us; the launch traced here: 72.8 us
  waiting for transfers between devices  40.4 us (55%)
  starting transfers between devices  17.2 us (24%)
  Pallas kernels  12.1 us (17%)
  local copies, waits for them, and re-layouts  2.36 us (3%)
  between operations  0.76 us (1%)
    all_to_all x1, waiting for transfers between devices, local(): lax.all_to_all(outgoing.reshape(devices, rows, k_count, LANES), axes, 0,...  16.1 us
    ppermute x1, waiting for transfers between devices, local(): lax.ppermute(coarse_pop[:, cx - edge:], 'grp', ring('grp', n_grp, 1))  9.3 us
    all_to_all x1, starting transfers between devices, local(): spread = lax.all_to_all(pieces, axes, 0, 0, tiled=True)  7.33 us
    ppermute x1, waiting for transfers between devices, local(): below = lax.ppermute(coarse[..., -1], 'wide', ring('wide', n_wide, 1))  5.33 us
    ppermute x1, waiting for transfers between devices, local(): lax.ppermute(by_x[:, -width:], 'grp', ring('grp', n_grp, 1))  4.87 us
    all_to_all x1, starting transfers between devices, local(): lax.all_to_all(outgoing.reshape(devices, rows, k_count, LANES), axes, 0,...  3.85 us
    pallas_call x1, Pallas kernels, local(): call(functools.partial(fine_body, ch_count, k_count), f32(Q * B * nq, LAN...  3.44 us
    ppermute x1, waiting for transfers between devices, local(): lax.ppermute(coarse_pop[:, :edge], 'grp', ring('grp', n_grp, -1))  2.94 us
  transfers between devices with their start and end apart: 8, of which 6 were waited for; matrix products, arithmetic and copies ran while one was open for 3% of the time, Pallas kernels for 6%

profile of v1, /device:TPU:0, one launch (start us, length us, event | category | flops | bytes accessed | tf_op | source)
XLA Modules:
  0.0 72.8 jit_solution(5720199421065456381)
XLA Ops:
  0.6 0.0 copy-start.1
  0.6 7.3 %all-to-all-start = ((f32[32,19,2,128]{3,2,1,0:T(2,128)}), f32[32,19,2,128]{3,2,1,0:T(2,128)S(1)}, u32[]{:S(2)}, u32[]{:S(2)}) async-start(f32[32,19,2,128]{3,2,1,0:T(2,128)} %bitcast.31), calls=%async_computation | async-start | bytes 1245184 | tf_op jit(solution)/shard_map/all_to_all | solution.py:444
  8.0 0.0 copy-done.1
  8.0 1.8 %collective-permute-start = (f32[19,2,8,128]{3,2,1,0:T(8,128)S(1)}, f32[19,2,8,128]{3,2,1,0:T(8,128)S(1)}, u32[]{:S(2)}, u32[]{:S(2)}) collective-permute-start(f32[19,2,8,128]{3,2,1,0:T(8,128)S(1)} %get-tuple-element.19), channel_id=1, source_target_pairs={{0,8},{8,16},{16,24},{24,0},{1,9},{9,17},{17,25},{25,1},{2,10},{10... | collective-permute-start | bytes 466952 | tf_op jit(solution)/shard_map/ppermute | solution.py:446
  9.8 1.2 %collective-permute-start.1 = (f32[19,2,8,128]{3,2,1,0:T(8,128)S(1)}, f32[19,2,8,128]{3,2,1,0:T(8,128)S(1)}, u32[]{:S(2)}, u32[]{:S(2)}) collective-permute-start(f32[19,2,8,128]{3,2,1,0:T(8,128)S(1)} %get-tuple-element.18), channel_id=1, source_target_pairs={{0,24},{8,0},{16,8},{24,16},{1,25},{9,1},{17,9},{25,17},{2,26},{10... | collective-permute-start | bytes 466952 | tf_op jit(solution)/shard_map/ppermute | solution.py:447
  11.0 9.3 %collective-permute-done = f32[19,2,8,128]{3,2,1,0:T(8,128)S(1)} collective-permute-done((f32[19,2,8,128]{3,2,1,0:T(8,128)S(1)}, f32[19,2,8,128]{3,2,1,0:T(8,128)S(1)}, u32[]{:S(2)}, u32[]{:S(2)}) %collective-permute-start) | collective-permute-done | bytes 155680 | tf_op jit(solution)/shard_map/ppermute | solution.py:446
  20.4 2.9 %collective-permute-done.1 = f32[19,2,8,128]{3,2,1,0:T(8,128)S(1)} collective-permute-done((f32[19,2,8,128]{3,2,1,0:T(8,128)S(1)}, f32[19,2,8,128]{3,2,1,0:T(8,128)S(1)}, u32[]{:S(2)}, u32[]{:S(2)}) %collective-permute-start.1) | collective-permute-done | bytes 155680 | tf_op jit(solution)/shard_map/ppermute | solution.py:447
  23.3 0.3 slice.24
  23.6 0.7 %copy.10 = f32[19,12,8,1]{0,2,3,1:T(8,128)S(1)} copy(f32[19,12,8,1]{3,2,1,0:T(8,128)S(1)} %slice.24) | data formatting | bytes 14592 | tf_op jit(solution)/shard_map/slice | solution.py:449
  24.4 0.0 copy-start
  24.4 0.0 collective-permute-start.2
  24.4 5.3 %collective-permute-done.2 = f32[19,12,8]{0,2,1:T(8,128)S(1)} collective-permute-done((f32[19,12,8]{0,2,1:T(8,128)S(1)}, f32[19,12,8]{0,2,1:T(8,128)S(1)}, u32[]{:S(2)}, u32[]{:S(2)}) %collective-permute-start.2) | collective-permute-done | bytes 7328 | tf_op jit(solution)/shard_map/ppermute | solution.py:449
  29.7 0.0 all-to-all-done
  29.7 0.0 copy-done
  29.7 2.2 %shard_map.50 = f32[1216,128]{1,0:T(8,128)} custom-call(s32[64]{0:T(128)S(1)} %copy-done, f32[1216,128]{1,0:T(8,128)S(1)} %bitcast.25), custom_call_target="tpu_custom_call" | custom-call | flops 1000000 | bytes 1245184 | tf_op jit(solution)/shard_map/pallas_call | solution.py:458
  32.0 3.9 %all-to-all-start.1 = ((f32[32,19,2,128]{3,2,1,0:T(2,128)}), f32[32,19,2,128]{3,2,1,0:T(2,128)S(1)}, u32[]{:S(2)}, u32[]{:S(2)}) async-start(f32[32,19,2,128]{3,2,1,0:T(2,128)} %bitcast.5), calls=%async_computation.1 | async-start | bytes 1245184 | tf_op jit(solution)/shard_map/all_to_all | solution.py:459
  35.8 0.7 %copy.11 = f32[19,12,8,1]{0,2,3,1:T(8,128)S(1)} copy(f32[19,12,8,1]{3,2,1,0:T(8,128)S(1)} %bitcast.21) | data formatting | bytes 14592 | tf_op jit(solution)/shard_map/slice | solution.py:462
  36.6 0.3 copy.12
  36.9 0.2 broadcast_in_dim.2
  37.1 1.0 %shard_map.51.ghosts = f32[2,6,2,24,128]{4,3,2,1,0:T(8,128)S(1)} custom-call(f32[2,456,8]{2,1,0:T(8,128)S(1)} %bitcast.26, f32[8,256]{1,0:T(8,128)S(1)} %fusion.spread), custom_call_target="tpu_custom_call" | custom-call | flops 1000000 | bytes 1000000 | tf_op jit(solution)/shard_map/pallas_call | solution.py:466
  38.1 16.1 %all-to-all-done.1 = f32[32,19,2,128]{3,2,1,0:T(2,128)S(1)} async-done(((f32[32,19,2,128]{3,2,1,0:T(2,128)}), f32[32,19,2,128]{3,2,1,0:T(2,128)S(1)}, u32[]{:S(2)}, u32[]{:S(2)}) %all-to-all-start.1) | async-done | bytes 622624 | tf_op jit(solution)/shard_map/all_to_all | solution.py:459
  54.2 0.1 collective-permute-start.3
  54.2 2.9 %collective-permute-start.4 = (f32[19,16,128]{2,1,0:T(8,128)S(1)}, f32[19,16,128]{2,1,0:T(8,128)S(1)}, u32[]{:S(2)}, u32[]{:S(2)}) collective-permute-start(f32[19,16,128]{2,1,0:T(8,128)S(1)} %get-tuple-element.16), channel_id=1, source_target_pairs={{0,24},{8,0},{16,8},{24,16},{1,25},{9,1},{17,9},{25,17},{2,26},{10... | collective-permute-start | bytes 466952 | tf_op jit(solution)/shard_map/ppermute | solution.py:478
  57.2 4.9 %collective-permute-done.3 = f32[19,16,128]{2,1,0:T(8,128)S(1)} collective-permute-done((f32[19,16,128]{2,1,0:T(8,128)S(1)}, f32[19,16,128]{2,1,0:T(8,128)S(1)}, u32[]{:S(2)}, u32[]{:S(2)}) %collective-permute-start.3) | collective-permute-done | bytes 155680 | tf_op jit(solution)/shard_map/ppermute | solution.py:477
  62.0 1.9 %collective-permute-done.4 = f32[19,16,128]{2,1,0:T(8,128)S(1)} collective-permute-done((f32[19,16,128]{2,1,0:T(8,128)S(1)}, f32[19,16,128]{2,1,0:T(8,128)S(1)}, u32[]{:S(2)}, u32[]{:S(2)}) %collective-permute-start.4) | collective-permute-done | bytes 155680 | tf_op jit(solution)/shard_map/ppermute | solution.py:478
  63.9 2.9 %shard_map.53 = (f32[5,8,128]{2,1,0:T(8,128)S(1)}, f32[5,8,128]{2,1,0:T(8,128)S(1)}) custom-call(f32[1216,128]{1,0:T(8,128)S(1)} %bitcast.23, f32[304,128]{1,0:T(8,128)S(1)} %bitcast.27, f32[304,128]{1,0:T(8,128)S(1)} %bitcast.29), custom_call_target="tpu_custom_call" | custom-call | flops 1000000 | bytes 1000000 | tf_op jit(solution)/shard_map/pallas_call | solution.py:481
  66.8 0.0 collective-permute-start.5
  66.8 3.4 %shard_map.52 = f32[1216,128]{1,0:T(8,128)} custom-call(f32[1216,128]{1,0:T(8,128)S(1)} %bitcast.24, f32[304,128]{1,0:T(8,128)S(1)} %bitcast.28, f32[304,128]{1,0:T(8,128)S(1)} %bitcast.30, f32[2,6,2,24,128]{4,3,2,1,0:T(8,128)S(1)} %shard_map.51.ghosts), custom_call_target="tpu_custom_call" | custom-call | flops 10000000 | bytes 1000000 | tf_op jit(solution)/shard_map/pallas_call | solution.py:490
  70.2 0.0 collective-permute-done.5.high
  70.2 2.5 %shard_map.54 = f32[19,8,8,128]{3,2,1,0:T(8,128)} custom-call(f32[19,12,8,128]{3,2,1,0:T(8,128)S(1)} %constant_dynamic-update-slice_fusion.state, f32[5,8,128]{2,1,0:T(8,128)S(1)} %get-tuple-element.14.low, f32[5,8,128]{2,1,0:T(8,128)S(1)} %collective-permute-done.5.high), custom_call_target="tpu_custom_call" | custom-call | flops 10000000 | bytes 1000000 | tf_op jit(solution)/shard_map/pallas_call | solution.py:503
  (8 shorter events, 0.1 us)
Async XLA Ops:
  0.6 7.4 %copy-start.1 = (f32[19,8,8,128]{3,2,1,0:T(8,128)S(1)}, f32[19,8,8,128]{3,2,1,0:T(8,128)}, u32[]{:S(2)}) copy-start(f32[19,8,8,128]{3,2,1,0:T(8,128)} %param.4) | copy-start | bytes 1867780
  0.6 29.1 %all-to-all-start = ((f32[32,19,2,128]{3,2,1,0:T(2,128)}), f32[32,19,2,128]{3,2,1,0:T(2,128)S(1)}, u32[]{:S(2)}, u32[]{:S(2)}) async-start(f32[32,19,2,128]{3,2,1,0:T(2,128)} %bitcast.31), calls=%async_computation | async-start | bytes 1245184 | tf_op jit(solution)/shard_map/all_to_all | solution.py:444
  8.0 12.3 %collective-permute-start = (f32[19,2,8,128]{3,2,1,0:T(8,128)S(1)}, f32[19,2,8,128]{3,2,1,0:T(8,128)S(1)}, u32[]{:S(2)}, u32[]{:S(2)}) collective-permute-start(f32[19,2,8,128]{3,2,1,0:T(8,128)S(1)} %get-tuple-element.19), channel_id=1, source_target_pairs={{0,8},{8,16},{16,24},{24,0},{1,9},{9,17},{17,25},{25,1},{2,10},{10... | collective-permute-start | bytes 466952 | tf_op jit(solution)/shard_map/ppermute | solution.py:446
  9.8 13.5 %collective-permute-start.1 = (f32[19,2,8,128]{3,2,1,0:T(8,128)S(1)}, f32[19,2,8,128]{3,2,1,0:T(8,128)S(1)}, u32[]{:S(2)}, u32[]{:S(2)}) collective-permute-start(f32[19,2,8,128]{3,2,1,0:T(8,128)S(1)} %get-tuple-element.18), channel_id=1, source_target_pairs={{0,24},{8,0},{16,8},{24,16},{1,25},{9,1},{17,9},{25,17},{2,26},{10... | collective-permute-start | bytes 466952 | tf_op jit(solution)/shard_map/ppermute | solution.py:447
  24.4 5.4 %copy-start = (s32[64]{0:T(128)S(1)}, s32[64]{0:T(128)}, u32[]{:S(2)}) copy-start(s32[64]{0:T(128)} %slot_ref.1) | copy-start | bytes 772
  24.4 5.4 %collective-permute-start.2 = (f32[19,12,8]{0,2,1:T(8,128)S(1)}, f32[19,12,8]{0,2,1:T(8,128)S(1)}, u32[]{:S(2)}, u32[]{:S(2)}) collective-permute-start(f32[19,12,8]{0,2,1:T(8,128)S(1)} %bitcast.35), channel_id=1, source_target_pairs={{0,1},{1,2},{2,3},{3,4},{4,5},{5,6},{6,7},{7,0},{8,9},{9,10},{10,1... | collective-permute-start | bytes 21896 | tf_op jit(solution)/shard_map/ppermute | solution.py:449
  32.0 22.2 %all-to-all-start.1 = ((f32[32,19,2,128]{3,2,1,0:T(2,128)}), f32[32,19,2,128]{3,2,1,0:T(2,128)S(1)}, u32[]{:S(2)}, u32[]{:S(2)}) async-start(f32[32,19,2,128]{3,2,1,0:T(2,128)} %bitcast.5), calls=%async_computation.1 | async-start | bytes 1245184 | tf_op jit(solution)/shard_map/all_to_all | solution.py:459
  54.2 7.8 %collective-permute-start.3 = (f32[19,16,128]{2,1,0:T(8,128)S(1)}, f32[19,16,128]{2,1,0:T(8,128)S(1)}, u32[]{:S(2)}, u32[]{:S(2)}) collective-permute-start(f32[19,16,128]{2,1,0:T(8,128)S(1)} %get-tuple-element.17), channel_id=1, source_target_pairs={{0,8},{8,16},{16,24},{24,0},{1,9},{9,17},{17,25},{25,1},{2,10},{10... | collective-permute-start | bytes 466952 | tf_op jit(solution)/shard_map/ppermute | solution.py:477
  54.2 9.6 %collective-permute-start.4 = (f32[19,16,128]{2,1,0:T(8,128)S(1)}, f32[19,16,128]{2,1,0:T(8,128)S(1)}, u32[]{:S(2)}, u32[]{:S(2)}) collective-permute-start(f32[19,16,128]{2,1,0:T(8,128)S(1)} %get-tuple-element.16), channel_id=1, source_target_pairs={{0,24},{8,0},{16,8},{24,16},{1,25},{9,1},{17,9},{25,17},{2,26},{10... | collective-permute-start | bytes 466952 | tf_op jit(solution)/shard_map/ppermute | solution.py:478
  66.8 3.5 %collective-permute-start.5 = (f32[5,8,128]{2,1,0:T(8,128)S(1)}, f32[5,8,128]{2,1,0:T(8,128)S(1)}, u32[]{:S(2)}, u32[]{:S(2)}) collective-permute-start(f32[5,8,128]{2,1,0:T(8,128)S(1)} %get-tuple-element.15), channel_id=1, source_target_pairs={{0,7},{1,0},{2,1},{3,2},{4,3},{5,4},{6,5},{7,6},{8,15},{9,8},{10,9... | collective-permute-start | bytes 61448 | tf_op jit(solution)/shard_map/ppermute | solution.py:487

commit v2 on v1

--- a/solution.py
+++ b/solution.py
@@ -297,92 +297,56 @@
                 out[side, NG - 1, ch, pl.ds(r, SUB), :] = potential
 
 
-STRIDE = 32
-PER = LANES // STRIDE
-
-
-def restrict_body(ch_count, k_count, own, left, right, out_low, out_high, buffer):
-    nq = ch_count * k_count
-    row = lax.broadcasted_iota(jnp.int32, (LANES, LANES), 0)
-    col = lax.broadcasted_iota(jnp.int32, (LANES, LANES), 1)
-    for side in range(2):
-        k = k_count - 1 if side == 0 else 0
-        y = row % B
-        picked = (y >= B - 2) if side == 0 else (y < 2)
-        total = None
+GROUP = 16
+STEP = 32
+PLANES = -(-Q // GROUP)
+
+
+def pack(load, ch_count, k_count, side):
+    lane = lax.broadcasted_iota(jnp.int32, (SUB, LANES), 1)
+    offset = B - 2 if side == 0 else 0
+    kept = lane % STEP == offset
+    k = k_count - 1 if side == 0 else 0
+    planes = [None] * PLANES
+    for i in range(Q):
         for ch in range(ch_count):
             q = ch * k_count + k
-
-            def gather(i, carry, ch=ch, q=q):
-                at = i * STRIDE
-                buffer[ch, pl.ds(at, HALO), :] = left[
-                    pl.ds(i * (HALO * nq) + q, HALO, stride=nq), :
-                ]
-                buffer[ch, pl.ds(at + HALO, B), :] = own[pl.ds(i * (B * nq) + q, B, stride=nq), :]
-                buffer[ch, pl.ds(at + HALO + B, HALO), :] = right[
-                    pl.ds(i * (HALO * nq) + q, HALO, stride=nq), :
-                ]
-                buffer[ch, pl.ds(at + 2 * HALO + B, STRIDE - 2 * HALO - B), :] = jnp.zeros(
-                    (STRIDE - 2 * HALO - B, LANES), jnp.float32
-                )
-                return carry
-
-            lax.fori_loop(0, Q, gather, 0)
-            coarse_z = ch * (LANES // B // 2) + row // (2 * B)
-            select = jnp.where(picked & (coarse_z == col), 0.125, 0.0).astype(jnp.float32)
-            part = jnp.dot(
-                buffer[ch, pl.ds(0, Q * STRIDE), :],
-                select,
-                precision=lax.Precision.HIGHEST,
-                preferred_element_type=jnp.float32,
-            )
-            total = part if total is None else total + part
-        for n in range(pl.cdiv(Q, PER)):
-            count = min(PER, Q - n * PER) * STRIDE
-            block = total[n * LANES : n * LANES + count]
-            if count < LANES:
-                block = jnp.concatenate(
-                    [block, jnp.zeros((LANES - count, LANES), jnp.float32)], axis=0
-                )
-            (out_low, out_high)[side][n] = block.T[:SUB]
-
-
-def coarse_body(planes, state, low, high, out, ghosts, parts, out_pad):
+            v = load(i, q, 0) + load(i, q, 1)
+            v = v + pltpu.roll(v, LANES - 1, 1)
+            v = v + pltpu.roll(v, LANES - B, 1)
+            v = jnp.where(kept, v, 0.0)
+            shift = (2 * (i % GROUP) + ch - offset) % LANES
+            if shift:
+                v = pltpu.roll(v, shift, 1)
+            n = i // GROUP
+            planes[n] = v if planes[n] is None else planes[n] + v
+    return planes
+
+
+def restrict_body(ch_count, k_count, own, low, high):
+    nq = ch_count * k_count
+
+    def load(i, q, half):
+        return own[pl.ds(i * (B * nq) + half * nq + q, SUB, stride=2 * nq), :]
+
+    for side, out in enumerate((low, high)):
+        for n, plane in enumerate(pack(load, ch_count, k_count, side)):
+            out[n] = plane
+
+
+def coarse_body(planes, state, out, packed, near, parts, out_pad):
     lane = lax.broadcasted_iota(jnp.int32, (SUB, LANES), 1)
-    first_y, last_y = lane == 0, lane == LANES - 1
-
-    for side, ref in enumerate((low, high)):
-        paired = []
-        for n in range(pl.cdiv(Q, PER)):
-            v = ref[n]
-            paired.append(v + pltpu.roll(v, LANES - 1, 1))
-        f = []
-        for i in range(Q):
-            s = (i % PER) * STRIDE
-            f.append(paired[i // PER] if s == 0 else pltpu.roll(paired[i // PER], LANES - s, 1))
-        wanted = UP if side == 0 else DOWN
-        potential, found = rescaled(f, TO_COARSE, wanted)
-        for n, v in enumerate([found[i] for i in wanted] + [potential]):
-            for x in range(planes):
-                ghosts[side, n, x] = jnp.broadcast_to(v[:, 2 * x : 2 * x + 1], (SUB, LANES))
-
-    def shifts(x):
-        def shift_y(v, c, which):
-            side = 0 if c > 0 else 1
-            place = NG - 1 if which == "p" else (UP if c > 0 else DOWN).index(which)
-            carry = ghosts[side, place, x]
-            own = pltpu.roll(v[0], 1 if c > 0 else LANES - 1, 1)
-            return [jnp.where(first_y if c > 0 else last_y, carry, own)]
-
-        def shift_z(v, c):
-            return [pltpu.roll(v[0], 1 if c > 0 else SUB - 1, 0)]
-
-        return shift_y, shift_z
+
+    def shift_y(v, c, which):
+        return [pltpu.roll(v[0], 1 if c > 0 else LANES - 1, 1)]
+
+    def shift_z(v, c):
+        return [pltpu.roll(v[0], 1 if c > 0 else SUB - 1, 0)]
 
     def prepare(x, carry):
         density, momentum = moments([state[i, x] for i in range(Q)])
         p = 1.0 - jnp.exp(-density)
-        values = gradient_parts([p], *shifts(x))
+        values = gradient_parts([p], shift_y, shift_z)
         values = [v[0] for v in values] + [p, density, *momentum]
         for n, v in enumerate(values):
             parts[n, x] = v
@@ -390,11 +354,10 @@
 
     lax.fori_loop(0, planes, prepare, 0, unroll=2)
 
-    inner = planes - 2 * (HALO // 2)
+    inner = planes - HALO
     base = HALO // 2
 
     def update(x, carry):
-        shift_y, shift_z = shifts(x)
         lower = [parts[n, x - 1] for n in range(3)]
         upper = [parts[n, x + 1] for n in range(3)]
         gy, gz, p, rho, mx, my, mz = (parts[n, x] for n in range(3, 10))
@@ -415,6 +378,101 @@
     lax.fori_loop(base - 1, base + inner + 1, update, 0, unroll=2)
     out[...] = out_pad[:, :inner]
 
+    def gather(i, carry):
+        total = jnp.zeros((SUB, LANES), jnp.float32)
+        for x in range(planes):
+            here = (lane == 2 * x + 1) | (lane == 2 * x + 2)
+            total = jnp.where(here, pltpu.roll(state[i, x], 2 * x + 2, 1), total)
+        packed[i] = total
+        return carry
+
+    lax.fori_loop(0, Q, gather, 0)
+    total = jnp.zeros((SUB, LANES), jnp.float32)
+    for x in range(planes):
+        p = parts[5, x]
+        total = jnp.where(lane == 2 * x + 2, pltpu.roll(p, 2 * x + 1, 1), total)
+        total = jnp.where(lane == 2 * x + 1, pltpu.roll(p, 2 * x + 3, 1), total)
+    near[...] = total
+
+
+def edges_body(
+    ch_count, k_count, planes, left, right, low, high, high_left, high_right, packed, near, step,
+    out, halo, rows, columns, ghost,
+):
+    nq = ch_count * k_count
+    edge = HALO // 2
+    inner = planes - HALO
+    lane = lax.broadcasted_iota(jnp.int32, (SUB, LANES), 1)
+    sided = lane % 2 == 0
+
+    halo[...] = jnp.zeros_like(halo)
+
+    def load(i, q, half):
+        for at, ref in ((0, left), (edge, right)):
+            start = i * (HALO * nq) + half * nq + q
+            halo[i % 2, q, half, pl.ds(at, edge), :] = ref[pl.ds(start, edge, stride=2 * nq), :]
+        return halo[i % 2, q, half]
+
+    beside = pack(load, ch_count, k_count, 0)
+    for n in range(PLANES):
+        own_x = 2 * edge
+        rows[n, pl.ds(2 + own_x, inner, stride=2), :] = low[n]
+        rows[n, pl.ds(2, edge, stride=2), :] = beside[n][:edge]
+        rows[n, pl.ds(2 + 2 * (edge + inner), edge, stride=2), :] = beside[n][edge : 2 * edge]
+        rows[n, pl.ds(1 + own_x, inner, stride=2), :] = high[n]
+        rows[n, pl.ds(1, edge, stride=2), :] = high_left[n, pl.ds(inner - edge, edge), :]
+        rows[n, pl.ds(1 + 2 * (edge + inner), edge, stride=2), :] = high_right[
+            n, pl.ds(0, edge), :
+        ]
+        columns[n] = rows[n].T
+    per = LANES // STEP
+    for i in range(Q):
+        for ch in range(ch_count):
+            ghost[i, pl.ds(ch * per, per), :] = (
+                0.125 * columns[i // GROUP, pl.ds(2 * (i % GROUP) + ch, per, stride=STEP), :]
+            )
+
+    beyond, entering = rescaled([ghost[i] for i in range(Q)], TO_COARSE, UP + DOWN)
+    density, momentum = moments([packed[i] for i in range(Q)])
+    p = 1.0 - jnp.exp(-density)
+    inside = near[...]
+    above = jnp.where(sided, inside, beyond)
+    below = jnp.where(sided, beyond, inside)
+
+    def shift_y(v, c, which):
+        return [below if c > 0 else above]
+
+    def shift_z(v, c):
+        return [pltpu.roll(v[0], 1 if c > 0 else SUB - 1, 0)]
+
+    def shift_x(v, c):
+        return pltpu.roll(v, 2 if c > 0 else LANES - 2, 1) if c else v
+
+    tx, dy, dz, gy, gz = (v[0] for v in gradient_parts([p], shift_y, shift_z))
+    pull = [
+        shift_x(tx, -1) - shift_x(tx, 1),
+        gy + (shift_x(dy, -1) + shift_x(dy, 1)),
+        gz + (shift_x(dz, -1) + shift_x(dz, 1)),
+    ]
+    u = velocity_of(density, momentum, p, pull, COARSE_TAU)
+    for i, balance in balances(density, u, 1.0 / COARSE_TAU):
+        cx, cy, cz = VELOCITIES[i]
+        v = packed[i] * (1.0 - 1.0 / COARSE_TAU) + balance
+        if cy > 0:
+            v = jnp.where(sided, entering[i], pltpu.roll(v, 1, 1))
+            touched = lane < 2
+        elif cy < 0:
+            v = jnp.where(sided, pltpu.roll(v, LANES - 1, 1), entering[i])
+            touched = lane >= LANES - 2
+        else:
+            touched = (lane == 0) | (lane == LANES - 1)
+        v = shift_x(v, cx)
+        if cz:
+            v = shift_z([v], cz)[0]
+        for x in range(inner):
+            column = pltpu.roll(v, LANES - (2 * (x + edge) + 2), 1)
+            out[i, x] = jnp.where(touched, column, step[i, x])
+
 
 def ring(axis, count, step):
     return [(i, (i + step) % count) for i in range(count)]
@@ -446,8 +504,7 @@
     coarse_left = lax.ppermute(coarse_pop[:, cx - edge :], "grp", ring("grp", n_grp, 1))
     coarse_right = lax.ppermute(coarse_pop[:, :edge], "grp", ring("grp", n_grp, -1))
     coarse = jnp.concatenate([coarse_left, coarse_pop, coarse_right], axis=1)
-    below = lax.ppermute(coarse[..., -1], "wide", ring("wide", n_wide, 1))
-    spread, coarse, below = lax.optimization_barrier((spread, coarse, below))
+    spread, coarse = lax.optimization_barrier((spread, coarse))
     total = devices * rows * k_count
     regroup = call(
         functools.partial(regroup_body, blocks, k_count, rows),
@@ -459,6 +516,7 @@
     arrived = lax.all_to_all(
         outgoing.reshape(devices, rows, k_count, LANES), axes, 0, 0, tiled=True
     )
+    below = lax.ppermute(coarse[..., -1], "wide", ring("wide", n_wide, 1))
     layers = jnp.repeat(jnp.stack([below, coarse[..., 0]]), 2, axis=2)
     layers = layers.reshape(2, Q * fine_rows, cz)
     lane = jnp.arange(ch_count * LANES) // (2 * B)
@@ -469,7 +527,19 @@
         [VMEM, VMEM],
         [pltpu.VMEM((Q * fine_rows, ch_count * LANES), jnp.float32)],
     )(layers, one_hot)
-    arrived, fine_ghosts = lax.optimization_barrier((arrived, fine_ghosts))
+    coarse_step, packed, near = call(
+        functools.partial(coarse_body, planes),
+        [f32(Q, cx, cz, cy), f32(Q, SUB, LANES), f32(SUB, LANES)],
+        [VMEM],
+        [
+            pltpu.VMEM((10, planes, SUB, LANES), jnp.float32),
+            pltpu.VMEM((Q, cx + 1, SUB, LANES), jnp.float32),
+        ],
+        flops=10**7,
+    )(coarse)
+    arrived, fine_ghosts, coarse_step, packed, near = lax.optimization_barrier(
+        (arrived, fine_ghosts, coarse_step, packed, near)
+    )
     own = arrived.reshape(total, LANES)[: Q * tiles * k_count]
 
     by_x = own.reshape(Q, B * nq, LANES)
@@ -477,14 +547,19 @@
     left = lax.ppermute(by_x[:, -width:], "grp", ring("grp", n_grp, 1)).reshape(Q * width, LANES)
     right = lax.ppermute(by_x[:, :width], "grp", ring("grp", n_grp, -1)).reshape(Q * width, LANES)
 
-    groups = pl.cdiv(Q, PER)
-    restricted = call(
+    low, first = call(
         functools.partial(restrict_body, ch_count, k_count),
-        [f32(groups, SUB, LANES)] * 2,
-        [VMEM, VMEM, VMEM],
-        [pltpu.VMEM((ch_count, Q * STRIDE, LANES), jnp.float32)],
-    )(own, left, right)
-    high = lax.ppermute(restricted[1], "wide", ring("wide", n_wide, -1))
+        [f32(PLANES, SUB, LANES)] * 2,
+        [VMEM],
+    )(own)
+    highs = []
+    for across in (0, 1, -1):
+        pairs = [
+            (g * n_wide + (w + 1) % n_wide, (g + across) % n_grp * n_wide + w)
+            for g in range(n_grp)
+            for w in range(n_wide)
+        ]
+        highs.append(lax.ppermute(first, axes, pairs))
 
     padded = PAD + fine_rows + PAD
     fine = call(
@@ -501,16 +576,16 @@
     )(own, left, right, fine_ghosts)
 
     coarse_out = call(
-        functools.partial(coarse_body, planes),
+        functools.partial(edges_body, ch_count, k_count, planes),
         f32(Q, cx, cz, cy),
-        [VMEM] * 3,
+        [VMEM] * 9,
         [
-            pltpu.VMEM((2, NG, planes, SUB, LANES), jnp.float32),
-            pltpu.VMEM((10, planes, SUB, LANES), jnp.float32),
-            pltpu.VMEM((Q, cx + 1, SUB, LANES), jnp.float32),
+            pltpu.VMEM((2, nq, 2, SUB, LANES), jnp.float32),
+            pltpu.VMEM((PLANES, LANES, LANES), jnp.float32),
+            pltpu.VMEM((PLANES, LANES, LANES), jnp.float32),
+            pltpu.VMEM((Q, SUB, LANES), jnp.float32),
         ],
-        flops=10**7,
-    )(coarse, restricted[0], high)
+    )(left, right, low, *highs, packed, near, coarse_step)
 
     fine_out = fine.reshape(Q, tiles, k_count, LANES).transpose(2, 0, 1, 3)
     fine_out = fine_out.reshape(k_count, q_count, cells)

time: 73 us -> 66.2 us (0.907)
  waiting for transfers between devices: 40.4 us -> 30.9 us
  local copies, waits for them, and re-layouts: 2.36 us -> 4.39 us
  starting transfers between devices: 17.2 us -> 18.3 us
    all_to_all x1, waiting for transfers between devices: 16.1 us -> 2.2 us  [local(): lax.all_to_all(outgoing.reshape(devices, rows, k_count, LANES), axes, 0,...]
    ppermute x1, waiting for transfers between devices: 2.94 us -> 8.62 us  [local(): lax.ppermute(coarse_pop[:, :edge], 'grp', ring('grp', n_grp, -1))]
    ppermute x1, waiting for transfers between devices: 9.3 us -> 5.33 us  [local(): lax.ppermute(coarse_pop[:, cx - edge:], 'grp', ring('grp', n_grp, 1))]
    ppermute x1, waiting for transfers between devices: 5.33 us -> 8.2 us  [local(): below = lax.ppermute(coarse[..., -1], 'wide', ring('wide', n_wide, 1))]
    slice x2, local copies, waits for them, and re-layouts: 1.04 us -> 3.14 us  [local(): below = lax.ppermute(coarse[..., -1], 'wide', ring('wide', n_wide, 1))]
    ppermute x1, waiting for transfers between devices: 4.87 us -> 2.78 us  [local(): lax.ppermute(by_x[:, -width:], 'grp', ring('grp', n_grp, 1))]
    ppermute x1, starting transfers between devices: 1.82 us -> 0.01 us  [local(): lax.ppermute(coarse_pop[:, cx - edge:], 'grp', ring('grp', n_grp, 1))]
    ppermute x1 -> x3, starting transfers between devices: 0.03 us -> 1.69 us  [local(): highs.append(lax.ppermute(first, axes, pairs))]
  transfers between devices with their start and end apart: 8 -> 10, of which waited for: 6 -> 7; matrix products, arithmetic and copies ran while one was open for 3% -> 7% of each run, Pallas kernels for 6% -> 12%
where the time goes in v2:
time: 66.2 us; the launch traced here: 65.9 us
  waiting for transfers between devices  30.9 us (47%)
  starting transfers between devices  18.3 us (28%)
  Pallas kernels  11.5 us (17%)
  local copies, waits for them, and re-layouts  4.39 us (7%)
  between operations  0.76 us (1%)
    ppermute x1, waiting for transfers between devices, local(): lax.ppermute(coarse_pop[:, :edge], 'grp', ring('grp', n_grp, -1))  8.62 us
    ppermute x1, waiting for transfers between devices, local(): below = lax.ppermute(coarse[..., -1], 'wide', ring('wide', n_wide, 1))  8.2 us
    all_to_all x1, starting transfers between devices, local(): spread = lax.all_to_all(pieces, axes, 0, 0, tiled=True)  7.33 us
    ppermute x1, waiting for transfers between devices, local(): lax.ppermute(coarse_pop[:, cx - edge:], 'grp', ring('grp', n_grp, 1))  5.33 us
    pallas_call x1, Pallas kernels, local(): call(functools.partial(fine_body, ch_count, k_count), f32(Q * B * nq, LAN...  3.43 us
    all_to_all x1, starting transfers between devices, local(): lax.all_to_all(outgoing.reshape(devices, rows, k_count, LANES), axes, 0,...  3.3 us
    slice x2, local copies, waits for them, and re-layouts, local(): below = lax.ppermute(coarse[..., -1], 'wide', ring('wide', n_wide, 1))  3.14 us
    ppermute x1, starting transfers between devices, local(): lax.ppermute(by_x[:, :width], 'grp', ring('grp', n_grp, -1))  2.91 us
  transfers between devices with their start and end apart: 10, of which 7 were waited for; matrix products, arithmetic and copies ran while one was open for 7% of the time, Pallas kernels for 12%

profile of v2, /device:TPU:0, one launch (start us, length us, event | category | flops | bytes accessed | tf_op | source)
XLA Modules:
  0.0 65.9 jit_solution(18257364975611447604)
XLA Ops:
  0.6 7.3 %all-to-all-start = ((f32[32,19,2,128]{3,2,1,0:T(2,128)}), f32[32,19,2,128]{3,2,1,0:T(2,128)S(1)}, u32[]{:S(2)}, u32[]{:S(2)}) async-start(f32[32,19,2,128]{3,2,1,0:T(2,128)} %bitcast.29), calls=%async_computation | async-start | bytes 1245184 | tf_op jit(solution)/shard_map/all_to_all | solution.py:502
  8.0 2.7 %collective-permute-start.1 = (f32[19,2,8,128]{3,2,1,0:T(8,128)S(1)}, f32[19,2,8,128]{3,2,1,0:T(8,128)S(1)}, u32[]{:S(2)}, u32[]{:S(2)}) collective-permute-start(f32[19,2,8,128]{3,2,1,0:T(8,128)S(1)} %get-tuple-element.31), channel_id=1, source_target_pairs={{0,24},{8,0},{16,8},{24,16},{1,25},{9,1},{17,9},{25,17},{2,26},{10... | collective-permute-start | bytes 466952 | tf_op jit(solution)/shard_map/ppermute | solution.py:505
  10.7 0.0 collective-permute-start
  10.7 8.6 %collective-permute-done.1 = f32[19,2,8,128]{3,2,1,0:T(8,128)S(1)} collective-permute-done((f32[19,2,8,128]{3,2,1,0:T(8,128)S(1)}, f32[19,2,8,128]{3,2,1,0:T(8,128)S(1)}, u32[]{:S(2)}, u32[]{:S(2)}) %collective-permute-start.1) | collective-permute-done | bytes 155680 | tf_op jit(solution)/shard_map/ppermute | solution.py:505
  19.4 5.3 %collective-permute-done = f32[19,2,8,128]{3,2,1,0:T(8,128)S(1)} collective-permute-done((f32[19,2,8,128]{3,2,1,0:T(8,128)S(1)}, f32[19,2,8,128]{3,2,1,0:T(8,128)S(1)}, u32[]{:S(2)}, u32[]{:S(2)}) %collective-permute-start) | collective-permute-done | bytes 155680 | tf_op jit(solution)/shard_map/ppermute | solution.py:504
  24.7 0.1 pad_maximum_fusion.state
  24.8 0.0 copy-start
  24.8 1.5 %all-to-all-done = f32[32,19,2,128]{3,2,1,0:T(2,128)S(1)} async-done(((f32[32,19,2,128]{3,2,1,0:T(2,128)}), f32[32,19,2,128]{3,2,1,0:T(2,128)S(1)}, u32[]{:S(2)}, u32[]{:S(2)}) %all-to-all-start) | async-done | bytes 622624 | tf_op jit(solution)/shard_map/all_to_all | solution.py:502
  26.3 2.2 %shard_map.50 = f32[1216,128]{1,0:T(8,128)} custom-call(s32[64]{0:T(128)S(1)} %copy-done, f32[1216,128]{1,0:T(8,128)S(1)} %bitcast.23), custom_call_target="tpu_custom_call" | custom-call | flops 1000000 | bytes 1245184 | tf_op jit(solution)/shard_map/pallas_call | solution.py:515
  28.5 3.3 %all-to-all-start.1 = ((f32[32,19,2,128]{3,2,1,0:T(2,128)}), f32[32,19,2,128]{3,2,1,0:T(2,128)S(1)}, u32[]{:S(2)}, u32[]{:S(2)}) async-start(f32[32,19,2,128]{3,2,1,0:T(2,128)} %bitcast.4), calls=%async_computation.1 | async-start | bytes 1245184 | tf_op jit(solution)/shard_map/all_to_all | solution.py:516
  31.9 1.3 %fusion.1 = (f32[19,12,8,1]{3,2,1,0:T(8,128)}, f32[19,12,8,1]{3,2,1,0:T(8,128)S(1)}) fusion(f32[19,12,8,128]{3,2,1,0:T(8,128)S(1)} %pad_maximum_fusion.state), kind=kLoop, calls=%fused_computation.8 | loop fusion | bytes 29184 | tf_op jit(solution)/shard_map/slice | solution.py:519
  33.1 1.9 %copy.10 = f32[19,12,8,1]{0,2,3,1:T(8,128)S(1)} copy(f32[19,12,8,1]{3,2,1,0:T(8,128)} %get-tuple-element.26) | data formatting | bytes 14592 | tf_op jit(solution)/shard_map/slice | solution.py:519
  35.0 0.3 collective-permute-start.2
  35.3 0.7 %copy.11 = f32[19,12,8,1]{0,2,3,1:T(8,128)S(1)} copy(f32[19,12,8,1]{3,2,1,0:T(8,128)S(1)} %get-tuple-element.27) | data formatting | bytes 14592 | tf_op jit(solution)/shard_map/slice | solution.py:520
  36.0 2.8 %shard_map.52 = (f32[19,8,8,128]{3,2,1,0:T(8,128)S(1)}, f32[19,8,128]{2,1,0:T(8,128)S(1)}, f32[8,128]{1,0:T(8,128)S(1)}) custom-call(f32[19,12,8,128]{3,2,1,0:T(8,128)S(1)} %pad_maximum_fusion.state), custom_call_target="tpu_custom_call" | custom-call | flops 10000000 | bytes 1000000 | tf_op jit(solution)/shard_map/pallas_call | solution.py:530
  38.8 8.2 %collective-permute-done.2 = f32[19,12,8]{0,2,1:T(8,128)S(1)} collective-permute-done((f32[19,12,8]{0,2,1:T(8,128)S(1)}, f32[19,12,8]{0,2,1:T(8,128)S(1)}, u32[]{:S(2)}, u32[]{:S(2)}) %collective-permute-start.2) | collective-permute-done | bytes 7328 | tf_op jit(solution)/shard_map/ppermute | solution.py:519
  47.0 0.3 copy.12
  47.3 0.2 broadcast_in_dim.2
  47.5 1.0 %shard_map.51.ghosts = f32[2,6,2,24,128]{4,3,2,1,0:T(8,128)S(1)} custom-call(f32[2,456,8]{2,1,0:T(8,128)S(1)} %bitcast.24, f32[8,256]{1,0:T(8,128)S(1)} %fusion.spread), custom_call_target="tpu_custom_call" | custom-call | flops 1000000 | bytes 1000000 | tf_op jit(solution)/shard_map/pallas_call | solution.py:524
  48.5 2.2 %all-to-all-done.1 = f32[32,19,2,128]{3,2,1,0:T(2,128)S(1)} async-done(((f32[32,19,2,128]{3,2,1,0:T(2,128)}), f32[32,19,2,128]{3,2,1,0:T(2,128)S(1)}, u32[]{:S(2)}, u32[]{:S(2)}) %all-to-all-start.1) | async-done | bytes 622624 | tf_op jit(solution)/shard_map/all_to_all | solution.py:516
  50.7 0.1 collective-permute-start.3
  50.8 2.9 %collective-permute-start.4 = (f32[19,16,128]{2,1,0:T(8,128)S(1)}, f32[19,16,128]{2,1,0:T(8,128)S(1)}, u32[]{:S(2)}, u32[]{:S(2)}) collective-permute-start(f32[19,16,128]{2,1,0:T(8,128)S(1)} %get-tuple-element.28), channel_id=1, source_target_pairs={{0,24},{8,0},{16,8},{24,16},{1,25},{9,1},{17,9},{25,17},{2,26},{10... | collective-permute-start | bytes 466952 | tf_op jit(solution)/shard_map/ppermute | solution.py:548
  53.7 0.4 shard_map.54
  54.1 0.0 collective-permute-start.5
  54.1 0.1 collective-permute-start.6
  54.2 1.6 %collective-permute-start.7 = (f32[2,8,128]{2,1,0:T(8,128)S(1)}, f32[2,8,128]{2,1,0:T(8,128)S(1)}, u32[]{:S(2)}, u32[]{:S(2)}) collective-permute-start(f32[2,8,128]{2,1,0:T(8,128)S(1)} %get-tuple-element.22), channel_id=1, source_target_pairs={{1,24},{2,25},{3,26},{4,27},{5,28},{6,29},{7,30},{0,31},{9,0},{10,... | collective-permute-start | bytes 24584 | tf_op jit(solution)/shard_map/ppermute | solution.py:562
  55.8 2.8 %collective-permute-done.3 = f32[19,16,128]{2,1,0:T(8,128)S(1)} collective-permute-done((f32[19,16,128]{2,1,0:T(8,128)S(1)}, f32[19,16,128]{2,1,0:T(8,128)S(1)}, u32[]{:S(2)}, u32[]{:S(2)}) %collective-permute-start.3) | collective-permute-done | bytes 155680 | tf_op jit(solution)/shard_map/ppermute | solution.py:547
  58.6 2.2 %collective-permute-done.4 = f32[19,16,128]{2,1,0:T(8,128)S(1)} collective-permute-done((f32[19,16,128]{2,1,0:T(8,128)S(1)}, f32[19,16,128]{2,1,0:T(8,128)S(1)}, u32[]{:S(2)}, u32[]{:S(2)}) %collective-permute-start.4) | collective-permute-done | bytes 155680 | tf_op jit(solution)/shard_map/ppermute | solution.py:548
  60.8 3.4 %shard_map.53 = f32[1216,128]{1,0:T(8,128)} custom-call(f32[1216,128]{1,0:T(8,128)S(1)} %bitcast.22, f32[304,128]{1,0:T(8,128)S(1)} %bitcast.25, f32[304,128]{1,0:T(8,128)S(1)} %bitcast.27, f32[2,6,2,24,128]{4,3,2,1,0:T(8,128)S(1)} %shard_map.51.ghosts), custom_call_target="tpu_custom_call" | custom-call | flops 10000000 | bytes 1000000 | tf_op jit(solution)/shard_map/pallas_call | solution.py:565
  64.2 0.0 collective-permute-done.6.high_left
  64.2 0.0 collective-permute-done.7.high_right
  64.2 1.7 %shard_map.55 = f32[19,8,8,128]{3,2,1,0:T(8,128)} custom-call(f32[304,128]{1,0:T(8,128)S(1)} %bitcast.26, f32[304,128]{1,0:T(8,128)S(1)} %bitcast.28, f32[2,8,128]{2,1,0:T(8,128)S(1)} %get-tuple-element.21.low, f32[2,8,128]{2,1,0:T(8,128)S(1)} %collective-permute-done.5.high, f32[2,8,128]{2,1,0:T(8,128)S(1)} %collective-permute-done.6.high_left, ...), custom_call_target="tpu_custom_call" | custom-call | flops 1000000 | bytes 1000000 | tf_op jit(solution)/shard_map/pallas_call | solution.py:578
  (9 shorter events, 0.1 us)
Async XLA Ops:
  0.6 7.4 %copy-start.1 = (f32[19,8,8,128]{3,2,1,0:T(8,128)S(1)}, f32[19,8,8,128]{3,2,1,0:T(8,128)}, u32[]{:S(2)}) copy-start(f32[19,8,8,128]{3,2,1,0:T(8,128)} %param.4) | copy-start | bytes 1867780
  0.6 25.7 %all-to-all-start = ((f32[32,19,2,128]{3,2,1,0:T(2,128)}), f32[32,19,2,128]{3,2,1,0:T(2,128)S(1)}, u32[]{:S(2)}, u32[]{:S(2)}) async-start(f32[32,19,2,128]{3,2,1,0:T(2,128)} %bitcast.29), calls=%async_computation | async-start | bytes 1245184 | tf_op jit(solution)/shard_map/all_to_all | solution.py:502
  8.0 11.3 %collective-permute-start.1 = (f32[19,2,8,128]{3,2,1,0:T(8,128)S(1)}, f32[19,2,8,128]{3,2,1,0:T(8,128)S(1)}, u32[]{:S(2)}, u32[]{:S(2)}) collective-permute-start(f32[19,2,8,128]{3,2,1,0:T(8,128)S(1)} %get-tuple-element.31), channel_id=1, source_target_pairs={{0,24},{8,0},{16,8},{24,16},{1,25},{9,1},{17,9},{25,17},{2,26},{10... | collective-permute-start | bytes 466952 | tf_op jit(solution)/shard_map/ppermute | solution.py:505
  10.7 14.0 %collective-permute-start = (f32[19,2,8,128]{3,2,1,0:T(8,128)S(1)}, f32[19,2,8,128]{3,2,1,0:T(8,128)S(1)}, u32[]{:S(2)}, u32[]{:S(2)}) collective-permute-start(f32[19,2,8,128]{3,2,1,0:T(8,128)S(1)} %get-tuple-element.30), channel_id=1, source_target_pairs={{0,8},{8,16},{16,24},{24,0},{1,9},{9,17},{17,25},{25,1},{2,10},{10... | collective-permute-start | bytes 466952 | tf_op jit(solution)/shard_map/ppermute | solution.py:504
  24.8 1.5 %copy-start = (s32[64]{0:T(128)S(1)}, s32[64]{0:T(128)}, u32[]{:S(2)}) copy-start(s32[64]{0:T(128)} %slot_ref.1) | copy-start | bytes 772
  28.5 22.2 %all-to-all-start.1 = ((f32[32,19,2,128]{3,2,1,0:T(2,128)}), f32[32,19,2,128]{3,2,1,0:T(2,128)S(1)}, u32[]{:S(2)}, u32[]{:S(2)}) async-start(f32[32,19,2,128]{3,2,1,0:T(2,128)} %bitcast.4), calls=%async_computation.1 | async-start | bytes 1245184 | tf_op jit(solution)/shard_map/all_to_all | solution.py:516
  35.0 12.0 %collective-permute-start.2 = (f32[19,12,8]{0,2,1:T(8,128)S(1)}, f32[19,12,8]{0,2,1:T(8,128)S(1)}, u32[]{:S(2)}, u32[]{:S(2)}) collective-permute-start(f32[19,12,8]{0,2,1:T(8,128)S(1)} %bitcast.33), channel_id=1, source_target_pairs={{0,1},{1,2},{2,3},{3,4},{4,5},{5,6},{6,7},{7,0},{8,9},{9,10},{10,1... | collective-permute-start | bytes 21896 | tf_op jit(solution)/shard_map/ppermute | solution.py:519
  50.7 7.8 %collective-permute-start.3 = (f32[19,16,128]{2,1,0:T(8,128)S(1)}, f32[19,16,128]{2,1,0:T(8,128)S(1)}, u32[]{:S(2)}, u32[]{:S(2)}) collective-permute-start(f32[19,16,128]{2,1,0:T(8,128)S(1)} %get-tuple-element.29), channel_id=1, source_target_pairs={{0,8},{8,16},{16,24},{24,0},{1,9},{9,17},{17,25},{25,1},{2,10},{10... | collective-permute-start | bytes 466952 | tf_op jit(solution)/shard_map/ppermute | solution.py:547
  50.8 10.0 %collective-permute-start.4 = (f32[19,16,128]{2,1,0:T(8,128)S(1)}, f32[19,16,128]{2,1,0:T(8,128)S(1)}, u32[]{:S(2)}, u32[]{:S(2)}) collective-permute-start(f32[19,16,128]{2,1,0:T(8,128)S(1)} %get-tuple-element.28), channel_id=1, source_target_pairs={{0,24},{8,0},{16,8},{24,16},{1,25},{9,1},{17,9},{25,17},{2,26},{10... | collective-permute-start | bytes 466952 | tf_op jit(solution)/shard_map/ppermute | solution.py:548
  54.1 10.1 %collective-permute-start.5 = (f32[2,8,128]{2,1,0:T(8,128)S(1)}, f32[2,8,128]{2,1,0:T(8,128)S(1)}, u32[]{:S(2)}, u32[]{:S(2)}) collective-permute-start(f32[2,8,128]{2,1,0:T(8,128)S(1)} %get-tuple-element.22), channel_id=1, source_target_pairs={{1,0},{2,1},{3,2},{4,3},{5,4},{6,5},{7,6},{0,7},{9,8},{10,9},{11,1... | collective-permute-start | bytes 24584 | tf_op jit(solution)/shard_map/ppermute | solution.py:562
  54.1 10.1 %collective-permute-start.6 = (f32[2,8,128]{2,1,0:T(8,128)S(1)}, f32[2,8,128]{2,1,0:T(8,128)S(1)}, u32[]{:S(2)}, u32[]{:S(2)}) collective-permute-start(f32[2,8,128]{2,1,0:T(8,128)S(1)} %get-tuple-element.22), channel_id=1, source_target_pairs={{1,8},{2,9},{3,10},{4,11},{5,12},{6,13},{7,14},{0,15},{9,16},{10,1... | collective-permute-start | bytes 24584 | tf_op jit(solution)/shard_map/ppermute | solution.py:562
  54.2 10.0 %collective-permute-start.7 = (f32[2,8,128]{2,1,0:T(8,128)S(1)}, f32[2,8,128]{2,1,0:T(8,128)S(1)}, u32[]{:S(2)}, u32[]{:S(2)}) collective-permute-start(f32[2,8,128]{2,1,0:T(8,128)S(1)} %get-tuple-element.22), channel_id=1, source_target_pairs={{1,24},{2,25},{3,26},{4,27},{5,28},{6,29},{7,30},{0,31},{9,0},{10,... | collective-permute-start | bytes 24584 | tf_op jit(solution)/shard_map/ppermute | solution.py:562

commit v3 on v2

--- a/solution.py
+++ b/solution.py
@@ -7,6 +7,7 @@
 from jax.experimental.layout import Layout, with_layout_constraint
 from jax.experimental.pallas import tpu as pltpu
 from jax.sharding import PartitionSpec as P
+
 
 B = 16
 LANES = 128
@@ -144,16 +145,14 @@
 
 
 def regroup_body(blocks, k_blocks, rows, slot_ref, in_ref, out_ref):
-    def step(b, carry):
+    for b in range(blocks):
         s = slot_ref[b]
         source = (b // k_blocks) * (rows * k_blocks) + b % k_blocks
-        target = (s // k_blocks) * (rows * k_blocks) + s % k_blocks
+        owner = lax.div(s, k_blocks)
+        target = owner * (rows * k_blocks) + (s - owner * k_blocks)
         out_ref[pl.ds(target, rows, stride=k_blocks), :] = in_ref[
             pl.ds(source, rows, stride=k_blocks), :
         ]
-        return carry
-
-    lax.fori_loop(0, blocks, step, 0, unroll=4)
 
 
 def lane_ids():
@@ -227,7 +226,7 @@
             return ghosts[side, place, ch, pl.ds(r, SUB), :]
 
         shift_y, shift_z = fine_shifts(ch_count, k_count, ghost)
-        density, streams = [], []
+        streams = []
         for q in qs:
             low = [parts[n, q, pl.ds(PAD + r - 1, SUB), :] for n in range(3)]
             high = [parts[n, q, pl.ds(PAD + r + 1, SUB), :] for n in range(3)]
@@ -474,8 +473,16 @@
             out[i, x] = jnp.where(touched, column, step[i, x])
 
 
-def ring(axis, count, step):
+def ring(count, step):
     return [(i, (i + step) % count) for i in range(count)]
+
+
+def slab_pairs(n_grp, n_wide, up, across):
+    return [
+        (g * n_wide + w, (g + across) % n_grp * n_wide + (w + up) % n_wide)
+        for g in range(n_grp)
+        for w in range(n_wide)
+    ]
 
 
 def local(fine_pop, coarse_pop, new_slot):
@@ -501,10 +508,12 @@
     pieces = pieces.reshape(devices, rows, k_count, LANES)
     spread = lax.all_to_all(pieces, axes, 0, 0, tiled=True)
     edge = HALO // 2
-    coarse_left = lax.ppermute(coarse_pop[:, cx - edge :], "grp", ring("grp", n_grp, 1))
-    coarse_right = lax.ppermute(coarse_pop[:, :edge], "grp", ring("grp", n_grp, -1))
-    coarse = jnp.concatenate([coarse_left, coarse_pop, coarse_right], axis=1)
-    spread, coarse = lax.optimization_barrier((spread, coarse))
+    coarse_left = lax.ppermute(coarse_pop[:, cx - edge :], "grp", ring(n_grp, 1))
+    coarse_right = lax.ppermute(coarse_pop[:, :edge], "grp", ring(n_grp, -1))
+    last = coarse_pop[..., -1]
+    below = []
+    for part, across in ((last[:, cx - edge :], 1), (last, 0), (last[:, :edge], -1)):
+        below.append(lax.ppermute(part, axes, slab_pairs(n_grp, n_wide, 1, across)))
     total = devices * rows * k_count
     regroup = call(
         functools.partial(regroup_body, blocks, k_count, rows),
@@ -516,7 +525,8 @@
     arrived = lax.all_to_all(
         outgoing.reshape(devices, rows, k_count, LANES), axes, 0, 0, tiled=True
     )
-    below = lax.ppermute(coarse[..., -1], "wide", ring("wide", n_wide, 1))
+    coarse = jnp.concatenate([coarse_left, coarse_pop, coarse_right], axis=1)
+    below = jnp.concatenate(below, axis=1)
     layers = jnp.repeat(jnp.stack([below, coarse[..., 0]]), 2, axis=2)
     layers = layers.reshape(2, Q * fine_rows, cz)
     lane = jnp.arange(ch_count * LANES) // (2 * B)
@@ -544,8 +554,8 @@
 
     by_x = own.reshape(Q, B * nq, LANES)
     width = HALO * nq
-    left = lax.ppermute(by_x[:, -width:], "grp", ring("grp", n_grp, 1)).reshape(Q * width, LANES)
-    right = lax.ppermute(by_x[:, :width], "grp", ring("grp", n_grp, -1)).reshape(Q * width, LANES)
+    left = lax.ppermute(by_x[:, -width:], "grp", ring(n_grp, 1)).reshape(Q * width, LANES)
+    right = lax.ppermute(by_x[:, :width], "grp", ring(n_grp, -1)).reshape(Q * width, LANES)
 
     low, first = call(
         functools.partial(restrict_body, ch_count, k_count),
@@ -554,12 +564,7 @@
     )(own)
     highs = []
     for across in (0, 1, -1):
-        pairs = [
-            (g * n_wide + (w + 1) % n_wide, (g + across) % n_grp * n_wide + w)
-            for g in range(n_grp)
-            for w in range(n_wide)
-        ]
-        highs.append(lax.ppermute(first, axes, pairs))
+        highs.append(lax.ppermute(first, axes, slab_pairs(n_grp, n_wide, -1, across)))
 
     padded = PAD + fine_rows + PAD
     fine = call(

time: 66.2 us -> 68.2 us (1.030)
  starting transfers between devices: 18.3 us -> 25.3 us
  local copies, waits for them, and re-layouts: 4.39 us -> 2.08 us
  waiting for transfers between devices: 30.9 us -> 29 us
    all_to_all x1, waiting for transfers between devices: 1.53 us -> 17.6 us  [local(): spread = lax.all_to_all(pieces, axes, 0, 0, tiled=True)]
    ppermute x8 -> x10, waiting for transfers between devices: 27.2 us -> 11.3 us  [the longest x3 9.31 us: local(): below.append(lax.ppermute(part, axes, slab_pairs(n_grp, n_wide, 1, across)))]
    ppermute x8 -> x10, starting transfers between devices: 7.66 us -> 15.3 us  [the longest x3 5.28 us: local(): lax.ppermute(first, axes, slab_pairs(n_grp, n_wide, -1, across))]
    slice x3, local copies, waits for them, and re-layouts: 3.16 us -> 0.25 us  [the longest x1 0.23 us: local(): last = coarse_pop[..., -1]]
    all_to_all x1, waiting for transfers between devices: 2.2 us -> 0.01 us  [local(): lax.all_to_all(outgoing.reshape(devices, rows, k_count, LANES), axes, 0,...]
    all_to_all x1, starting transfers between devices: 3.3 us -> 2.61 us  [local(): lax.all_to_all(outgoing.reshape(devices, rows, k_count, LANES), axes, 0,...]
  transfers between devices with their start and end apart: 10 -> 12, of which waited for: 7 -> 4; matrix products, arithmetic and copies ran while one was open for 7% -> 3% of each run, Pallas kernels for 12% -> 13%
where the time goes in v3:
time: 68.2 us; the launch traced here: 68 us
  waiting for transfers between devices  29 us (43%)
  starting transfers between devices  25.3 us (37%)
  Pallas kernels  10.9 us (16%)
  local copies, waits for them, and re-layouts  2.08 us (3%)
  between operations  0.77 us (1%)
    all_to_all x1, waiting for transfers between devices, local(): spread = lax.all_to_all(pieces, axes, 0, 0, tiled=True)  17.6 us
    ppermute x3, waiting for transfers between devices, local(): below.append(lax.ppermute(part, axes, slab_pairs(n_grp, n_wide, 1, across)))  9.31 us
    all_to_all x1, starting transfers between devices, local(): spread = lax.all_to_all(pieces, axes, 0, 0, tiled=True)  7.33 us
    ppermute x3, starting transfers between devices, local(): lax.ppermute(first, axes, slab_pairs(n_grp, n_wide, -1, across))  5.28 us
    ppermute x3, starting transfers between devices, local(): below.append(lax.ppermute(part, axes, slab_pairs(n_grp, n_wide, 1, across)))  4.11 us
    pallas_call x1, Pallas kernels, local(): call(functools.partial(fine_body, ch_count, k_count), f32(Q * B * nq, LAN...  3.43 us
    pallas_call x1, Pallas kernels, local(): call(functools.partial(coarse_body, planes), [f32(Q, cx, cz, cy), f32(Q,...  2.8 us
    all_to_all x1, starting transfers between devices, local(): lax.all_to_all(outgoing.reshape(devices, rows, k_count, LANES), axes, 0,...  2.61 us
  transfers between devices with their start and end apart: 12, of which 4 were waited for; matrix products, arithmetic and copies ran while one was open for 3% of the time, Pallas kernels for 13%

profile of v3, /device:TPU:0, one launch (start us, length us, event | category | flops | bytes accessed | tf_op | source)
XLA Modules:
  0.0 68.0 jit_solution(13943726094281246798)
XLA Ops:
  0.6 7.3 %all-to-all-start = ((f32[32,19,2,128]{3,2,1,0:T(2,128)}), f32[32,19,2,128]{3,2,1,0:T(2,128)S(1)}, u32[]{:S(2)}, u32[]{:S(2)}) async-start(f32[32,19,2,128]{3,2,1,0:T(2,128)} %bitcast.32), calls=%async_computation | async-start | bytes 1245184 | tf_op jit(solution)/shard_map/all_to_all | solution.py:509
  8.0 0.2 slice.24
  8.2 0.5 copy.11
  8.7 0.3 collective-permute-start.1
  9.0 17.6 %all-to-all-done = f32[32,19,2,128]{3,2,1,0:T(2,128)S(1)} async-done(((f32[32,19,2,128]{3,2,1,0:T(2,128)}), f32[32,19,2,128]{3,2,1,0:T(2,128)S(1)}, u32[]{:S(2)}, u32[]{:S(2)}) %all-to-all-start) | async-done | bytes 622624 | tf_op jit(solution)/shard_map/all_to_all | solution.py:509
  26.7 1.6 %shard_map.50 = f32[1216,128]{1,0:T(8,128)} custom-call(s32[64]{0:T(128)S(1)} %copy-done, f32[1216,128]{1,0:T(8,128)S(1)} %bitcast.26), custom_call_target="tpu_custom_call" | custom-call | flops 1000000 | bytes 1245184 | tf_op jit(solution)/shard_map/pallas_call | solution.py:524
  28.2 2.6 %all-to-all-start.1 = ((f32[32,19,2,128]{3,2,1,0:T(2,128)}), f32[32,19,2,128]{3,2,1,0:T(2,128)S(1)}, u32[]{:S(2)}, u32[]{:S(2)}) async-start(f32[32,19,2,128]{3,2,1,0:T(2,128)} %bitcast.4), calls=%async_computation.1 | async-start | bytes 1245184 | tf_op jit(solution)/shard_map/all_to_all | solution.py:525
  30.9 1.4 %collective-permute-start = (f32[19,2,8]{0,2,1:T(8,128)S(1)}, f32[19,2,8]{0,2,1:T(8,128)S(1)}, u32[]{:S(2)}, u32[]{:S(2)}) collective-permute-start(f32[19,2,8]{0,2,1:T(8,128)S(1)} %get-tuple-element.26), channel_id=1, source_target_pairs={{0,9},{1,10},{2,11},{3,12},{4,13},{5,14},{6,15},{7,8},{8,17},{9,18... | collective-permute-start | bytes 3656 | tf_op jit(solution)/shard_map/ppermute | solution.py:516
  32.3 2.4 %collective-permute-start.2 = (f32[19,2,8]{0,2,1:T(8,128)S(1)}, f32[19,2,8]{0,2,1:T(8,128)S(1)}, u32[]{:S(2)}, u32[]{:S(2)}) collective-permute-start(f32[19,2,8]{0,2,1:T(8,128)S(1)} %get-tuple-element.27), channel_id=1, source_target_pairs={{0,25},{1,26},{2,27},{3,28},{4,29},{5,30},{6,31},{7,24},{8,1},{9,2... | collective-permute-start | bytes 3656 | tf_op jit(solution)/shard_map/ppermute | solution.py:516
  34.7 0.6 collective-permute-start.3
  35.4 2.3 %collective-permute-start.4 = (f32[19,2,8,128]{3,2,1,0:T(8,128)S(1)}, f32[19,2,8,128]{3,2,1,0:T(8,128)S(1)}, u32[]{:S(2)}, u32[]{:S(2)}) collective-permute-start(f32[19,2,8,128]{3,2,1,0:T(8,128)S(1)} %get-tuple-element.24), channel_id=1, source_target_pairs={{0,24},{8,0},{16,8},{24,16},{1,25},{9,1},{17,9},{25,17},{2,26},{10... | collective-permute-start | bytes 466952 | tf_op jit(solution)/shard_map/ppermute | solution.py:512
  37.7 9.3 %collective-permute-done = f32[19,2,8]{0,2,1:T(8,128)S(1)} collective-permute-done((f32[19,2,8]{0,2,1:T(8,128)S(1)}, f32[19,2,8]{0,2,1:T(8,128)S(1)}, u32[]{:S(2)}, u32[]{:S(2)}) %collective-permute-start) | collective-permute-done | bytes 1248 | tf_op jit(solution)/shard_map/ppermute | solution.py:516
  47.0 0.0 collective-permute-done.2
  47.0 0.0 collective-permute-done.1
  47.0 0.0 collective-permute-done.3
  47.1 0.7 collective-permute-done.4
  47.8 0.7 %copy.8 = f32[19,12,8,1]{0,2,3,1:T(8,128)S(1)} copy(f32[19,12,8,1]{3,2,1,0:T(8,128)S(1)} %bitcast.25) | data formatting | bytes 14592 | tf_op jit(solution)/shard_map/slice | solution.py:530
  48.5 0.3 copy.9
  48.9 0.2 broadcast_in_dim.2
  49.0 1.0 %shard_map.51.ghosts = f32[2,6,2,24,128]{4,3,2,1,0:T(8,128)S(1)} custom-call(f32[2,456,8]{2,1,0:T(8,128)S(1)} %bitcast.27, f32[8,256]{1,0:T(8,128)S(1)} %fusion.spread), custom_call_target="tpu_custom_call" | custom-call | flops 1000000 | bytes 1000000 | tf_op jit(solution)/shard_map/pallas_call | solution.py:534
  50.0 2.8 %shard_map.52 = (f32[19,8,8,128]{3,2,1,0:T(8,128)S(1)}, f32[19,8,128]{2,1,0:T(8,128)S(1)}, f32[8,128]{1,0:T(8,128)S(1)}) custom-call(f32[19,12,8,128]{3,2,1,0:T(8,128)S(1)} %constant_dynamic-update-slice_fusion.state), custom_call_target="tpu_custom_call" | custom-call | flops 10000000 | bytes 1000000 | tf_op jit(solution)/shard_map/pallas_call | solution.py:540
  52.8 0.0 all-to-all-done.1
  52.9 1.9 %collective-permute-start.5 = (f32[19,16,128]{2,1,0:T(8,128)S(1)}, f32[19,16,128]{2,1,0:T(8,128)S(1)}, u32[]{:S(2)}, u32[]{:S(2)}) collective-permute-start(f32[19,16,128]{2,1,0:T(8,128)S(1)} %get-tuple-element.23), channel_id=1, source_target_pairs={{0,8},{8,16},{16,24},{24,0},{1,9},{9,17},{17,25},{25,1},{2,10},{10... | collective-permute-start | bytes 466952 | tf_op jit(solution)/shard_map/ppermute | solution.py:557
  54.8 1.1 %collective-permute-start.6 = (f32[19,16,128]{2,1,0:T(8,128)S(1)}, f32[19,16,128]{2,1,0:T(8,128)S(1)}, u32[]{:S(2)}, u32[]{:S(2)}) collective-permute-start(f32[19,16,128]{2,1,0:T(8,128)S(1)} %get-tuple-element.22), channel_id=1, source_target_pairs={{0,24},{8,0},{16,8},{24,16},{1,25},{9,1},{17,9},{25,17},{2,26},{10... | collective-permute-start | bytes 466952 | tf_op jit(solution)/shard_map/ppermute | solution.py:558
  55.9 0.4 shard_map.54
  56.2 2.2 %collective-permute-start.7 = (f32[2,8,128]{2,1,0:T(8,128)S(1)}, f32[2,8,128]{2,1,0:T(8,128)S(1)}, u32[]{:S(2)}, u32[]{:S(2)}) collective-permute-start(f32[2,8,128]{2,1,0:T(8,128)S(1)} %get-tuple-element.18), channel_id=1, source_target_pairs={{0,7},{1,0},{2,1},{3,2},{4,3},{5,4},{6,5},{7,6},{8,15},{9,8},{10,9... | collective-permute-start | bytes 24584 | tf_op jit(solution)/shard_map/ppermute | solution.py:567
  58.5 1.0 %collective-permute-start.8 = (f32[2,8,128]{2,1,0:T(8,128)S(1)}, f32[2,8,128]{2,1,0:T(8,128)S(1)}, u32[]{:S(2)}, u32[]{:S(2)}) collective-permute-start(f32[2,8,128]{2,1,0:T(8,128)S(1)} %get-tuple-element.18), channel_id=1, source_target_pairs={{0,15},{1,8},{2,9},{3,10},{4,11},{5,12},{6,13},{7,14},{8,23},{9,16... | collective-permute-start | bytes 24584 | tf_op jit(solution)/shard_map/ppermute | solution.py:567
  59.5 2.1 %collective-permute-start.9 = (f32[2,8,128]{2,1,0:T(8,128)S(1)}, f32[2,8,128]{2,1,0:T(8,128)S(1)}, u32[]{:S(2)}, u32[]{:S(2)}) collective-permute-start(f32[2,8,128]{2,1,0:T(8,128)S(1)} %get-tuple-element.18), channel_id=1, source_target_pairs={{0,31},{1,24},{2,25},{3,26},{4,27},{5,28},{6,29},{7,30},{8,7},{9,0... | collective-permute-start | bytes 24584 | tf_op jit(solution)/shard_map/ppermute | solution.py:567
  61.5 0.0 collective-permute-done.5
  61.5 1.3 %collective-permute-done.6 = f32[19,16,128]{2,1,0:T(8,128)S(1)} collective-permute-done((f32[19,16,128]{2,1,0:T(8,128)S(1)}, f32[19,16,128]{2,1,0:T(8,128)S(1)}, u32[]{:S(2)}, u32[]{:S(2)}) %collective-permute-start.6) | collective-permute-done | bytes 155680 | tf_op jit(solution)/shard_map/ppermute | solution.py:558
  62.9 3.4 %shard_map.53 = f32[1216,128]{1,0:T(8,128)} custom-call(f32[1216,128]{1,0:T(8,128)S(1)} %bitcast.24, f32[304,128]{1,0:T(8,128)S(1)} %bitcast.28, f32[304,128]{1,0:T(8,128)S(1)} %bitcast.30, f32[2,6,2,24,128]{4,3,2,1,0:T(8,128)S(1)} %shard_map.51.ghosts), custom_call_target="tpu_custom_call" | custom-call | flops 10000000 | bytes 1000000 | tf_op jit(solution)/shard_map/pallas_call | solution.py:570
  66.3 1.7 %shard_map.55 = f32[19,8,8,128]{3,2,1,0:T(8,128)} custom-call(f32[304,128]{1,0:T(8,128)S(1)} %bitcast.29, f32[304,128]{1,0:T(8,128)S(1)} %bitcast.31, f32[2,8,128]{2,1,0:T(8,128)S(1)} %get-tuple-element.17.low, f32[2,8,128]{2,1,0:T(8,128)S(1)} %collective-permute-done.7.high, f32[2,8,128]{2,1,0:T(8,128)S(1)} %collective-permute-done.8.high_left, ...), custom_call_target="tpu_custom_call" | custom-call | flops 1000000 | bytes 1000000 | tf_op jit(solution)/shard_map/pallas_call | solution.py:583
  (17 shorter events, 0.2 us)
Async XLA Ops:
  0.6 7.4 %copy-start.1 = (f32[19,8,8,128]{3,2,1,0:T(8,128)S(1)}, f32[19,8,8,128]{3,2,1,0:T(8,128)}, u32[]{:S(2)}) copy-start(f32[19,8,8,128]{3,2,1,0:T(8,128)} %param.4) | copy-start | bytes 1867780
  0.6 26.0 %all-to-all-start = ((f32[32,19,2,128]{3,2,1,0:T(2,128)}), f32[32,19,2,128]{3,2,1,0:T(2,128)S(1)}, u32[]{:S(2)}, u32[]{:S(2)}) async-start(f32[32,19,2,128]{3,2,1,0:T(2,128)} %bitcast.32), calls=%async_computation | async-start | bytes 1245184 | tf_op jit(solution)/shard_map/all_to_all | solution.py:509
  8.7 17.9 %copy-start = (s32[64]{0:T(128)S(1)}, s32[64]{0:T(128)}, u32[]{:S(2)}) copy-start(s32[64]{0:T(128)} %slot_ref.1) | copy-start | bytes 772
  8.7 38.3 %collective-permute-start.1 = (f32[19,8,8]{0,2,1:T(8,128)S(1)}, f32[19,8,8]{0,2,1:T(8,128)S(1)}, u32[]{:S(2)}, u32[]{:S(2)}) collective-permute-start(f32[19,8,8]{0,2,1:T(8,128)S(1)} %bitcast.35), channel_id=1, source_target_pairs={{0,1},{1,2},{2,3},{3,4},{4,5},{5,6},{6,7},{7,0},{8,9},{9,10},{10,1... | collective-permute-start | bytes 14600 | tf_op jit(solution)/shard_map/ppermute | solution.py:516
  28.2 24.6 %all-to-all-start.1 = ((f32[32,19,2,128]{3,2,1,0:T(2,128)}), f32[32,19,2,128]{3,2,1,0:T(2,128)S(1)}, u32[]{:S(2)}, u32[]{:S(2)}) async-start(f32[32,19,2,128]{3,2,1,0:T(2,128)} %bitcast.4), calls=%async_computation.1 | async-start | bytes 1245184 | tf_op jit(solution)/shard_map/all_to_all | solution.py:525
  30.9 16.1 %collective-permute-start = (f32[19,2,8]{0,2,1:T(8,128)S(1)}, f32[19,2,8]{0,2,1:T(8,128)S(1)}, u32[]{:S(2)}, u32[]{:S(2)}) collective-permute-start(f32[19,2,8]{0,2,1:T(8,128)S(1)} %get-tuple-element.26), channel_id=1, source_target_pairs={{0,9},{1,10},{2,11},{3,12},{4,13},{5,14},{6,15},{7,8},{8,17},{9,18... | collective-permute-start | bytes 3656 | tf_op jit(solution)/shard_map/ppermute | solution.py:516
  32.3 14.7 %collective-permute-start.2 = (f32[19,2,8]{0,2,1:T(8,128)S(1)}, f32[19,2,8]{0,2,1:T(8,128)S(1)}, u32[]{:S(2)}, u32[]{:S(2)}) collective-permute-start(f32[19,2,8]{0,2,1:T(8,128)S(1)} %get-tuple-element.27), channel_id=1, source_target_pairs={{0,25},{1,26},{2,27},{3,28},{4,29},{5,30},{6,31},{7,24},{8,1},{9,2... | collective-permute-start | bytes 3656 | tf_op jit(solution)/shard_map/ppermute | solution.py:516
  34.7 12.3 %collective-permute-start.3 = (f32[19,2,8,128]{3,2,1,0:T(8,128)S(1)}, f32[19,2,8,128]{3,2,1,0:T(8,128)S(1)}, u32[]{:S(2)}, u32[]{:S(2)}) collective-permute-start(f32[19,2,8,128]{3,2,1,0:T(8,128)S(1)} %get-tuple-element.25), channel_id=1, source_target_pairs={{0,8},{8,16},{16,24},{24,0},{1,9},{9,17},{17,25},{25,1},{2,10},{10... | collective-permute-start | bytes 466952 | tf_op jit(solution)/shard_map/ppermute | solution.py:511
  35.4 12.4 %collective-permute-start.4 = (f32[19,2,8,128]{3,2,1,0:T(8,128)S(1)}, f32[19,2,8,128]{3,2,1,0:T(8,128)S(1)}, u32[]{:S(2)}, u32[]{:S(2)}) collective-permute-start(f32[19,2,8,128]{3,2,1,0:T(8,128)S(1)} %get-tuple-element.24), channel_id=1, source_target_pairs={{0,24},{8,0},{16,8},{24,16},{1,25},{9,1},{17,9},{25,17},{2,26},{10... | collective-permute-start | bytes 466952 | tf_op jit(solution)/shard_map/ppermute | solution.py:512
  52.9 8.6 %collective-permute-start.5 = (f32[19,16,128]{2,1,0:T(8,128)S(1)}, f32[19,16,128]{2,1,0:T(8,128)S(1)}, u32[]{:S(2)}, u32[]{:S(2)}) collective-permute-start(f32[19,16,128]{2,1,0:T(8,128)S(1)} %get-tuple-element.23), channel_id=1, source_target_pairs={{0,8},{8,16},{16,24},{24,0},{1,9},{9,17},{17,25},{25,1},{2,10},{10... | collective-permute-start | bytes 466952 | tf_op jit(solution)/shard_map/ppermute | solution.py:557
  54.8 8.1 %collective-permute-start.6 = (f32[19,16,128]{2,1,0:T(8,128)S(1)}, f32[19,16,128]{2,1,0:T(8,128)S(1)}, u32[]{:S(2)}, u32[]{:S(2)}) collective-permute-start(f32[19,16,128]{2,1,0:T(8,128)S(1)} %get-tuple-element.22), channel_id=1, source_target_pairs={{0,24},{8,0},{16,8},{24,16},{1,25},{9,1},{17,9},{25,17},{2,26},{10... | collective-permute-start | bytes 466952 | tf_op jit(solution)/shard_map/ppermute | solution.py:558
  56.2 10.0 %collective-permute-start.7 = (f32[2,8,128]{2,1,0:T(8,128)S(1)}, f32[2,8,128]{2,1,0:T(8,128)S(1)}, u32[]{:S(2)}, u32[]{:S(2)}) collective-permute-start(f32[2,8,128]{2,1,0:T(8,128)S(1)} %get-tuple-element.18), channel_id=1, source_target_pairs={{0,7},{1,0},{2,1},{3,2},{4,3},{5,4},{6,5},{7,6},{8,15},{9,8},{10,9... | collective-permute-start | bytes 24584 | tf_op jit(solution)/shard_map/ppermute | solution.py:567
  58.5 7.8 %collective-permute-start.8 = (f32[2,8,128]{2,1,0:T(8,128)S(1)}, f32[2,8,128]{2,1,0:T(8,128)S(1)}, u32[]{:S(2)}, u32[]{:S(2)}) collective-permute-start(f32[2,8,128]{2,1,0:T(8,128)S(1)} %get-tuple-element.18), channel_id=1, source_target_pairs={{0,15},{1,8},{2,9},{3,10},{4,11},{5,12},{6,13},{7,14},{8,23},{9,16... | collective-permute-start | bytes 24584 | tf_op jit(solution)/shard_map/ppermute | solution.py:567
  59.5 6.8 %collective-permute-start.9 = (f32[2,8,128]{2,1,0:T(8,128)S(1)}, f32[2,8,128]{2,1,0:T(8,128)S(1)}, u32[]{:S(2)}, u32[]{:S(2)}) collective-permute-start(f32[2,8,128]{2,1,0:T(8,128)S(1)} %get-tuple-element.18), channel_id=1, source_target_pairs={{0,31},{1,24},{2,25},{3,26},{4,27},{5,28},{6,29},{7,30},{8,7},{9,0... | collective-permute-start | bytes 24584 | tf_op jit(solution)/shard_map/ppermute | solution.py:567

commit v4 on v3

--- a/solution.py
+++ b/solution.py
@@ -39,7 +39,6 @@
 )
 Q = len(VELOCITIES)
 WEIGHTS = (1.0 / 3.0,) + (1.0 / 18.0,) * 6 + (1.0 / 36.0,) * 12
-W_AXIS = WEIGHTS[1]
 W_DIAG = WEIGHTS[7]
 COUPLING = -5.0
 FINE_TAU = 1.1
@@ -87,32 +86,38 @@
     return density, momentum
 
 
-def balances(density, u, scale):
-    base = 1.0 - 1.5 * (u[0] * u[0] + u[1] * u[1] + u[2] * u[2])
-    scaled = {w: density * (w * scale) for w in set(WEIGHTS)}
-    yield 0, scaled[WEIGHTS[0]] * base
-    for i in range(1, Q, 2):
-        along = None
-        for j in range(3):
-            c = VELOCITIES[i][j]
-            if c:
-                if along is None:
-                    along = u[j] if c > 0 else -u[j]
-                else:
-                    along = along + u[j] if c > 0 else along - u[j]
-        weight = scaled[WEIGHTS[i]]
-        even = weight * (base + 4.5 * (along * along))
-        odd = weight * (3.0 * along)
-        yield i, even + odd
-        yield i + 1, even - odd
+def balances(density, flux, scale):
+    w = density * (W_DIAG * scale)
+    half = 1.5 / density
+    v = [x * half for x in flux]
+    g = [x * (3.0 * W_DIAG * scale) for x in flux]
+    g2 = [x + x for x in g]
+    h = [g[j] * v[j] for j in range(3)]
+    total = h[0] + h[1] + h[2]
+    base = w - total * (1.0 / 3.0)
+    base2 = base + base
+    yield 0, base2 * (0.5 * WEIGHTS[0] / W_DIAG)
+    for j in range(3):
+        even = base2 + (h[j] + h[j])
+        yield 2 * j + 1, even + g2[j]
+        yield 2 * j + 2, even - g2[j]
+    all_h = base + total
+    i = 7
+    for a, b, c in ((0, 1, 2), (0, 2, 1), (1, 2, 0)):
+        even = all_h - h[c]
+        cross = g2[a] * v[b]
+        for sign in (1, -1):
+            side = even + cross if sign > 0 else even - cross
+            odd = g[a] + g[b] if sign > 0 else g[a] - g[b]
+            yield i, side + odd
+            yield i + 1, side - odd
+            i += 2
 
 
 def rescaled(f, factor, wanted):
     density, momentum = moments(f)
-    inverse = 1.0 / density
-    u = [m * inverse for m in momentum]
     found = {}
-    for i, balance in balances(density, u, 1.0):
+    for i, balance in balances(density, momentum, 1.0):
         if i in wanted:
             found[i] = balance + factor * (f[i] - balance)
     return 1.0 - jnp.exp(-density), found
@@ -125,23 +130,21 @@
     back = shift_z(p, 1)
     n = range(len(p))
     dy = [above[q] - below[q] for q in n]
-    sy = [above[q] + below[q] for q in n]
     dz = [front[q] - back[q] for q in n]
-    tx = [W_AXIS * p[q] + W_DIAG * (sy[q] + (front[q] + back[q])) for q in n]
-    mixed = [W_AXIS * p[q] + W_DIAG * sy[q] for q in n]
+    mixed = [(p[q] + p[q]) + (above[q] + below[q]) for q in n]
+    tx = [mixed[q] + (front[q] + back[q]) for q in n]
     mixed_front = shift_z(mixed, -1)
     mixed_back = shift_z(mixed, 1)
     dy_front = shift_z(dy, -1)
     dy_back = shift_z(dy, 1)
-    gy = [W_AXIS * dy[q] + W_DIAG * (dy_front[q] + dy_back[q]) for q in n]
+    gy = [(dy[q] + dy[q]) + (dy_front[q] + dy_back[q]) for q in n]
     gz = [mixed_front[q] - mixed_back[q] for q in n]
-    return tx, [W_DIAG * v for v in dy], [W_DIAG * v for v in dz], gy, gz
-
-
-def velocity_of(density, momentum, potential, pull, tau):
-    inverse = 1.0 / density
-    force = (-tau * COUPLING) * potential
-    return [(momentum[j] + force * pull[j]) * inverse for j in range(3)]
+    return tx, dy, dz, gy, gz
+
+
+def flux_of(momentum, potential, pull, tau):
+    force = (-tau * COUPLING * W_DIAG) * potential
+    return [momentum[j] + force * pull[j] for j in range(3)]
 
 
 def regroup_body(blocks, k_blocks, rows, slot_ref, in_ref, out_ref):
@@ -200,22 +203,23 @@
     return shift_y, shift_z
 
 
-def fine_step(src, offset, dst, ghosts, parts, ch_count, k_count, chunks):
-    nq = ch_count * k_count
-    qs = range(nq)
+def substep(load, store, ghosts, start, parts, ch_count, k_count, chunks, density_of=None):
+    qs = range(ch_count * k_count)
     for chunk in range(chunks):
         r = chunk * SUB
-        f = [[src[i, q, pl.ds(offset + r, SUB), :] for i in range(Q)] for q in qs]
-        moved = [moments(f[q]) for q in qs]
-        p = [1.0 - jnp.exp(-moved[q][0]) for q in qs]
 
         def ghost(side, which, ch, r=r):
-            return ghosts[side, NG - 1, ch, pl.ds(r, SUB), :]
-
+            return ghosts[side, NG - 1, ch, pl.ds(start + r, SUB), :]
+
+        moved = [moments([load(i, q, r) for i in range(Q)]) for q in qs]
+        density = [moved[q][0] for q in qs]
+        if density_of is not None:
+            density = [density_of(q, r, density[q]) for q in qs]
+        p = [1.0 - jnp.exp(-density[q]) for q in qs]
         shift_y, shift_z = fine_shifts(ch_count, k_count, ghost)
         tx, dy, dz, gy, gz = gradient_parts(p, shift_y, shift_z)
         for q in qs:
-            values = (tx[q], dy[q], dz[q], gy[q], gz[q], p[q], moved[q][0], *moved[q][1])
+            values = (tx[q], dy[q], dz[q], gy[q], gz[q], p[q], density[q], *moved[q][1])
             for n, v in enumerate(values):
                 parts[n, q, pl.ds(PAD + r, SUB), :] = v
     for chunk in range(chunks):
@@ -223,7 +227,7 @@
 
         def ghost(side, which, ch, r=r):
             place = (UP if side == 0 else DOWN).index(which)
-            return ghosts[side, place, ch, pl.ds(r, SUB), :]
+            return ghosts[side, place, ch, pl.ds(start + r, SUB), :]
 
         shift_y, shift_z = fine_shifts(ch_count, k_count, ghost)
         streams = []
@@ -234,49 +238,181 @@
                 parts[n, q, pl.ds(PAD + r, SUB), :] for n in range(3, 10)
             )
             pull = [high[0] - low[0], gy + (high[1] + low[1]), gz + (high[2] + low[2])]
-            u = velocity_of(rho, (mx, my, mz), p, pull, FINE_TAU)
-            streams.append(balances(rho, u, 1.0 / FINE_TAU))
+            flux = flux_of((mx, my, mz), p, pull, FINE_TAU)
+            streams.append(balances(rho, flux, 1.0 / FINE_TAU))
         for i in range(Q):
             cx, cy, cz = VELOCITIES[i]
             post = []
             for q in qs:
                 _, balance = next(streams[q])
-                h = src[i, q, pl.ds(offset + r, SUB), :]
-                post.append(h * (1.0 - 1.0 / FINE_TAU) + balance)
+                post.append(load(i, q, r) * (1.0 - 1.0 / FINE_TAU) + balance)
             if cy:
                 post = shift_y(post, cy, i)
             if cz:
                 post = shift_z(post, cz)
             for q in qs:
-                dst[i, q, pl.ds(PAD + r + cx, SUB), :] = post[q]
-
-
-def fine_body(ch_count, k_count, own, left, right, ghosts, out, first, second, third, parts):
+                store(i, q, r, cx, post[q])
+
+
+CROSS = 5
+FROM_DENSITY = Q
+FROM_ENTER = Q + 1
+FROM_PARTIAL = Q + 1 + CROSS
+SENT = Q + 2 + CROSS
+
+
+def edge_rows(nq):
+    return SENT * nq + PLANES * (HALO // 2)
+
+
+def sent_rows(nq):
+    return -(-edge_rows(nq) // SUB) * SUB
+
+
+def along(c):
+    return [i for i in range(Q) if VELOCITIES[i][0] == c]
+
+
+def send_body(
+    ch_count, k_count, own, ghosts, to_left, to_right, low, high, rim, moved, parts
+):
     nq = ch_count * k_count
-
-    def gather(i, carry):
+    per = B * nq
+    edge = HALO // 2
+
+    for i in range(Q):
         for q in range(nq):
-            first[i, q, pl.ds(0, HALO), :] = left[pl.ds(i * (HALO * nq) + q, HALO, stride=nq), :]
-            first[i, q, pl.ds(HALO, B), :] = own[pl.ds(i * (B * nq) + q, B, stride=nq), :]
-            first[i, q, pl.ds(HALO + B, HALO), :] = right[
-                pl.ds(i * (HALO * nq) + q, HALO, stride=nq), :
+            rim[i, q, pl.ds(0, HALO), :] = own[pl.ds(i * per + q, HALO, stride=nq), :]
+            rim[i, q, pl.ds(HALO, HALO), :] = own[
+                pl.ds(i * per + (B - HALO) * nq + q, HALO, stride=nq), :
             ]
-        return carry
-
-    lax.fori_loop(0, Q, gather, 0)
+
+    def load(i, q, r):
+        return rim[i, q]
+
+    def store(i, q, r, cx, v):
+        moved[i, q, pl.ds(PAD + cx, SUB), :] = v
+
+    substep(load, store, ghosts, 0, parts, ch_count, k_count, 1)
+
+    def restricted(i, q, half):
+        return own[pl.ds(i * per + half * nq + q, SUB, stride=2 * nq), :]
+
+    lows = pack(restricted, ch_count, k_count, 0)
+    for n, plane in enumerate(lows):
+        low[n] = plane
+    for n, plane in enumerate(pack(restricted, ch_count, k_count, 1)):
+        high[n] = plane
+
+    for c, out, outer in ((1, to_right, B - 1), (-1, to_left, 0)):
+        first = PAD + (SUB - 1 if c > 0 else 0)
+        second = first - c
+        for i in range(Q):
+            out[pl.ds(i * nq, nq), :] = own[pl.ds(i * per + outer * nq, nq), :]
+        for q in range(nq):
+            out[pl.ds(FROM_DENSITY * nq + q, 1), :] = parts[6, q, pl.ds(second, 1), :]
+            for n, i in enumerate(along(c)):
+                out[pl.ds((FROM_ENTER + n) * nq + q, 1), :] = moved[i, q, pl.ds(first, 1), :]
+            total = None
+            for i in along(0) + along(c):
+                v = moved[i, q, pl.ds(second, 1), :]
+                total = v if total is None else total + v
+            out[pl.ds(FROM_PARTIAL * nq + q, 1), :] = total
+        for n in range(PLANES):
+            x = SUB - edge if c > 0 else 0
+            out[pl.ds(SENT * nq + n * edge, edge), :] = lows[n][x : x + edge]
+        spare = sent_rows(nq) - edge_rows(nq)
+        if spare:
+            out[pl.ds(edge_rows(nq), spare), :] = jnp.zeros((spare, LANES), jnp.float32)
+
+
+def inner_body(ch_count, k_count, own, ghosts, out, parts):
+    nq = ch_count * k_count
+
+    def load(i, q, r):
+        return own[pl.ds(i * (B * nq) + r * nq + q, SUB, stride=nq), :]
+
+    def store(i, q, r, cx, v):
+        out[i, q, pl.ds(PAD + r + cx, SUB), :] = v
+
+    substep(load, store, ghosts, HALO, parts, ch_count, k_count, B // SUB)
+
+
+def fine_body(
+    ch_count, k_count, own, left, right, inner, ghosts, rim_ghosts, out, rim, half, third, parts
+):
+    nq = ch_count * k_count
+    per = B * nq
+    row = lax.broadcasted_iota(jnp.int32, (SUB, LANES), 0)
+    origin = PAD + HALO
+
+    layers = Q * nq
+    rim[pl.ds(1, layers, stride=SUB), :] = left[pl.ds(0, layers), :]
+    rim[pl.ds(6, layers, stride=SUB), :] = right[pl.ds(0, layers), :]
+    for i in range(Q):
+        for sub, x in ((2, 0), (3, 1), (4, B - 2), (5, B - 1)):
+            rim[pl.ds(i * (nq * SUB) + sub, nq, stride=SUB), :] = own[
+                pl.ds(i * per + x * nq, nq), :
+            ]
+
+    def spread(ref, plane, q):
+        return jnp.broadcast_to(ref[pl.ds(plane * nq + q, 1), :], (SUB, LANES))
+
+    def load_rim(i, q, r):
+        return rim[pl.ds((i * nq + q) * SUB, SUB), :]
+
+    def rim_density(q, r, density):
+        density = jnp.where(row == 0, spread(left, FROM_DENSITY, q), density)
+        return jnp.where(row == SUB - 1, spread(right, FROM_DENSITY, q), density)
+
+    outgoing = {(c, q): None for c in (-1, 1) for q in range(nq)}
+
+    def store_rim(i, q, r, cx, v):
+        half[i, q, pl.ds(origin - 2 + cx, SUB), :] = v
+        half[i, q, pl.ds(origin + B - 6 + cx, SUB), :] = v
+        if cx:
+            seen = outgoing[cx, q]
+            outgoing[cx, q] = v if seen is None else seen + v
+
+    substep(load_rim, store_rim, rim_ghosts, 0, parts, ch_count, k_count, 1, rim_density)
+    for i in range(Q):
+        cx = VELOCITIES[i][0]
+        for q in range(nq):
+            half[i, q, pl.ds(origin + 1 + cx, B - 2), :] = inner[i, q, pl.ds(PAD + 1 + cx, B - 2), :]
+            if cx:
+                ref = left if cx > 0 else right
+                at = origin - 1 if cx > 0 else origin + B
+                place = FROM_ENTER + along(cx).index(i)
+                half[i, q, pl.ds(at, 1), :] = ref[pl.ds(place * nq + q, 1), :]
+
+    def load(i, q, r):
+        return half[i, q, pl.ds(PAD + r, SUB), :]
+
+    def store(i, q, r, cx, v):
+        third[i, q, pl.ds(PAD + r + cx, SUB), :] = v
+
     chunks = (B + 2 * HALO) // SUB
-    fine_step(first, 0, second, ghosts, parts, ch_count, k_count, chunks)
-    fine_step(second, PAD, third, ghosts, parts, ch_count, k_count, chunks)
+
+    def density_of(q, r, density):
+        if r == 0:
+            value = spread(left, FROM_PARTIAL, q) + pltpu.roll(outgoing[-1, q], 1, 0)
+            return jnp.where(row == HALO - 2, value, density)
+        if r == (chunks - 1) * SUB:
+            value = spread(right, FROM_PARTIAL, q) + pltpu.roll(outgoing[1, q], SUB - 1, 0)
+            return jnp.where(row == SUB - HALO + 1, value, density)
+        return density
+
+    substep(load, store, ghosts, 0, parts, ch_count, k_count, chunks, density_of)
 
     def scatter(i, carry):
         for q in range(nq):
-            out[pl.ds(i * (B * nq) + q, B, stride=nq), :] = third[i, q, pl.ds(PAD + HALO, B), :]
+            out[pl.ds(i * per + q, B, stride=nq), :] = third[i, q, pl.ds(origin, B), :]
         return carry
 
     lax.fori_loop(0, Q, scatter, 0)
 
 
-def fine_ghost_body(ch_count, rows, layers, spread, out, wide):
+def fine_ghost_body(ch_count, rows, layers, spread, out, send_ghosts, rim_ghosts, wide):
     for side in range(2):
         wide[...] = jnp.dot(
             layers[side],
@@ -294,6 +430,15 @@
                 for n, i in enumerate(wanted):
                     out[side, n, ch, pl.ds(r, SUB), :] = found[i]
                 out[side, NG - 1, ch, pl.ds(r, SUB), :] = potential
+            for n in range(NG):
+                for ref, lower, upper in (
+                    (send_ghosts, HALO, rows - 2 * HALO),
+                    (rim_ghosts, 2, rows - HALO - 2),
+                ):
+                    ref[side, n, ch, pl.ds(0, HALO), :] = out[side, n, ch, pl.ds(lower, HALO), :]
+                    ref[side, n, ch, pl.ds(HALO, HALO), :] = out[
+                        side, n, ch, pl.ds(upper, HALO), :
+                    ]
 
 
 GROUP = 16
@@ -322,17 +467,6 @@
     return planes
 
 
-def restrict_body(ch_count, k_count, own, low, high):
-    nq = ch_count * k_count
-
-    def load(i, q, half):
-        return own[pl.ds(i * (B * nq) + half * nq + q, SUB, stride=2 * nq), :]
-
-    for side, out in enumerate((low, high)):
-        for n, plane in enumerate(pack(load, ch_count, k_count, side)):
-            out[n] = plane
-
-
 def coarse_body(planes, state, out, packed, near, parts, out_pad):
     lane = lax.broadcasted_iota(jnp.int32, (SUB, LANES), 1)
 
@@ -361,8 +495,8 @@
         upper = [parts[n, x + 1] for n in range(3)]
         gy, gz, p, rho, mx, my, mz = (parts[n, x] for n in range(3, 10))
         pull = [upper[0] - lower[0], gy + (upper[1] + lower[1]), gz + (upper[2] + lower[2])]
-        u = velocity_of(rho, (mx, my, mz), p, pull, COARSE_TAU)
-        for i, balance in balances(rho, u, 1.0 / COARSE_TAU):
+        flux = flux_of((mx, my, mz), p, pull, COARSE_TAU)
+        for i, balance in balances(rho, flux, 1.0 / COARSE_TAU):
             cx, cy, cz = VELOCITIES[i]
             post = [state[i, x] * (1.0 - 1.0 / COARSE_TAU) + balance]
             if cy:
@@ -396,7 +530,7 @@
 
 def edges_body(
     ch_count, k_count, planes, left, right, low, high, high_left, high_right, packed, near, step,
-    out, halo, rows, columns, ghost,
+    out, rows, columns, ghost,
 ):
     nq = ch_count * k_count
     edge = HALO // 2
@@ -404,20 +538,14 @@
     lane = lax.broadcasted_iota(jnp.int32, (SUB, LANES), 1)
     sided = lane % 2 == 0
 
-    halo[...] = jnp.zeros_like(halo)
-
-    def load(i, q, half):
-        for at, ref in ((0, left), (edge, right)):
-            start = i * (HALO * nq) + half * nq + q
-            halo[i % 2, q, half, pl.ds(at, edge), :] = ref[pl.ds(start, edge, stride=2 * nq), :]
-        return halo[i % 2, q, half]
-
-    beside = pack(load, ch_count, k_count, 0)
     for n in range(PLANES):
         own_x = 2 * edge
         rows[n, pl.ds(2 + own_x, inner, stride=2), :] = low[n]
-        rows[n, pl.ds(2, edge, stride=2), :] = beside[n][:edge]
-        rows[n, pl.ds(2 + 2 * (edge + inner), edge, stride=2), :] = beside[n][edge : 2 * edge]
+        beside = SENT * nq + n * edge
+        rows[n, pl.ds(2, edge, stride=2), :] = left[pl.ds(beside, edge), :]
+        rows[n, pl.ds(2 + 2 * (edge + inner), edge, stride=2), :] = right[
+            pl.ds(beside, edge), :
+        ]
         rows[n, pl.ds(1 + own_x, inner, stride=2), :] = high[n]
         rows[n, pl.ds(1, edge, stride=2), :] = high_left[n, pl.ds(inner - edge, edge), :]
         rows[n, pl.ds(1 + 2 * (edge + inner), edge, stride=2), :] = high_right[
@@ -453,8 +581,8 @@
         gy + (shift_x(dy, -1) + shift_x(dy, 1)),
         gz + (shift_x(dz, -1) + shift_x(dz, 1)),
     ]
-    u = velocity_of(density, momentum, p, pull, COARSE_TAU)
-    for i, balance in balances(density, u, 1.0 / COARSE_TAU):
+    flux = flux_of(momentum, p, pull, COARSE_TAU)
+    for i, balance in balances(density, flux, 1.0 / COARSE_TAU):
         cx, cy, cz = VELOCITIES[i]
         v = packed[i] * (1.0 - 1.0 / COARSE_TAU) + balance
         if cy > 0:
@@ -531,9 +659,9 @@
     layers = layers.reshape(2, Q * fine_rows, cz)
     lane = jnp.arange(ch_count * LANES) // (2 * B)
     one_hot = (jnp.arange(cz)[:, None] == lane[None, :]).astype(jnp.float32)
-    fine_ghosts = call(
+    fine_ghosts, send_ghosts, rim_ghosts = call(
         functools.partial(fine_ghost_body, ch_count, fine_rows),
-        f32(2, NG, ch_count, fine_rows, LANES),
+        [f32(2, NG, ch_count, n, LANES) for n in (fine_rows, SUB, SUB)],
         [VMEM, VMEM],
         [pltpu.VMEM((Q * fine_rows, ch_count * LANES), jnp.float32)],
     )(layers, one_hot)
@@ -547,45 +675,53 @@
         ],
         flops=10**7,
     )(coarse)
-    arrived, fine_ghosts, coarse_step, packed, near = lax.optimization_barrier(
-        (arrived, fine_ghosts, coarse_step, packed, near)
-    )
+    hidden = (fine_ghosts, send_ghosts, rim_ghosts, coarse_step, packed, near)
+    arrived, hidden = lax.optimization_barrier((arrived, hidden))
+    fine_ghosts, send_ghosts, rim_ghosts, coarse_step, packed, near = hidden
     own = arrived.reshape(total, LANES)[: Q * tiles * k_count]
 
-    by_x = own.reshape(Q, B * nq, LANES)
-    width = HALO * nq
-    left = lax.ppermute(by_x[:, -width:], "grp", ring(n_grp, 1)).reshape(Q * width, LANES)
-    right = lax.ppermute(by_x[:, :width], "grp", ring(n_grp, -1)).reshape(Q * width, LANES)
-
-    low, first = call(
-        functools.partial(restrict_body, ch_count, k_count),
-        [f32(PLANES, SUB, LANES)] * 2,
-        [VMEM],
-    )(own)
+    padded = PAD + fine_rows + PAD
+    to_left, to_right, low, first = call(
+        functools.partial(send_body, ch_count, k_count),
+        [f32(sent_rows(nq), LANES)] * 2 + [f32(PLANES, SUB, LANES)] * 2,
+        [VMEM] * 2,
+        [
+            pltpu.VMEM((Q, nq, SUB, LANES), jnp.float32),
+            pltpu.VMEM((Q, nq, 3 * PAD, LANES), jnp.float32),
+            pltpu.VMEM((10, nq, 3 * PAD, LANES), jnp.float32),
+        ],
+    )(own, send_ghosts)
+    left = lax.ppermute(to_right, "grp", ring(n_grp, 1))
+    right = lax.ppermute(to_left, "grp", ring(n_grp, -1))
+    inner = call(
+        functools.partial(inner_body, ch_count, k_count),
+        f32(Q, nq, PAD + B + PAD, LANES),
+        [VMEM] * 2,
+        [pltpu.VMEM((10, nq, PAD + B + PAD, LANES), jnp.float32)],
+        flops=10**7,
+    )(own, fine_ghosts)
     highs = []
     for across in (0, 1, -1):
         highs.append(lax.ppermute(first, axes, slab_pairs(n_grp, n_wide, -1, across)))
 
-    padded = PAD + fine_rows + PAD
     fine = call(
         functools.partial(fine_body, ch_count, k_count),
         f32(Q * B * nq, LANES),
-        [VMEM] * 4,
+        [VMEM] * 6,
         [
-            pltpu.VMEM((Q, nq, fine_rows, LANES), jnp.float32),
+            pltpu.VMEM((Q * nq * SUB, LANES), jnp.float32),
             pltpu.VMEM((Q, nq, padded, LANES), jnp.float32),
             pltpu.VMEM((Q, nq, padded, LANES), jnp.float32),
             pltpu.VMEM((10, nq, padded, LANES), jnp.float32),
         ],
         flops=10**7,
-    )(own, left, right, fine_ghosts)
+    )(own, left, right, inner, fine_ghosts, rim_ghosts)
 
     coarse_out = call(
         functools.partial(edges_body, ch_count, k_count, planes),
         f32(Q, cx, cz, cy),
         [VMEM] * 9,
         [
-            pltpu.VMEM((2, nq, 2, SUB, LANES), jnp.float32),
             pltpu.VMEM((PLANES, LANES, LANES), jnp.float32),
             pltpu.VMEM((PLANES, LANES, LANES), jnp.float32),
             pltpu.VMEM((Q, SUB, LANES), jnp.float32),

time: 68.2 us -> 66.5 us (0.975)
  blocking collectives: 0 us -> 25.7 us
  waiting for transfers between devices: 29 us -> 9.24 us
  starting transfers between devices: 25.3 us -> 17.3 us
    all_to_all x0 -> x1, blocking collectives: none -> 25.7 us  [local(): spread = lax.all_to_all(pieces, axes, 0, 0, tiled=True)]
    all_to_all x1 -> x0, waiting for transfers between devices: 17.6 us -> none  [local(): spread = lax.all_to_all(pieces, axes, 0, 0, tiled=True)]
    all_to_all x1 -> x0, starting transfers between devices: 7.33 us -> none  [local(): spread = lax.all_to_all(pieces, axes, 0, 0, tiled=True)]
    pallas_call x2 -> x3, Pallas kernels: 1.37 us -> 3.18 us  [the longest x1 1.65 us: local(): call(functools.partial(send_body, ch_count, k_count), [f32(sent_rows(nq),...]
    ppermute x2, waiting for transfers between devices: 1.34 us -> 0.01 us  [the longest x1 0.01 us: local(): right = lax.ppermute(to_left, 'grp', ring(n_grp, -1))]
    pallas_call x1, Pallas kernels: 3.43 us -> 2.14 us  [local(): call(functools.partial(fine_body, ch_count, k_count), f32(Q * B * nq, LAN...]
  transfers between devices with their start and end apart: 12 -> 11, of which waited for: 4 -> 1; matrix products, arithmetic and copies ran while one was open for 3% -> 3% of each run, Pallas kernels for 13% -> 10%
where the time goes in v4:
time: 66.5 us; the launch traced here: 66.2 us
  blocking collectives  25.7 us (39%)
  starting transfers between devices  17.3 us (26%)
  Pallas kernels  11.1 us (17%)
  waiting for transfers between devices  9.24 us (14%)
  local copies, waits for them, and re-layouts  2.06 us (3%)
  between operations  0.8 us (1%)
    all_to_all x1, blocking collectives, local(): spread = lax.all_to_all(pieces, axes, 0, 0, tiled=True)  25.7 us
    ppermute x3, waiting for transfers between devices, local(): below.append(lax.ppermute(part, axes, slab_pairs(n_grp, n_wide, 1, across)))  9.22 us
    ppermute x3, starting transfers between devices, local(): lax.ppermute(first, axes, slab_pairs(n_grp, n_wide, -1, across))  4.92 us
    ppermute x3, starting transfers between devices, local(): below.append(lax.ppermute(part, axes, slab_pairs(n_grp, n_wide, 1, across)))  4.19 us
    pallas_call x1, Pallas kernels, local(): call(functools.partial(coarse_body, planes), [f32(Q, cx, cz, cy), f32(Q,...  2.81 us
    ppermute x1, starting transfers between devices, local(): coarse_right = lax.ppermute(coarse_pop[:, :edge], 'grp', ring(n_grp, -1))  2.62 us
    all_to_all x1, starting transfers between devices, local(): lax.all_to_all(outgoing.reshape(devices, rows, k_count, LANES), axes, 0,...  2.61 us
    ppermute x1, starting transfers between devices, local(): right = lax.ppermute(to_left, 'grp', ring(n_grp, -1))  2.21 us
  transfers between devices with their start and end apart: 11, of which 1 were waited for; matrix products, arithmetic and copies ran while one was open for 3% of the time, Pallas kernels for 10%

profile of v4, /device:TPU:0, one launch (start us, length us, event | category | flops | bytes accessed | tf_op | source)
XLA Modules:
  0.0 66.2 jit_solution(1603554301973286610)
XLA Ops:
  0.6 25.7 %all_to_all.10 = f32[32,19,2,128]{3,2,1,0:T(2,128)S(1)} all-to-all(f32[32,19,2,128]{3,2,1,0:T(2,128)} %bitcast.25), channel_id=1, replica_groups=mesh['grp'=4,'wide'=8] {'grp','wide'}, dimensions={0} | all-to-all | bytes 1245184 | tf_op jit(solution)/shard_map/all_to_all | solution.py:637
  26.3 1.6 %shard_map.50 = f32[1216,128]{1,0:T(8,128)} custom-call(s32[64]{0:T(128)S(1)} %copy-done, f32[1216,128]{1,0:T(8,128)S(1)} %bitcast.23), custom_call_target="tpu_custom_call" | custom-call | flops 1000000 | bytes 1245184 | tf_op jit(solution)/shard_map/pallas_call | solution.py:652
  27.9 2.6 %all-to-all-start.1 = ((f32[32,19,2,128]{3,2,1,0:T(2,128)}), f32[32,19,2,128]{3,2,1,0:T(2,128)S(1)}, u32[]{:S(2)}, u32[]{:S(2)}) async-start(f32[32,19,2,128]{3,2,1,0:T(2,128)} %bitcast.4), calls=%async_computation.1 | async-start | bytes 1245184 | tf_op jit(solution)/shard_map/all_to_all | solution.py:653
  30.6 2.6 %collective-permute-start.4 = (f32[19,2,8,128]{3,2,1,0:T(8,128)S(1)}, f32[19,2,8,128]{3,2,1,0:T(8,128)S(1)}, u32[]{:S(2)}, u32[]{:S(2)}) collective-permute-start(f32[19,2,8,128]{3,2,1,0:T(8,128)S(1)} %get-tuple-element.36), channel_id=1, source_target_pairs={{0,24},{8,0},{16,8},{24,16},{1,25},{9,1},{17,9},{25,17},{2,26},{10... | collective-permute-start | bytes 466952 | tf_op jit(solution)/shard_map/ppermute | solution.py:640
  33.2 0.0 collective-permute-start.3
  33.2 0.2 slice.18
  33.4 0.5 copy.11
  33.9 0.0 collective-permute-start.1
  34.0 3.2 %collective-permute-start = (f32[19,2,8]{0,2,1:T(8,128)S(1)}, f32[19,2,8]{0,2,1:T(8,128)S(1)}, u32[]{:S(2)}, u32[]{:S(2)}) collective-permute-start(f32[19,2,8]{0,2,1:T(8,128)S(1)} %get-tuple-element.38), channel_id=1, source_target_pairs={{0,9},{1,10},{2,11},{3,12},{4,13},{5,14},{6,15},{7,8},{8,17},{9,18... | collective-permute-start | bytes 3656 | tf_op jit(solution)/shard_map/ppermute | solution.py:644
  37.2 0.9 %collective-permute-start.2 = (f32[19,2,8]{0,2,1:T(8,128)S(1)}, f32[19,2,8]{0,2,1:T(8,128)S(1)}, u32[]{:S(2)}, u32[]{:S(2)}) collective-permute-start(f32[19,2,8]{0,2,1:T(8,128)S(1)} %get-tuple-element.39), channel_id=1, source_target_pairs={{0,25},{1,26},{2,27},{3,28},{4,29},{5,30},{6,31},{7,24},{8,1},{9,2... | collective-permute-start | bytes 3656 | tf_op jit(solution)/shard_map/ppermute | solution.py:644
  38.2 9.2 %collective-permute-done = f32[19,2,8]{0,2,1:T(8,128)S(1)} collective-permute-done((f32[19,2,8]{0,2,1:T(8,128)S(1)}, f32[19,2,8]{0,2,1:T(8,128)S(1)}, u32[]{:S(2)}, u32[]{:S(2)}) %collective-permute-start) | collective-permute-done | bytes 1248 | tf_op jit(solution)/shard_map/ppermute | solution.py:644
  47.4 0.0 collective-permute-done.2
  47.4 0.0 collective-permute-done.1
  47.4 0.0 collective-permute-done.3
  47.5 0.0 collective-permute-done.4
  47.5 0.7 %copy.8 = f32[19,12,8,1]{0,2,3,1:T(8,128)S(1)} copy(f32[19,12,8,1]{3,2,1,0:T(8,128)S(1)} %bitcast.22) | data formatting | bytes 14592 | tf_op jit(solution)/shard_map/slice | solution.py:658
  48.3 0.3 copy.9
  48.6 0.2 broadcast_in_dim.2
  48.7 1.0 %shard_map.51 = (f32[2,6,2,24,128]{4,3,2,1,0:T(8,128)S(1)}, f32[2,6,2,8,128]{4,3,2,1,0:T(8,128)S(1)}, f32[2,6,2,8,128]{4,3,2,1,0:T(8,128)S(1)}) custom-call(f32[2,456,8]{2,1,0:T(8,128)S(1)} %bitcast.24, f32[8,256]{1,0:T(8,128)S(1)} %fusion.spread), custom_call_target="tpu_custom_call" | custom-call | flops 1000000 | bytes 1000000 | tf_op jit(solution)/shard_map/pallas_call | solution.py:662
  49.8 2.8 %shard_map.52 = (f32[19,8,8,128]{3,2,1,0:T(8,128)S(1)}, f32[19,8,128]{2,1,0:T(8,128)S(1)}, f32[8,128]{1,0:T(8,128)S(1)}) custom-call(f32[19,12,8,128]{3,2,1,0:T(8,128)S(1)} %constant_dynamic-update-slice_fusion.state), custom_call_target="tpu_custom_call" | custom-call | flops 10000000 | bytes 1000000 | tf_op jit(solution)/shard_map/pallas_call | solution.py:668
  52.6 0.0 all-to-all-done.1
  52.6 1.7 %shard_map.53 = (f32[112,128]{1,0:T(8,128)S(1)}, f32[112,128]{1,0:T(8,128)S(1)}, f32[2,8,128]{2,1,0:T(8,128)S(1)}, f32[2,8,128]{2,1,0:T(8,128)S(1)}) custom-call(f32[1216,128]{1,0:T(8,128)S(1)} %bitcast.19, f32[2,6,2,8,128]{4,3,2,1,0:T(8,128)S(1)} %get-tuple-element.26.ghosts), custom_call_target="tpu_custom_call" | custom-call | flops 1000000 | bytes 1000000 | tf_op jit(solution)/shard_map/pallas_call | solution.py:684
  54.2 0.8 %collective-permute-start.5 = (f32[112,128]{1,0:T(8,128)S(1)}, f32[112,128]{1,0:T(8,128)S(1)}, u32[]{:S(2)}, u32[]{:S(2)}) collective-permute-start(f32[112,128]{1,0:T(8,128)S(1)} %get-tuple-element.27), channel_id=1, source_target_pairs={{0,8},{8,16},{16,24},{24,0},{1,9},{9,17},{17,25},{25,1},{2,10},{10... | collective-permute-start | bytes 172040 | tf_op jit(solution)/shard_map/ppermute | solution.py:694
  55.0 2.2 %collective-permute-start.6 = (f32[112,128]{1,0:T(8,128)S(1)}, f32[112,128]{1,0:T(8,128)S(1)}, u32[]{:S(2)}, u32[]{:S(2)}) collective-permute-start(f32[112,128]{1,0:T(8,128)S(1)} %get-tuple-element.28), channel_id=1, source_target_pairs={{0,24},{8,0},{16,8},{24,16},{1,25},{9,1},{17,9},{25,17},{2,26},{10... | collective-permute-start | bytes 172040 | tf_op jit(solution)/shard_map/ppermute | solution.py:695
  57.2 2.6 %collective-permute-start.9 = (f32[2,8,128]{2,1,0:T(8,128)S(1)}, f32[2,8,128]{2,1,0:T(8,128)S(1)}, u32[]{:S(2)}, u32[]{:S(2)}) collective-permute-start(f32[2,8,128]{2,1,0:T(8,128)S(1)} %get-tuple-element.32), channel_id=1, source_target_pairs={{0,31},{1,24},{2,25},{3,26},{4,27},{5,28},{6,29},{7,30},{8,7},{9,0... | collective-permute-start | bytes 24584 | tf_op jit(solution)/shard_map/ppermute | solution.py:705
  59.8 2.3 %collective-permute-start.8 = (f32[2,8,128]{2,1,0:T(8,128)S(1)}, f32[2,8,128]{2,1,0:T(8,128)S(1)}, u32[]{:S(2)}, u32[]{:S(2)}) collective-permute-start(f32[2,8,128]{2,1,0:T(8,128)S(1)} %get-tuple-element.32), channel_id=1, source_target_pairs={{0,15},{1,8},{2,9},{3,10},{4,11},{5,12},{6,13},{7,14},{8,23},{9,16... | collective-permute-start | bytes 24584 | tf_op jit(solution)/shard_map/ppermute | solution.py:705
  62.1 0.5 shard_map.54.inner
  62.7 0.0 collective-permute-done.6.right
  62.7 2.1 %shard_map.55 = f32[1216,128]{1,0:T(8,128)} custom-call(f32[1216,128]{1,0:T(8,128)S(1)} %bitcast.21, f32[112,128]{1,0:T(8,128)S(1)} %collective-permute-done.5.left, f32[112,128]{1,0:T(8,128)S(1)} %collective-permute-done.6.right, f32[19,4,32,128]{3,2,1,0:T(8,128)S(1)} %shard_map.54.inner, f32[2,6,2,24,128]{4,3,2,1,0:T(8,128)S(1)} %get-tuple-element.29.ghosts, ...), custom_call_target="tpu_custom_call" | custom-call | flops 10000000 | bytes 1000000 | tf_op jit(solution)/shard_map/pallas_call | solution.py:707
  64.8 0.0 collective-permute-done.8.high_left
  64.8 0.0 collective-permute-done.7.high
  64.8 1.4 %shard_map.56 = f32[19,8,8,128]{3,2,1,0:T(8,128)} custom-call(f32[112,128]{1,0:T(8,128)S(1)} %collective-permute-done.5.left, f32[112,128]{1,0:T(8,128)S(1)} %collective-permute-done.6.right, f32[2,8,128]{2,1,0:T(8,128)S(1)} %get-tuple-element.31.low, f32[2,8,128]{2,1,0:T(8,128)S(1)} %collective-permute-done.7.high, ...), custom_call_target="tpu_custom_call" | custom-call | flops 1000000 | bytes 1000000 | tf_op jit(solution)/shard_map/pallas_call | solution.py:720
  (16 shorter events, 0.1 us)
Async XLA Ops:
  0.6 25.7 %copy-start = (s32[64]{0:T(128)S(1)}, s32[64]{0:T(128)}, u32[]{:S(2)}) copy-start(s32[64]{0:T(128)} %slot_ref.1) | copy-start | bytes 772
  26.3 4.2 %copy-start.1 = (f32[19,8,8,128]{3,2,1,0:T(8,128)S(1)}, f32[19,8,8,128]{3,2,1,0:T(8,128)}, u32[]{:S(2)}) copy-start(f32[19,8,8,128]{3,2,1,0:T(8,128)} %param.4) | copy-start | bytes 1867780
  27.9 24.7 %all-to-all-start.1 = ((f32[32,19,2,128]{3,2,1,0:T(2,128)}), f32[32,19,2,128]{3,2,1,0:T(2,128)S(1)}, u32[]{:S(2)}, u32[]{:S(2)}) async-start(f32[32,19,2,128]{3,2,1,0:T(2,128)} %bitcast.4), calls=%async_computation.1 | async-start | bytes 1245184 | tf_op jit(solution)/shard_map/all_to_all | solution.py:653
  30.6 16.9 %collective-permute-start.4 = (f32[19,2,8,128]{3,2,1,0:T(8,128)S(1)}, f32[19,2,8,128]{3,2,1,0:T(8,128)S(1)}, u32[]{:S(2)}, u32[]{:S(2)}) collective-permute-start(f32[19,2,8,128]{3,2,1,0:T(8,128)S(1)} %get-tuple-element.36), channel_id=1, source_target_pairs={{0,24},{8,0},{16,8},{24,16},{1,25},{9,1},{17,9},{25,17},{2,26},{10... | collective-permute-start | bytes 466952 | tf_op jit(solution)/shard_map/ppermute | solution.py:640
  33.2 14.2 %collective-permute-start.3 = (f32[19,2,8,128]{3,2,1,0:T(8,128)S(1)}, f32[19,2,8,128]{3,2,1,0:T(8,128)S(1)}, u32[]{:S(2)}, u32[]{:S(2)}) collective-permute-start(f32[19,2,8,128]{3,2,1,0:T(8,128)S(1)} %get-tuple-element.37), channel_id=1, source_target_pairs={{0,8},{8,16},{16,24},{24,0},{1,9},{9,17},{17,25},{25,1},{2,10},{10... | collective-permute-start | bytes 466952 | tf_op jit(solution)/shard_map/ppermute | solution.py:639
  33.9 13.4 %collective-permute-start.1 = (f32[19,8,8]{0,2,1:T(8,128)S(1)}, f32[19,8,8]{0,2,1:T(8,128)S(1)}, u32[]{:S(2)}, u32[]{:S(2)}) collective-permute-start(f32[19,8,8]{0,2,1:T(8,128)S(1)} %bitcast.28), channel_id=1, source_target_pairs={{0,1},{1,2},{2,3},{3,4},{4,5},{5,6},{6,7},{7,0},{8,9},{9,10},{10,1... | collective-permute-start | bytes 14600 | tf_op jit(solution)/shard_map/ppermute | solution.py:644
  34.0 13.4 %collective-permute-start = (f32[19,2,8]{0,2,1:T(8,128)S(1)}, f32[19,2,8]{0,2,1:T(8,128)S(1)}, u32[]{:S(2)}, u32[]{:S(2)}) collective-permute-start(f32[19,2,8]{0,2,1:T(8,128)S(1)} %get-tuple-element.38), channel_id=1, source_target_pairs={{0,9},{1,10},{2,11},{3,12},{4,13},{5,14},{6,15},{7,8},{8,17},{9,18... | collective-permute-start | bytes 3656 | tf_op jit(solution)/shard_map/ppermute | solution.py:644
  37.2 10.2 %collective-permute-start.2 = (f32[19,2,8]{0,2,1:T(8,128)S(1)}, f32[19,2,8]{0,2,1:T(8,128)S(1)}, u32[]{:S(2)}, u32[]{:S(2)}) collective-permute-start(f32[19,2,8]{0,2,1:T(8,128)S(1)} %get-tuple-element.39), channel_id=1, source_target_pairs={{0,25},{1,26},{2,27},{3,28},{4,29},{5,30},{6,31},{7,24},{8,1},{9,2... | collective-permute-start | bytes 3656 | tf_op jit(solution)/shard_map/ppermute | solution.py:644
  54.2 8.4 %collective-permute-start.5 = (f32[112,128]{1,0:T(8,128)S(1)}, f32[112,128]{1,0:T(8,128)S(1)}, u32[]{:S(2)}, u32[]{:S(2)}) collective-permute-start(f32[112,128]{1,0:T(8,128)S(1)} %get-tuple-element.27), channel_id=1, source_target_pairs={{0,8},{8,16},{16,24},{24,0},{1,9},{9,17},{17,25},{25,1},{2,10},{10... | collective-permute-start | bytes 172040 | tf_op jit(solution)/shard_map/ppermute | solution.py:694
  55.0 7.7 %collective-permute-start.6 = (f32[112,128]{1,0:T(8,128)S(1)}, f32[112,128]{1,0:T(8,128)S(1)}, u32[]{:S(2)}, u32[]{:S(2)}) collective-permute-start(f32[112,128]{1,0:T(8,128)S(1)} %get-tuple-element.28), channel_id=1, source_target_pairs={{0,24},{8,0},{16,8},{24,16},{1,25},{9,1},{17,9},{25,17},{2,26},{10... | collective-permute-start | bytes 172040 | tf_op jit(solution)/shard_map/ppermute | solution.py:695
  57.2 7.6 %collective-permute-start.9 = (f32[2,8,128]{2,1,0:T(8,128)S(1)}, f32[2,8,128]{2,1,0:T(8,128)S(1)}, u32[]{:S(2)}, u32[]{:S(2)}) collective-permute-start(f32[2,8,128]{2,1,0:T(8,128)S(1)} %get-tuple-element.32), channel_id=1, source_target_pairs={{0,31},{1,24},{2,25},{3,26},{4,27},{5,28},{6,29},{7,30},{8,7},{9,0... | collective-permute-start | bytes 24584 | tf_op jit(solution)/shard_map/ppermute | solution.py:705
  59.8 5.0 %collective-permute-start.8 = (f32[2,8,128]{2,1,0:T(8,128)S(1)}, f32[2,8,128]{2,1,0:T(8,128)S(1)}, u32[]{:S(2)}, u32[]{:S(2)}) collective-permute-start(f32[2,8,128]{2,1,0:T(8,128)S(1)} %get-tuple-element.32), channel_id=1, source_target_pairs={{0,15},{1,8},{2,9},{3,10},{4,11},{5,12},{6,13},{7,14},{8,23},{9,16... | collective-permute-start | bytes 24584 | tf_op jit(solution)/shard_map/ppermute | solution.py:705
  62.1 2.7 %collective-permute-start.7 = (f32[2,8,128]{2,1,0:T(8,128)S(1)}, f32[2,8,128]{2,1,0:T(8,128)S(1)}, u32[]{:S(2)}, u32[]{:S(2)}) collective-permute-start(f32[2,8,128]{2,1,0:T(8,128)S(1)} %get-tuple-element.32), channel_id=1, source_target_pairs={{0,7},{1,0},{2,1},{3,2},{4,3},{5,4},{6,5},{7,6},{8,15},{9,8},{10,9... | collective-permute-start | bytes 24584 | tf_op jit(solution)/shard_map/ppermute | solution.py:705

commit v5 on v4

--- a/solution.py
+++ b/solution.py
@@ -15,6 +15,7 @@
 HALO = 4
 PAD = 8
 GRANT = 24 << 20
+PIECES = 8
 
 VELOCITIES = (
     (0, 0, 0),
@@ -51,14 +52,15 @@
 
 VMEM = pl.BlockSpec(memory_space=pltpu.VMEM)
 SMEM = pl.BlockSpec(memory_space=pltpu.SMEM)
-
-
-def call(body, outs, specs, scratch=(), flops=10**6, moved=10**6):
+HBM = pl.BlockSpec(memory_space=pl.ANY)
+
+
+def call(body, outs, specs, scratch=(), flops=10**6, moved=10**6, place=VMEM):
     return pl.pallas_call(
         body,
         out_shape=outs,
         in_specs=specs,
-        out_specs=jax.tree.map(lambda _: VMEM, outs),
+        out_specs=jax.tree.map(lambda _: place, outs),
         scratch_shapes=list(scratch),
         cost_estimate=pl.CostEstimate(flops=flops, bytes_accessed=moved, transcendentals=0),
         compiler_params=pltpu.CompilerParams(vmem_limit_bytes=GRANT),
@@ -147,13 +149,10 @@
     return [momentum[j] + force * pull[j] for j in range(3)]
 
 
-def regroup_body(blocks, k_blocks, rows, slot_ref, in_ref, out_ref):
+def regroup_body(blocks, k_blocks, rows, target_ref, in_ref, out_ref):
     for b in range(blocks):
-        s = slot_ref[b]
         source = (b // k_blocks) * (rows * k_blocks) + b % k_blocks
-        owner = lax.div(s, k_blocks)
-        target = owner * (rows * k_blocks) + (s - owner * k_blocks)
-        out_ref[pl.ds(target, rows, stride=k_blocks), :] = in_ref[
+        out_ref[pl.ds(target_ref[b], rows, stride=k_blocks), :] = in_ref[
             pl.ds(source, rows, stride=k_blocks), :
         ]
 
@@ -269,13 +268,27 @@
     return -(-edge_rows(nq) // SUB) * SUB
 
 
+def parts_of(count, pieces):
+    cuts = [count * n // pieces for n in range(pieces + 1)]
+    return list(zip(cuts[:-1], cuts[1:]))
+
+
 def along(c):
     return [i for i in range(Q) if VELOCITIES[i][0] == c]
 
 
-def send_body(
-    ch_count, k_count, own, ghosts, to_left, to_right, low, high, rim, moved, parts
-):
+def restrict_body(ch_count, k_count, own, low, high):
+    nq = ch_count * k_count
+
+    def restricted(i, q, half):
+        return own[pl.ds(i * (B * nq) + half * nq + q, SUB, stride=2 * nq), :]
+
+    for side, out in enumerate((low, high)):
+        for n, plane in enumerate(pack(restricted, ch_count, k_count, side)):
+            out[n] = plane
+
+
+def send_body(ch_count, k_count, own, ghosts, low, to_left, to_right, rim, moved, parts):
     nq = ch_count * k_count
     per = B * nq
     edge = HALO // 2
@@ -294,15 +307,6 @@
         moved[i, q, pl.ds(PAD + cx, SUB), :] = v
 
     substep(load, store, ghosts, 0, parts, ch_count, k_count, 1)
-
-    def restricted(i, q, half):
-        return own[pl.ds(i * per + half * nq + q, SUB, stride=2 * nq), :]
-
-    lows = pack(restricted, ch_count, k_count, 0)
-    for n, plane in enumerate(lows):
-        low[n] = plane
-    for n, plane in enumerate(pack(restricted, ch_count, k_count, 1)):
-        high[n] = plane
 
     for c, out, outer in ((1, to_right, B - 1), (-1, to_left, 0)):
         first = PAD + (SUB - 1 if c > 0 else 0)
@@ -320,7 +324,7 @@
             out[pl.ds(FROM_PARTIAL * nq + q, 1), :] = total
         for n in range(PLANES):
             x = SUB - edge if c > 0 else 0
-            out[pl.ds(SENT * nq + n * edge, edge), :] = lows[n][x : x + edge]
+            out[pl.ds(SENT * nq + n * edge, edge), :] = low[n, pl.ds(x, edge), :]
         spare = sent_rows(nq) - edge_rows(nq)
         if spare:
             out[pl.ds(edge_rows(nq), spare), :] = jnp.zeros((spare, LANES), jnp.float32)
@@ -339,7 +343,7 @@
 
 
 def fine_body(
-    ch_count, k_count, own, left, right, inner, ghosts, rim_ghosts, out, rim, half, third, parts
+    ch_count, k_count, own, left, right, inner, ghosts, rim_ghosts, out, rim, half, third, parts, held, sems
 ):
     nq = ch_count * k_count
     per = B * nq
@@ -404,12 +408,16 @@
 
     substep(load, store, ghosts, 0, parts, ch_count, k_count, chunks, density_of)
 
-    def scatter(i, carry):
-        for q in range(nq):
-            out[pl.ds(i * per + q, B, stride=nq), :] = third[i, q, pl.ds(origin, B), :]
-        return carry
-
-    lax.fori_loop(0, Q, scatter, 0)
+    copies = []
+    for n, (i0, i1) in enumerate(parts_of(Q, PIECES)):
+        for i in range(i0, i1):
+            for q in range(nq):
+                held[pl.ds(i * per + q, B, stride=nq), :] = third[i, q, pl.ds(origin, B), :]
+        part = pl.ds(i0 * per, (i1 - i0) * per)
+        copies.append(pltpu.make_async_copy(held.at[part], out.at[part], sems.at[n]))
+        copies[-1].start()
+    for copy in copies:
+        copy.wait()
 
 
 def fine_ghost_body(ch_count, rows, layers, spread, out, send_ghosts, rim_ghosts, wide):
@@ -530,7 +538,7 @@
 
 def edges_body(
     ch_count, k_count, planes, left, right, low, high, high_left, high_right, packed, near, step,
-    out, rows, columns, ghost,
+    out, rows, columns, ghost, held, sems,
 ):
     nq = ch_count * k_count
     edge = HALO // 2
@@ -551,7 +559,7 @@
         rows[n, pl.ds(1 + 2 * (edge + inner), edge, stride=2), :] = high_right[
             n, pl.ds(0, edge), :
         ]
-        columns[n] = rows[n].T
+        columns[n, :, pl.ds(0, STEP)] = rows[n, pl.ds(0, STEP), :].T
     per = LANES // STEP
     for i in range(Q):
         for ch in range(ch_count):
@@ -582,6 +590,7 @@
         gz + (shift_x(dz, -1) + shift_x(dz, 1)),
     ]
     flux = flux_of(momentum, p, pull, COARSE_TAU)
+    copies = []
     for i, balance in balances(density, flux, 1.0 / COARSE_TAU):
         cx, cy, cz = VELOCITIES[i]
         v = packed[i] * (1.0 - 1.0 / COARSE_TAU) + balance
@@ -598,7 +607,14 @@
             v = shift_z([v], cz)[0]
         for x in range(inner):
             column = pltpu.roll(v, LANES - (2 * (x + edge) + 2), 1)
-            out[i, x] = jnp.where(touched, column, step[i, x])
+            held[i, x] = jnp.where(touched, column, step[i, x])
+        for n, (i0, i1) in enumerate(parts_of(Q, PIECES)):
+            if i == i1 - 1:
+                part = pl.ds(i0, i1 - i0)
+                copies.append(pltpu.make_async_copy(held.at[part], out.at[part], sems.at[n]))
+                copies[-1].start()
+    for copy in copies:
+        copy.wait()
 
 
 def ring(count, step):
@@ -649,7 +665,8 @@
         [SMEM, VMEM],
         moved=8 * total * LANES,
     )
-    outgoing = regroup(new_slot, spread.reshape(total, LANES))
+    targets = rows * new_slot - (rows - 1) * (new_slot % k_count)
+    outgoing = regroup(targets, spread.reshape(total, LANES))
     arrived = lax.all_to_all(
         outgoing.reshape(devices, rows, k_count, LANES), axes, 0, 0, tiled=True
     )
@@ -681,16 +698,21 @@
     own = arrived.reshape(total, LANES)[: Q * tiles * k_count]
 
     padded = PAD + fine_rows + PAD
-    to_left, to_right, low, first = call(
+    low, first = call(
+        functools.partial(restrict_body, ch_count, k_count),
+        [f32(PLANES, SUB, LANES)] * 2,
+        [VMEM],
+    )(own)
+    to_left, to_right = call(
         functools.partial(send_body, ch_count, k_count),
-        [f32(sent_rows(nq), LANES)] * 2 + [f32(PLANES, SUB, LANES)] * 2,
-        [VMEM] * 2,
+        [f32(sent_rows(nq), LANES)] * 2,
+        [VMEM] * 3,
         [
             pltpu.VMEM((Q, nq, SUB, LANES), jnp.float32),
             pltpu.VMEM((Q, nq, 3 * PAD, LANES), jnp.float32),
             pltpu.VMEM((10, nq, 3 * PAD, LANES), jnp.float32),
         ],
-    )(own, send_ghosts)
+    )(own, send_ghosts, low)
     left = lax.ppermute(to_right, "grp", ring(n_grp, 1))
     right = lax.ppermute(to_left, "grp", ring(n_grp, -1))
     inner = call(
@@ -713,8 +735,11 @@
             pltpu.VMEM((Q, nq, padded, LANES), jnp.float32),
             pltpu.VMEM((Q, nq, padded, LANES), jnp.float32),
             pltpu.VMEM((10, nq, padded, LANES), jnp.float32),
+            pltpu.VMEM((Q * B * nq, LANES), jnp.float32),
+            pltpu.SemaphoreType.DMA((PIECES,)),
         ],
         flops=10**7,
+        place=HBM,
     )(own, left, right, inner, fine_ghosts, rim_ghosts)
 
     coarse_out = call(
@@ -725,7 +750,10 @@
             pltpu.VMEM((PLANES, LANES, LANES), jnp.float32),
             pltpu.VMEM((PLANES, LANES, LANES), jnp.float32),
             pltpu.VMEM((Q, SUB, LANES), jnp.float32),
+            pltpu.VMEM((Q, cx, cz, cy), jnp.float32),
+            pltpu.SemaphoreType.DMA((PIECES,)),
         ],
+        place=HBM,
     )(left, right, low, *highs, packed, near, coarse_step)
 
     fine_out = fine.reshape(Q, tiles, k_count, LANES).transpose(2, 0, 1, 3)

time: 66.5 us -> 65.5 us (0.985)
  blocking collectives: 25.7 us -> 0 us
  waiting for transfers between devices: 9.24 us -> 27.6 us
  starting transfers between devices: 17.3 us -> 24.7 us
  Pallas kernels: 11.1 us -> 10 us
    all_to_all x1 -> x0, blocking collectives: 25.7 us -> none  [local(): spread = lax.all_to_all(pieces, axes, 0, 0, tiled=True)]
    all_to_all x0 -> x1, waiting for transfers between devices: none -> 18.3 us  [local(): spread = lax.all_to_all(pieces, axes, 0, 0, tiled=True)]
    all_to_all x0 -> x1, starting transfers between devices: none -> 7.33 us  [local(): spread = lax.all_to_all(pieces, axes, 0, 0, tiled=True)]
    pallas_call x1, Pallas kernels: 1.65 us -> 0.54 us  [local(): call(functools.partial(send_body, ch_count, k_count), [f32(sent_rows(nq),...]
    pallas_call x1 -> x2, Pallas kernels: 1.57 us -> 1.83 us  [the longest x1 1.45 us: local(): outgoing = regroup(targets, spread.reshape(total, LANES))]
  transfers between devices with their start and end apart: 11 -> 12, of which waited for: 1 -> 2; matrix products, arithmetic and copies ran while one was open for 3% -> 3% of each run, Pallas kernels for 10% -> 10%
where the time goes in v5:
time: 65.5 us; the launch traced here: 65.2 us
  waiting for transfers between devices  27.6 us (42%)
  starting transfers between devices  24.7 us (38%)
  Pallas kernels  10 us (15%)
  local copies, waits for them, and re-layouts  2.06 us (3%)
  between operations  0.84 us (1%)
    all_to_all x1, waiting for transfers between devices, local(): spread = lax.all_to_all(pieces, axes, 0, 0, tiled=True)  18.3 us
    ppermute x3, waiting for transfers between devices, local(): below.append(lax.ppermute(part, axes, slab_pairs(n_grp, n_wide, 1, across)))  9.22 us
    all_to_all x1, starting transfers between devices, local(): spread = lax.all_to_all(pieces, axes, 0, 0, tiled=True)  7.33 us
    ppermute x3, starting transfers between devices, local(): lax.ppermute(first, axes, slab_pairs(n_grp, n_wide, -1, across))  4.94 us
    ppermute x3, starting transfers between devices, local(): below.append(lax.ppermute(part, axes, slab_pairs(n_grp, n_wide, 1, across)))  4.19 us
    pallas_call x1, Pallas kernels, local(): call(functools.partial(coarse_body, planes), [f32(Q, cx, cz, cy), f32(Q,...  2.81 us
    ppermute x1, starting transfers between devices, local(): coarse_right = lax.ppermute(coarse_pop[:, :edge], 'grp', ring(n_grp, -1))  2.62 us
    all_to_all x1, starting transfers between devices, local(): lax.all_to_all(outgoing.reshape(devices, rows, k_count, LANES), axes, 0,...  2.61 us
  transfers between devices with their start and end apart: 12, of which 2 were waited for; matrix products, arithmetic and copies ran while one was open for 3% of the time, Pallas kernels for 10%

profile of v5, /device:TPU:0, one launch (start us, length us, event | category | flops | bytes accessed | tf_op | source)
XLA Modules:
  0.0 65.2 jit_solution(5881267842193730014)
XLA Ops:
  0.6 7.3 %all-to-all-start = ((f32[32,19,2,128]{3,2,1,0:T(2,128)}), f32[32,19,2,128]{3,2,1,0:T(2,128)S(1)}, u32[]{:S(2)}, u32[]{:S(2)}) async-start(f32[32,19,2,128]{3,2,1,0:T(2,128)} %bitcast.26), calls=%async_computation | async-start | bytes 1245184 | tf_op jit(solution)/shard_map/all_to_all | solution.py:653
  8.0 18.3 %all-to-all-done = f32[32,19,2,128]{3,2,1,0:T(2,128)S(1)} async-done(((f32[32,19,2,128]{3,2,1,0:T(2,128)}), f32[32,19,2,128]{3,2,1,0:T(2,128)S(1)}, u32[]{:S(2)}, u32[]{:S(2)}) %all-to-all-start) | async-done | bytes 622624 | tf_op jit(solution)/shard_map/all_to_all | solution.py:653
  26.3 1.5 %shard_map.50 = f32[1216,128]{1,0:T(8,128)} custom-call(s32[64]{0:T(128)S(1)} %fusion.2.target_ref, f32[1216,128]{1,0:T(8,128)S(1)} %bitcast.24), custom_call_target="tpu_custom_call" | custom-call | flops 1000000 | bytes 1245184 | tf_op jit(solution)/shard_map/pallas_call | solution.py:669
  27.8 2.6 %all-to-all-start.1 = ((f32[32,19,2,128]{3,2,1,0:T(2,128)}), f32[32,19,2,128]{3,2,1,0:T(2,128)S(1)}, u32[]{:S(2)}, u32[]{:S(2)}) async-start(f32[32,19,2,128]{3,2,1,0:T(2,128)} %bitcast.4), calls=%async_computation.1 | async-start | bytes 1245184 | tf_op jit(solution)/shard_map/all_to_all | solution.py:670
  30.4 2.6 %collective-permute-start.4 = (f32[19,2,8,128]{3,2,1,0:T(8,128)S(1)}, f32[19,2,8,128]{3,2,1,0:T(8,128)S(1)}, u32[]{:S(2)}, u32[]{:S(2)}) collective-permute-start(f32[19,2,8,128]{3,2,1,0:T(8,128)S(1)} %get-tuple-element.36), channel_id=1, source_target_pairs={{0,24},{8,0},{16,8},{24,16},{1,25},{9,1},{17,9},{25,17},{2,26},{10... | collective-permute-start | bytes 466952 | tf_op jit(solution)/shard_map/ppermute | solution.py:656
  33.1 0.0 collective-permute-start.3
  33.1 0.2 slice.18
  33.3 0.5 copy.11
  33.8 0.0 collective-permute-start.1
  33.9 3.2 %collective-permute-start = (f32[19,2,8]{0,2,1:T(8,128)S(1)}, f32[19,2,8]{0,2,1:T(8,128)S(1)}, u32[]{:S(2)}, u32[]{:S(2)}) collective-permute-start(f32[19,2,8]{0,2,1:T(8,128)S(1)} %get-tuple-element.38), channel_id=1, source_target_pairs={{0,9},{1,10},{2,11},{3,12},{4,13},{5,14},{6,15},{7,8},{8,17},{9,18... | collective-permute-start | bytes 3656 | tf_op jit(solution)/shard_map/ppermute | solution.py:660
  37.1 0.9 %collective-permute-start.2 = (f32[19,2,8]{0,2,1:T(8,128)S(1)}, f32[19,2,8]{0,2,1:T(8,128)S(1)}, u32[]{:S(2)}, u32[]{:S(2)}) collective-permute-start(f32[19,2,8]{0,2,1:T(8,128)S(1)} %get-tuple-element.39), channel_id=1, source_target_pairs={{0,25},{1,26},{2,27},{3,28},{4,29},{5,30},{6,31},{7,24},{8,1},{9,2... | collective-permute-start | bytes 3656 | tf_op jit(solution)/shard_map/ppermute | solution.py:660
  38.0 9.2 %collective-permute-done = f32[19,2,8]{0,2,1:T(8,128)S(1)} collective-permute-done((f32[19,2,8]{0,2,1:T(8,128)S(1)}, f32[19,2,8]{0,2,1:T(8,128)S(1)}, u32[]{:S(2)}, u32[]{:S(2)}) %collective-permute-start) | collective-permute-done | bytes 1248 | tf_op jit(solution)/shard_map/ppermute | solution.py:660
  47.2 0.0 collective-permute-done.2
  47.3 0.0 collective-permute-done.1
  47.4 0.7 %copy.8 = f32[19,12,8,1]{0,2,3,1:T(8,128)S(1)} copy(f32[19,12,8,1]{3,2,1,0:T(8,128)S(1)} %bitcast.23) | data formatting | bytes 14592 | tf_op jit(solution)/shard_map/slice | solution.py:675
  48.1 0.3 copy.9
  48.4 0.2 broadcast_in_dim.2
  48.6 1.0 %shard_map.51 = (f32[2,6,2,24,128]{4,3,2,1,0:T(8,128)S(1)}, f32[2,6,2,8,128]{4,3,2,1,0:T(8,128)S(1)}, f32[2,6,2,8,128]{4,3,2,1,0:T(8,128)S(1)}) custom-call(f32[2,456,8]{2,1,0:T(8,128)S(1)} %bitcast.25, f32[8,256]{1,0:T(8,128)S(1)} %fusion.spread), custom_call_target="tpu_custom_call" | custom-call | flops 1000000 | bytes 1000000 | tf_op jit(solution)/shard_map/pallas_call | solution.py:679
  49.6 2.8 %shard_map.52 = (f32[19,8,8,128]{3,2,1,0:T(8,128)S(1)}, f32[19,8,128]{2,1,0:T(8,128)S(1)}, f32[8,128]{1,0:T(8,128)S(1)}) custom-call(f32[19,12,8,128]{3,2,1,0:T(8,128)S(1)} %constant_dynamic-update-slice_fusion.state), custom_call_target="tpu_custom_call" | custom-call | flops 10000000 | bytes 1000000 | tf_op jit(solution)/shard_map/pallas_call | solution.py:685
  52.4 0.0 all-to-all-done.1
  52.4 0.4 shard_map.53
  52.8 0.5 shard_map.54
  53.4 0.8 %collective-permute-start.5 = (f32[112,128]{1,0:T(8,128)S(1)}, f32[112,128]{1,0:T(8,128)S(1)}, u32[]{:S(2)}, u32[]{:S(2)}) collective-permute-start(f32[112,128]{1,0:T(8,128)S(1)} %get-tuple-element.28), channel_id=1, source_target_pairs={{0,8},{8,16},{16,24},{24,0},{1,9},{9,17},{17,25},{25,1},{2,10},{10... | collective-permute-start | bytes 172040 | tf_op jit(solution)/shard_map/ppermute | solution.py:716
  54.1 2.2 %collective-permute-start.6 = (f32[112,128]{1,0:T(8,128)S(1)}, f32[112,128]{1,0:T(8,128)S(1)}, u32[]{:S(2)}, u32[]{:S(2)}) collective-permute-start(f32[112,128]{1,0:T(8,128)S(1)} %get-tuple-element.29), channel_id=1, source_target_pairs={{0,24},{8,0},{16,8},{24,16},{1,25},{9,1},{17,9},{25,17},{2,26},{10... | collective-permute-start | bytes 172040 | tf_op jit(solution)/shard_map/ppermute | solution.py:717
  56.3 2.6 %collective-permute-start.9 = (f32[2,8,128]{2,1,0:T(8,128)S(1)}, f32[2,8,128]{2,1,0:T(8,128)S(1)}, u32[]{:S(2)}, u32[]{:S(2)}) collective-permute-start(f32[2,8,128]{2,1,0:T(8,128)S(1)} %get-tuple-element.32), channel_id=1, source_target_pairs={{0,31},{1,24},{2,25},{3,26},{4,27},{5,28},{6,29},{7,30},{8,7},{9,0... | collective-permute-start | bytes 24584 | tf_op jit(solution)/shard_map/ppermute | solution.py:727
  58.9 2.3 %collective-permute-start.8 = (f32[2,8,128]{2,1,0:T(8,128)S(1)}, f32[2,8,128]{2,1,0:T(8,128)S(1)}, u32[]{:S(2)}, u32[]{:S(2)}) collective-permute-start(f32[2,8,128]{2,1,0:T(8,128)S(1)} %get-tuple-element.32), channel_id=1, source_target_pairs={{0,15},{1,8},{2,9},{3,10},{4,11},{5,12},{6,13},{7,14},{8,23},{9,16... | collective-permute-start | bytes 24584 | tf_op jit(solution)/shard_map/ppermute | solution.py:727
  61.3 0.0 collective-permute-start.7
  61.3 0.5 shard_map.55.inner
  61.8 0.0 collective-permute-done.6.right
  61.8 2.0 %shard_map.56 = f32[1216,128]{1,0:T(8,128)} custom-call(f32[1216,128]{1,0:T(8,128)S(1)} %bitcast.22, f32[112,128]{1,0:T(8,128)S(1)} %collective-permute-done.5.left, f32[112,128]{1,0:T(8,128)S(1)} %collective-permute-done.6.right, f32[19,4,32,128]{3,2,1,0:T(8,128)S(1)} %shard_map.55.inner, f32[2,6,2,24,128]{4,3,2,1,0:T(8,128)S(1)} %get-tuple-element.30.ghosts, ...), custom_call_target="tpu_custom_call" | custom-call | flops 10000000 | bytes 1000000 | tf_op jit(solution)/shard_map/pallas_call | solution.py:729
  63.8 0.0 collective-permute-done.9.high_right
  63.9 1.3 %shard_map.57 = f32[19,8,8,128]{3,2,1,0:T(8,128)} custom-call(f32[112,128]{1,0:T(8,128)S(1)} %collective-permute-done.5.left, f32[112,128]{1,0:T(8,128)S(1)} %collective-permute-done.6.right, f32[2,8,128]{2,1,0:T(8,128)S(1)} %get-tuple-element.27.low, f32[2,8,128]{2,1,0:T(8,128)S(1)} %collective-permute-done.7.high, ...), custom_call_target="tpu_custom_call" | custom-call | flops 1000000 | bytes 1000000 | tf_op jit(solution)/shard_map/pallas_call | solution.py:745
  (19 shorter events, 0.2 us)
Async XLA Ops:
  0.6 7.4 %copy-start.1 = (s32[64]{0:T(128)S(1)}, s32[64]{0:T(128)}, u32[]{:S(2)}) copy-start(s32[64]{0:T(128)} %param.5) | copy-start | bytes 772
  0.6 25.7 %all-to-all-start = ((f32[32,19,2,128]{3,2,1,0:T(2,128)}), f32[32,19,2,128]{3,2,1,0:T(2,128)S(1)}, u32[]{:S(2)}, u32[]{:S(2)}) async-start(f32[32,19,2,128]{3,2,1,0:T(2,128)} %bitcast.26), calls=%async_computation | async-start | bytes 1245184 | tf_op jit(solution)/shard_map/all_to_all | solution.py:653
  26.3 4.1 %copy-start = (f32[19,8,8,128]{3,2,1,0:T(8,128)S(1)}, f32[19,8,8,128]{3,2,1,0:T(8,128)}, u32[]{:S(2)}) copy-start(f32[19,8,8,128]{3,2,1,0:T(8,128)} %param.4) | copy-start | bytes 1867780
  27.8 24.7 %all-to-all-start.1 = ((f32[32,19,2,128]{3,2,1,0:T(2,128)}), f32[32,19,2,128]{3,2,1,0:T(2,128)S(1)}, u32[]{:S(2)}, u32[]{:S(2)}) async-start(f32[32,19,2,128]{3,2,1,0:T(2,128)} %bitcast.4), calls=%async_computation.1 | async-start | bytes 1245184 | tf_op jit(solution)/shard_map/all_to_all | solution.py:670
  30.4 16.9 %collective-permute-start.4 = (f32[19,2,8,128]{3,2,1,0:T(8,128)S(1)}, f32[19,2,8,128]{3,2,1,0:T(8,128)S(1)}, u32[]{:S(2)}, u32[]{:S(2)}) collective-permute-start(f32[19,2,8,128]{3,2,1,0:T(8,128)S(1)} %get-tuple-element.36), channel_id=1, source_target_pairs={{0,24},{8,0},{16,8},{24,16},{1,25},{9,1},{17,9},{25,17},{2,26},{10... | collective-permute-start | bytes 466952 | tf_op jit(solution)/shard_map/ppermute | solution.py:656
  33.1 14.2 %collective-permute-start.3 = (f32[19,2,8,128]{3,2,1,0:T(8,128)S(1)}, f32[19,2,8,128]{3,2,1,0:T(8,128)S(1)}, u32[]{:S(2)}, u32[]{:S(2)}) collective-permute-start(f32[19,2,8,128]{3,2,1,0:T(8,128)S(1)} %get-tuple-element.37), channel_id=1, source_target_pairs={{0,8},{8,16},{16,24},{24,0},{1,9},{9,17},{17,25},{25,1},{2,10},{10... | collective-permute-start | bytes 466952 | tf_op jit(solution)/shard_map/ppermute | solution.py:655
  33.8 13.4 %collective-permute-start.1 = (f32[19,8,8]{0,2,1:T(8,128)S(1)}, f32[19,8,8]{0,2,1:T(8,128)S(1)}, u32[]{:S(2)}, u32[]{:S(2)}) collective-permute-start(f32[19,8,8]{0,2,1:T(8,128)S(1)} %bitcast.29), channel_id=1, source_target_pairs={{0,1},{1,2},{2,3},{3,4},{4,5},{5,6},{6,7},{7,0},{8,9},{9,10},{10,1... | collective-permute-start | bytes 14600 | tf_op jit(solution)/shard_map/ppermute | solution.py:660
  33.9 13.4 %collective-permute-start = (f32[19,2,8]{0,2,1:T(8,128)S(1)}, f32[19,2,8]{0,2,1:T(8,128)S(1)}, u32[]{:S(2)}, u32[]{:S(2)}) collective-permute-start(f32[19,2,8]{0,2,1:T(8,128)S(1)} %get-tuple-element.38), channel_id=1, source_target_pairs={{0,9},{1,10},{2,11},{3,12},{4,13},{5,14},{6,15},{7,8},{8,17},{9,18... | collective-permute-start | bytes 3656 | tf_op jit(solution)/shard_map/ppermute | solution.py:660
  37.1 10.2 %collective-permute-start.2 = (f32[19,2,8]{0,2,1:T(8,128)S(1)}, f32[19,2,8]{0,2,1:T(8,128)S(1)}, u32[]{:S(2)}, u32[]{:S(2)}) collective-permute-start(f32[19,2,8]{0,2,1:T(8,128)S(1)} %get-tuple-element.39), channel_id=1, source_target_pairs={{0,25},{1,26},{2,27},{3,28},{4,29},{5,30},{6,31},{7,24},{8,1},{9,2... | collective-permute-start | bytes 3656 | tf_op jit(solution)/shard_map/ppermute | solution.py:660
  53.4 8.4 %collective-permute-start.5 = (f32[112,128]{1,0:T(8,128)S(1)}, f32[112,128]{1,0:T(8,128)S(1)}, u32[]{:S(2)}, u32[]{:S(2)}) collective-permute-start(f32[112,128]{1,0:T(8,128)S(1)} %get-tuple-element.28), channel_id=1, source_target_pairs={{0,8},{8,16},{16,24},{24,0},{1,9},{9,17},{17,25},{25,1},{2,10},{10... | collective-permute-start | bytes 172040 | tf_op jit(solution)/shard_map/ppermute | solution.py:716
  54.1 7.7 %collective-permute-start.6 = (f32[112,128]{1,0:T(8,128)S(1)}, f32[112,128]{1,0:T(8,128)S(1)}, u32[]{:S(2)}, u32[]{:S(2)}) collective-permute-start(f32[112,128]{1,0:T(8,128)S(1)} %get-tuple-element.29), channel_id=1, source_target_pairs={{0,24},{8,0},{16,8},{24,16},{1,25},{9,1},{17,9},{25,17},{2,26},{10... | collective-permute-start | bytes 172040 | tf_op jit(solution)/shard_map/ppermute | solution.py:717
  56.3 7.5 %collective-permute-start.9 = (f32[2,8,128]{2,1,0:T(8,128)S(1)}, f32[2,8,128]{2,1,0:T(8,128)S(1)}, u32[]{:S(2)}, u32[]{:S(2)}) collective-permute-start(f32[2,8,128]{2,1,0:T(8,128)S(1)} %get-tuple-element.32), channel_id=1, source_target_pairs={{0,31},{1,24},{2,25},{3,26},{4,27},{5,28},{6,29},{7,30},{8,7},{9,0... | collective-permute-start | bytes 24584 | tf_op jit(solution)/shard_map/ppermute | solution.py:727
  58.9 4.9 %collective-permute-start.8 = (f32[2,8,128]{2,1,0:T(8,128)S(1)}, f32[2,8,128]{2,1,0:T(8,128)S(1)}, u32[]{:S(2)}, u32[]{:S(2)}) collective-permute-start(f32[2,8,128]{2,1,0:T(8,128)S(1)} %get-tuple-element.32), channel_id=1, source_target_pairs={{0,15},{1,8},{2,9},{3,10},{4,11},{5,12},{6,13},{7,14},{8,23},{9,16... | collective-permute-start | bytes 24584 | tf_op jit(solution)/shard_map/ppermute | solution.py:727
  61.3 2.6 %collective-permute-start.7 = (f32[2,8,128]{2,1,0:T(8,128)S(1)}, f32[2,8,128]{2,1,0:T(8,128)S(1)}, u32[]{:S(2)}, u32[]{:S(2)}) collective-permute-start(f32[2,8,128]{2,1,0:T(8,128)S(1)} %get-tuple-element.32), channel_id=1, source_target_pairs={{0,7},{1,0},{2,1},{3,2},{4,3},{5,4},{6,5},{7,6},{8,15},{9,8},{10,9... | collective-permute-start | bytes 24584 | tf_op jit(solution)/shard_map/ppermute | solution.py:727

commit v6 on v5

--- a/solution.py
+++ b/solution.py
@@ -261,7 +261,7 @@
 
 
 def edge_rows(nq):
-    return SENT * nq + PLANES * (HALO // 2)
+    return SENT * nq + 2 * PLANES * (HALO // 2)
 
 
 def sent_rows(nq):
@@ -288,7 +288,11 @@
             out[n] = plane
 
 
-def send_body(ch_count, k_count, own, ghosts, low, to_left, to_right, rim, moved, parts):
+def right_turn():
+    return lax.axis_index("grp") % 2
+
+
+def send_body(ch_count, k_count, own, ghosts, low, high, turn_0, turn_1, rim, moved, parts, sides):
     nq = ch_count * k_count
     per = B * nq
     edge = HALO // 2
@@ -308,7 +312,8 @@
 
     substep(load, store, ghosts, 0, parts, ch_count, k_count, 1)
 
-    for c, out, outer in ((1, to_right, B - 1), (-1, to_left, 0)):
+    right = right_turn()
+    for c, out, outer in ((1, sides.at[right], B - 1), (-1, sides.at[1 - right], 0)):
         first = PAD + (SUB - 1 if c > 0 else 0)
         second = first - c
         for i in range(Q):
@@ -322,12 +327,16 @@
                 v = moved[i, q, pl.ds(second, 1), :]
                 total = v if total is None else total + v
             out[pl.ds(FROM_PARTIAL * nq + q, 1), :] = total
-        for n in range(PLANES):
-            x = SUB - edge if c > 0 else 0
-            out[pl.ds(SENT * nq + n * edge, edge), :] = low[n, pl.ds(x, edge), :]
+        x = SUB - edge if c > 0 else 0
+        for place, ref in enumerate((low, high)):
+            for n in range(PLANES):
+                at = SENT * nq + (place * PLANES + n) * edge
+                out[pl.ds(at, edge), :] = ref[n, pl.ds(x, edge), :]
         spare = sent_rows(nq) - edge_rows(nq)
         if spare:
             out[pl.ds(edge_rows(nq), spare), :] = jnp.zeros((spare, LANES), jnp.float32)
+    turn_0[...] = sides[0]
+    turn_1[...] = sides[1]
 
 
 def inner_body(ch_count, k_count, own, ghosts, out, parts):
@@ -343,12 +352,16 @@
 
 
 def fine_body(
-    ch_count, k_count, own, left, right, inner, ghosts, rim_ghosts, out, rim, half, third, parts, held, sems
+    ch_count, k_count, own, turn_0, turn_1, inner, ghosts, rim_ghosts,
+    out, rim, half, third, parts, held, sems, sides,
 ):
     nq = ch_count * k_count
     per = B * nq
     row = lax.broadcasted_iota(jnp.int32, (SUB, LANES), 0)
     origin = PAD + HALO
+    sides[0] = turn_0[...]
+    sides[1] = turn_1[...]
+    left, right = sides.at[1 - right_turn()], sides.at[right_turn()]
 
     layers = Q * nq
     rim[pl.ds(1, layers, stride=SUB), :] = left[pl.ds(0, layers), :]
@@ -537,28 +550,33 @@
 
 
 def edges_body(
-    ch_count, k_count, planes, left, right, low, high, high_left, high_right, packed, near, step,
-    out, rows, columns, ghost, held, sems,
+    ch_count, k_count, planes, turn_0, turn_1, low, high, packed, near, step,
+    out, rows, columns, ghost, held, sems, sides,
 ):
     nq = ch_count * k_count
     edge = HALO // 2
     inner = planes - HALO
     lane = lax.broadcasted_iota(jnp.int32, (SUB, LANES), 1)
     sided = lane % 2 == 0
+    tail = pl.ds(SENT * nq, PLANES * edge)
+    sides[0] = turn_0[tail, :]
+    sides[1] = turn_1[tail, :]
+    left, right = sides.at[1 - right_turn()], sides.at[right_turn()]
 
     for n in range(PLANES):
         own_x = 2 * edge
         rows[n, pl.ds(2 + own_x, inner, stride=2), :] = low[n]
-        beside = SENT * nq + n * edge
+        beside = n * edge
         rows[n, pl.ds(2, edge, stride=2), :] = left[pl.ds(beside, edge), :]
         rows[n, pl.ds(2 + 2 * (edge + inner), edge, stride=2), :] = right[
             pl.ds(beside, edge), :
         ]
-        rows[n, pl.ds(1 + own_x, inner, stride=2), :] = high[n]
-        rows[n, pl.ds(1, edge, stride=2), :] = high_left[n, pl.ds(inner - edge, edge), :]
-        rows[n, pl.ds(1 + 2 * (edge + inner), edge, stride=2), :] = high_right[
-            n, pl.ds(0, edge), :
-        ]
+        rows[n, pl.ds(1 + own_x, inner, stride=2), :] = high[pl.ds(n * SUB, inner), :]
+        turn = right_turn()
+        for at, place in ((1, 1 - turn), (1 + 2 * (edge + inner), turn)):
+            rows[n, pl.ds(at, edge, stride=2), :] = high[
+                pl.ds(PLANES * SUB + (place * PLANES + n) * edge, edge), :
+            ]
         columns[n, :, pl.ds(0, STEP)] = rows[n, pl.ds(0, STEP), :].T
     per = LANES // STEP
     for i in range(Q):
@@ -703,18 +721,22 @@
         [f32(PLANES, SUB, LANES)] * 2,
         [VMEM],
     )(own)
-    to_left, to_right = call(
+    turns = call(
         functools.partial(send_body, ch_count, k_count),
         [f32(sent_rows(nq), LANES)] * 2,
-        [VMEM] * 3,
+        [VMEM] * 4,
         [
             pltpu.VMEM((Q, nq, SUB, LANES), jnp.float32),
             pltpu.VMEM((Q, nq, 3 * PAD, LANES), jnp.float32),
             pltpu.VMEM((10, nq, 3 * PAD, LANES), jnp.float32),
+            pltpu.VMEM((2, sent_rows(nq), LANES), jnp.float32),
         ],
-    )(own, send_ghosts, low)
-    left = lax.ppermute(to_right, "grp", ring(n_grp, 1))
-    right = lax.ppermute(to_left, "grp", ring(n_grp, -1))
+    )(own, send_ghosts, low, first)
+    assert n_grp % 2 == 0
+    swaps = []
+    for turn, values in enumerate(turns):
+        ends = [((g + turn) % n_grp, (g + turn + 1) % n_grp) for g in range(0, n_grp, 2)]
+        swaps.append(lax.ppermute(values, "grp", ends + [(j, i) for i, j in ends]))
     inner = call(
         functools.partial(inner_body, ch_count, k_count),
         f32(Q, nq, PAD + B + PAD, LANES),
@@ -722,9 +744,12 @@
         [pltpu.VMEM((10, nq, PAD + B + PAD, LANES), jnp.float32)],
         flops=10**7,
     )(own, fine_ghosts)
-    highs = []
-    for across in (0, 1, -1):
-        highs.append(lax.ppermute(first, axes, slab_pairs(n_grp, n_wide, -1, across)))
+    tail = edge_rows(nq) - PLANES * edge
+    widened = jnp.concatenate(
+        [first.reshape(PLANES * SUB, LANES)]
+        + [swap[tail : tail + PLANES * edge] for swap in swaps]
+    )
+    high = lax.ppermute(widened, "wide", ring(n_wide, -1))
 
     fine = call(
         functools.partial(fine_body, ch_count, k_count),
@@ -737,24 +762,26 @@
             pltpu.VMEM((10, nq, padded, LANES), jnp.float32),
             pltpu.VMEM((Q * B * nq, LANES), jnp.float32),
             pltpu.SemaphoreType.DMA((PIECES,)),
+            pltpu.VMEM((2, sent_rows(nq), LANES), jnp.float32),
         ],
         flops=10**7,
         place=HBM,
-    )(own, left, right, inner, fine_ghosts, rim_ghosts)
+    )(own, *swaps, inner, fine_ghosts, rim_ghosts)
 
     coarse_out = call(
         functools.partial(edges_body, ch_count, k_count, planes),
         f32(Q, cx, cz, cy),
-        [VMEM] * 9,
+        [VMEM] * 7,
         [
             pltpu.VMEM((PLANES, LANES, LANES), jnp.float32),
             pltpu.VMEM((PLANES, LANES, LANES), jnp.float32),
             pltpu.VMEM((Q, SUB, LANES), jnp.float32),
             pltpu.VMEM((Q, cx, cz, cy), jnp.float32),
             pltpu.SemaphoreType.DMA((PIECES,)),
+            pltpu.VMEM((2, PLANES * edge, LANES), jnp.float32),
         ],
         place=HBM,
-    )(left, right, low, *highs, packed, near, coarse_step)
+    )(*swaps, low, high, packed, near, coarse_step)
 
     fine_out = fine.reshape(Q, tiles, k_count, LANES).transpose(2, 0, 1, 3)
     fine_out = fine_out.reshape(k_count, q_count, cells)

time: 65.5 us -> 65.9 us (level)
  waiting for transfers between devices: 27.6 us -> 31.1 us
  starting transfers between devices: 24.7 us -> 21.6 us
    ppermute x5 -> x3, waiting for transfers between devices: 0.01 us -> 3.6 us  [the longest x2 3.6 us: local(): swaps.append(lax.ppermute(values, 'grp', ends + [(j, i) for i, j in ends]))]
    ppermute x5 -> x3, starting transfers between devices: 7.91 us -> 4.81 us  [the longest x1 2.55 us: local(): high = lax.ppermute(widened, 'wide', ring(n_wide, -1))]
  transfers between devices with their start and end apart: 12 -> 10, of which waited for: 2 -> 4; matrix products, arithmetic and copies ran while one was open for 3% -> 3% of each run, Pallas kernels for 10% -> 10%
where the time goes in v6:
time: 65.9 us; the launch traced here: 65.7 us
  waiting for transfers between devices  31.1 us (47%)
  starting transfers between devices  21.6 us (33%)
  Pallas kernels  10 us (15%)
  local copies, waits for them, and re-layouts  2.07 us (3%)
  between operations  0.81 us (1%)
    all_to_all x1, waiting for transfers between devices, local(): spread = lax.all_to_all(pieces, axes, 0, 0, tiled=True)  18.3 us
    ppermute x3, waiting for transfers between devices, local(): below.append(lax.ppermute(part, axes, slab_pairs(n_grp, n_wide, 1, across)))  9.22 us
    all_to_all x1, starting transfers between devices, local(): spread = lax.all_to_all(pieces, axes, 0, 0, tiled=True)  7.33 us
    ppermute x3, starting transfers between devices, local(): below.append(lax.ppermute(part, axes, slab_pairs(n_grp, n_wide, 1, across)))  4.19 us
    ppermute x2, waiting for transfers between devices, local(): swaps.append(lax.ppermute(values, 'grp', ends + [(j, i) for i, j in ends]))  3.6 us
    pallas_call x1, Pallas kernels, local(): call(functools.partial(coarse_body, planes), [f32(Q, cx, cz, cy), f32(Q,...  2.81 us
    ppermute x1, starting transfers between devices, local(): coarse_right = lax.ppermute(coarse_pop[:, :edge], 'grp', ring(n_grp, -1))  2.62 us
    all_to_all x1, starting transfers between devices, local(): lax.all_to_all(outgoing.reshape(devices, rows, k_count, LANES), axes, 0,...  2.61 us
  transfers between devices with their start and end apart: 10, of which 4 were waited for; matrix products, arithmetic and copies ran while one was open for 3% of the time, Pallas kernels for 10%

profile of v6, /device:TPU:0, one launch (start us, length us, event | category | flops | bytes accessed | tf_op | source)
XLA Modules:
  0.0 65.7 jit_solution(4318026754277911719)
XLA Ops:
  0.6 7.3 %all-to-all-start = ((f32[32,19,2,128]{3,2,1,0:T(2,128)}), f32[32,19,2,128]{3,2,1,0:T(2,128)S(1)}, u32[]{:S(2)}, u32[]{:S(2)}) async-start(f32[32,19,2,128]{3,2,1,0:T(2,128)} %bitcast.28), calls=%async_computation | async-start | bytes 1245184 | tf_op jit(solution)/shard_map/all_to_all | solution.py:671
  8.0 18.3 %all-to-all-done = f32[32,19,2,128]{3,2,1,0:T(2,128)S(1)} async-done(((f32[32,19,2,128]{3,2,1,0:T(2,128)}), f32[32,19,2,128]{3,2,1,0:T(2,128)S(1)}, u32[]{:S(2)}, u32[]{:S(2)}) %all-to-all-start) | async-done | bytes 622624 | tf_op jit(solution)/shard_map/all_to_all | solution.py:671
  26.3 1.5 %shard_map.50 = f32[1216,128]{1,0:T(8,128)} custom-call(s32[64]{0:T(128)S(1)} %fusion.2.target_ref, f32[1216,128]{1,0:T(8,128)S(1)} %bitcast.25), custom_call_target="tpu_custom_call" | custom-call | flops 1000000 | bytes 1245184 | tf_op jit(solution)/shard_map/pallas_call | solution.py:687
  27.8 2.6 %all-to-all-start.1 = ((f32[32,19,2,128]{3,2,1,0:T(2,128)}), f32[32,19,2,128]{3,2,1,0:T(2,128)S(1)}, u32[]{:S(2)}, u32[]{:S(2)}) async-start(f32[32,19,2,128]{3,2,1,0:T(2,128)} %bitcast.4), calls=%async_computation.1 | async-start | bytes 1245184 | tf_op jit(solution)/shard_map/all_to_all | solution.py:688
  30.4 2.6 %collective-permute-start.4 = (f32[19,2,8,128]{3,2,1,0:T(8,128)S(1)}, f32[19,2,8,128]{3,2,1,0:T(8,128)S(1)}, u32[]{:S(2)}, u32[]{:S(2)}) collective-permute-start(f32[19,2,8,128]{3,2,1,0:T(8,128)S(1)} %get-tuple-element.36), channel_id=1, source_target_pairs={{0,24},{8,0},{16,8},{24,16},{1,25},{9,1},{17,9},{25,17},{2,26},{10... | collective-permute-start | bytes 466952 | tf_op jit(solution)/shard_map/ppermute | solution.py:674
  33.1 0.0 collective-permute-start.3
  33.1 0.2 slice.24
  33.3 0.5 copy.11
  33.8 0.0 collective-permute-start.1
  33.9 3.2 %collective-permute-start = (f32[19,2,8]{0,2,1:T(8,128)S(1)}, f32[19,2,8]{0,2,1:T(8,128)S(1)}, u32[]{:S(2)}, u32[]{:S(2)}) collective-permute-start(f32[19,2,8]{0,2,1:T(8,128)S(1)} %get-tuple-element.38), channel_id=1, source_target_pairs={{0,9},{1,10},{2,11},{3,12},{4,13},{5,14},{6,15},{7,8},{8,17},{9,18... | collective-permute-start | bytes 3656 | tf_op jit(solution)/shard_map/ppermute | solution.py:678
  37.1 0.9 %collective-permute-start.2 = (f32[19,2,8]{0,2,1:T(8,128)S(1)}, f32[19,2,8]{0,2,1:T(8,128)S(1)}, u32[]{:S(2)}, u32[]{:S(2)}) collective-permute-start(f32[19,2,8]{0,2,1:T(8,128)S(1)} %get-tuple-element.39), channel_id=1, source_target_pairs={{0,25},{1,26},{2,27},{3,28},{4,29},{5,30},{6,31},{7,24},{8,1},{9,2... | collective-permute-start | bytes 3656 | tf_op jit(solution)/shard_map/ppermute | solution.py:678
  38.0 9.2 %collective-permute-done = f32[19,2,8]{0,2,1:T(8,128)S(1)} collective-permute-done((f32[19,2,8]{0,2,1:T(8,128)S(1)}, f32[19,2,8]{0,2,1:T(8,128)S(1)}, u32[]{:S(2)}, u32[]{:S(2)}) %collective-permute-start) | collective-permute-done | bytes 1248 | tf_op jit(solution)/shard_map/ppermute | solution.py:678
  47.2 0.0 collective-permute-done.2
  47.3 0.0 collective-permute-done.1
  47.3 0.0 collective-permute-done.3
  47.4 0.7 %copy.8 = f32[19,12,8,1]{0,2,3,1:T(8,128)S(1)} copy(f32[19,12,8,1]{3,2,1,0:T(8,128)S(1)} %bitcast.24) | data formatting | bytes 14592 | tf_op jit(solution)/shard_map/slice | solution.py:693
  48.1 0.3 copy.9
  48.4 0.2 broadcast_in_dim.2
  48.6 1.0 %shard_map.51 = (f32[2,6,2,24,128]{4,3,2,1,0:T(8,128)S(1)}, f32[2,6,2,8,128]{4,3,2,1,0:T(8,128)S(1)}, f32[2,6,2,8,128]{4,3,2,1,0:T(8,128)S(1)}) custom-call(f32[2,456,8]{2,1,0:T(8,128)S(1)} %bitcast.26, f32[8,256]{1,0:T(8,128)S(1)} %fusion.spread), custom_call_target="tpu_custom_call" | custom-call | flops 1000000 | bytes 1000000 | tf_op jit(solution)/shard_map/pallas_call | solution.py:697
  49.6 2.8 %shard_map.52 = (f32[19,8,8,128]{3,2,1,0:T(8,128)S(1)}, f32[19,8,128]{2,1,0:T(8,128)S(1)}, f32[8,128]{1,0:T(8,128)S(1)}) custom-call(f32[19,12,8,128]{3,2,1,0:T(8,128)S(1)} %constant_dynamic-update-slice_fusion.state), custom_call_target="tpu_custom_call" | custom-call | flops 10000000 | bytes 1000000 | tf_op jit(solution)/shard_map/pallas_call | solution.py:703
  52.4 0.0 all-to-all-done.1
  52.4 0.4 shard_map.53
  52.8 0.5 shard_map.54
  53.4 0.8 %collective-permute-start.5 = (f32[112,128]{1,0:T(8,128)S(1)}, f32[112,128]{1,0:T(8,128)S(1)}, u32[]{:S(2)}, u32[]{:S(2)}) collective-permute-start(f32[112,128]{1,0:T(8,128)S(1)} %get-tuple-element.29), channel_id=1, source_target_pairs={{0,8},{16,24},{8,0},{24,16},{1,9},{17,25},{9,1},{25,17},{2,10},{18... | collective-permute-start | bytes 172040 | tf_op jit(solution)/shard_map/ppermute | solution.py:739
  54.1 1.5 %collective-permute-start.6 = (f32[112,128]{1,0:T(8,128)S(1)}, f32[112,128]{1,0:T(8,128)S(1)}, u32[]{:S(2)}, u32[]{:S(2)}) collective-permute-start(f32[112,128]{1,0:T(8,128)S(1)} %get-tuple-element.30), channel_id=1, source_target_pairs={{8,16},{24,0},{16,8},{0,24},{9,17},{25,1},{17,9},{1,25},{10,18},{2... | collective-permute-start | bytes 172040 | tf_op jit(solution)/shard_map/ppermute | solution.py:739
  55.6 2.0 %collective-permute-done.5.turn_0 = f32[112,128]{1,0:T(8,128)S(1)} collective-permute-done((f32[112,128]{1,0:T(8,128)S(1)}, f32[112,128]{1,0:T(8,128)S(1)}, u32[]{:S(2)}, u32[]{:S(2)}) %collective-permute-start.5) | collective-permute-done | bytes 57376 | tf_op jit(solution)/shard_map/ppermute | solution.py:739
  57.7 1.6 %collective-permute-done.6.turn_1 = f32[112,128]{1,0:T(8,128)S(1)} collective-permute-done((f32[112,128]{1,0:T(8,128)S(1)}, f32[112,128]{1,0:T(8,128)S(1)}, u32[]{:S(2)}, u32[]{:S(2)}) %collective-permute-start.6) | collective-permute-done | bytes 57376 | tf_op jit(solution)/shard_map/ppermute | solution.py:739
  59.2 2.5 %collective-permute-start.7 = (f32[24,128]{1,0:T(8,128)S(1)}, f32[24,128]{1,0:T(8,128)S(1)}, u32[]{:S(2)}, u32[]{:S(2)}) collective-permute-start(f32[24,128]{1,0:T(8,128)S(1)} %pad_maximum_fusion.1), channel_id=1, source_target_pairs={{0,7},{1,0},{2,1},{3,2},{4,3},{5,4},{6,5},{7,6},{8,15},{9,8},{10,9... | collective-permute-start | bytes 36872 | tf_op jit(solution)/shard_map/ppermute | solution.py:752
  61.8 0.5 shard_map.55.inner
  62.3 2.0 %shard_map.56 = f32[1216,128]{1,0:T(8,128)} custom-call(f32[1216,128]{1,0:T(8,128)S(1)} %bitcast.23, f32[112,128]{1,0:T(8,128)S(1)} %collective-permute-done.5.turn_0, f32[112,128]{1,0:T(8,128)S(1)} %collective-permute-done.6.turn_1, f32[19,4,32,128]{3,2,1,0:T(8,128)S(1)} %shard_map.55.inner, f32[2,6,2,24,128]{4,3,2,1,0:T(8,128)S(1)} %get-tuple-element.31.ghosts, ...), custom_call_target="tpu_custom_call" | custom-call | flops 10000000 | bytes 1000000 | tf_op jit(solution)/shard_map/pallas_call | solution.py:754
  64.3 0.0 collective-permute-done.7.high
  64.3 1.4 %shard_map.57 = f32[19,8,8,128]{3,2,1,0:T(8,128)} custom-call(f32[112,128]{1,0:T(8,128)S(1)} %collective-permute-done.5.turn_0, f32[112,128]{1,0:T(8,128)S(1)} %collective-permute-done.6.turn_1, f32[2,8,128]{2,1,0:T(8,128)S(1)} %get-tuple-element.27.low, f32[24,128]{1,0:T(8,128)S(1)} %collective-permute-done.7.high, ...), custom_call_target="tpu_custom_call" | custom-call | flops 1000000 | bytes 1000000 | tf_op jit(solution)/shard_map/pallas_call | solution.py:771
  (18 shorter events, 0.2 us)
Async XLA Ops:
  0.6 7.4 %copy-start.1 = (s32[64]{0:T(128)S(1)}, s32[64]{0:T(128)}, u32[]{:S(2)}) copy-start(s32[64]{0:T(128)} %param.5) | copy-start | bytes 772
  0.6 25.7 %all-to-all-start = ((f32[32,19,2,128]{3,2,1,0:T(2,128)}), f32[32,19,2,128]{3,2,1,0:T(2,128)S(1)}, u32[]{:S(2)}, u32[]{:S(2)}) async-start(f32[32,19,2,128]{3,2,1,0:T(2,128)} %bitcast.28), calls=%async_computation | async-start | bytes 1245184 | tf_op jit(solution)/shard_map/all_to_all | solution.py:671
  26.3 4.1 %copy-start = (f32[19,8,8,128]{3,2,1,0:T(8,128)S(1)}, f32[19,8,8,128]{3,2,1,0:T(8,128)}, u32[]{:S(2)}) copy-start(f32[19,8,8,128]{3,2,1,0:T(8,128)} %param.4) | copy-start | bytes 1867780
  27.8 24.7 %all-to-all-start.1 = ((f32[32,19,2,128]{3,2,1,0:T(2,128)}), f32[32,19,2,128]{3,2,1,0:T(2,128)S(1)}, u32[]{:S(2)}, u32[]{:S(2)}) async-start(f32[32,19,2,128]{3,2,1,0:T(2,128)} %bitcast.4), calls=%async_computation.1 | async-start | bytes 1245184 | tf_op jit(solution)/shard_map/all_to_all | solution.py:688
  30.4 16.9 %collective-permute-start.4 = (f32[19,2,8,128]{3,2,1,0:T(8,128)S(1)}, f32[19,2,8,128]{3,2,1,0:T(8,128)S(1)}, u32[]{:S(2)}, u32[]{:S(2)}) collective-permute-start(f32[19,2,8,128]{3,2,1,0:T(8,128)S(1)} %get-tuple-element.36), channel_id=1, source_target_pairs={{0,24},{8,0},{16,8},{24,16},{1,25},{9,1},{17,9},{25,17},{2,26},{10... | collective-permute-start | bytes 466952 | tf_op jit(solution)/shard_map/ppermute | solution.py:674
  33.1 14.2 %collective-permute-start.3 = (f32[19,2,8,128]{3,2,1,0:T(8,128)S(1)}, f32[19,2,8,128]{3,2,1,0:T(8,128)S(1)}, u32[]{:S(2)}, u32[]{:S(2)}) collective-permute-start(f32[19,2,8,128]{3,2,1,0:T(8,128)S(1)} %get-tuple-element.37), channel_id=1, source_target_pairs={{0,8},{8,16},{16,24},{24,0},{1,9},{9,17},{17,25},{25,1},{2,10},{10... | collective-permute-start | bytes 466952 | tf_op jit(solution)/shard_map/ppermute | solution.py:673
  33.8 13.4 %collective-permute-start.1 = (f32[19,8,8]{0,2,1:T(8,128)S(1)}, f32[19,8,8]{0,2,1:T(8,128)S(1)}, u32[]{:S(2)}, u32[]{:S(2)}) collective-permute-start(f32[19,8,8]{0,2,1:T(8,128)S(1)} %bitcast.31), channel_id=1, source_target_pairs={{0,1},{1,2},{2,3},{3,4},{4,5},{5,6},{6,7},{7,0},{8,9},{9,10},{10,1... | collective-permute-start | bytes 14600 | tf_op jit(solution)/shard_map/ppermute | solution.py:678
  33.9 13.4 %collective-permute-start = (f32[19,2,8]{0,2,1:T(8,128)S(1)}, f32[19,2,8]{0,2,1:T(8,128)S(1)}, u32[]{:S(2)}, u32[]{:S(2)}) collective-permute-start(f32[19,2,8]{0,2,1:T(8,128)S(1)} %get-tuple-element.38), channel_id=1, source_target_pairs={{0,9},{1,10},{2,11},{3,12},{4,13},{5,14},{6,15},{7,8},{8,17},{9,18... | collective-permute-start | bytes 3656 | tf_op jit(solution)/shard_map/ppermute | solution.py:678
  37.1 10.2 %collective-permute-start.2 = (f32[19,2,8]{0,2,1:T(8,128)S(1)}, f32[19,2,8]{0,2,1:T(8,128)S(1)}, u32[]{:S(2)}, u32[]{:S(2)}) collective-permute-start(f32[19,2,8]{0,2,1:T(8,128)S(1)} %get-tuple-element.39), channel_id=1, source_target_pairs={{0,25},{1,26},{2,27},{3,28},{4,29},{5,30},{6,31},{7,24},{8,1},{9,2... | collective-permute-start | bytes 3656 | tf_op jit(solution)/shard_map/ppermute | solution.py:678
  53.4 4.3 %collective-permute-start.5 = (f32[112,128]{1,0:T(8,128)S(1)}, f32[112,128]{1,0:T(8,128)S(1)}, u32[]{:S(2)}, u32[]{:S(2)}) collective-permute-start(f32[112,128]{1,0:T(8,128)S(1)} %get-tuple-element.29), channel_id=1, source_target_pairs={{0,8},{16,24},{8,0},{24,16},{1,9},{17,25},{9,1},{25,17},{2,10},{18... | collective-permute-start | bytes 172040 | tf_op jit(solution)/shard_map/ppermute | solution.py:739
  54.1 5.1 %collective-permute-start.6 = (f32[112,128]{1,0:T(8,128)S(1)}, f32[112,128]{1,0:T(8,128)S(1)}, u32[]{:S(2)}, u32[]{:S(2)}) collective-permute-start(f32[112,128]{1,0:T(8,128)S(1)} %get-tuple-element.30), channel_id=1, source_target_pairs={{8,16},{24,0},{16,8},{0,24},{9,17},{25,1},{17,9},{1,25},{10,18},{2... | collective-permute-start | bytes 172040 | tf_op jit(solution)/shard_map/ppermute | solution.py:739
  59.2 5.1 %collective-permute-start.7 = (f32[24,128]{1,0:T(8,128)S(1)}, f32[24,128]{1,0:T(8,128)S(1)}, u32[]{:S(2)}, u32[]{:S(2)}) collective-permute-start(f32[24,128]{1,0:T(8,128)S(1)} %pad_maximum_fusion.1), channel_id=1, source_target_pairs={{0,7},{1,0},{2,1},{3,2},{4,3},{5,4},{6,5},{7,6},{8,15},{9,8},{10,9... | collective-permute-start | bytes 36872 | tf_op jit(solution)/shard_map/ppermute | solution.py:752

commit v7 on v6

--- a/solution.py
+++ b/solution.py
@@ -150,9 +150,10 @@
 
 
 def regroup_body(blocks, k_blocks, rows, target_ref, in_ref, out_ref):
+    targets = target_ref[...]
     for b in range(blocks):
         source = (b // k_blocks) * (rows * k_blocks) + b % k_blocks
-        out_ref[pl.ds(target_ref[b], rows, stride=k_blocks), :] = in_ref[
+        out_ref[pl.ds(targets[0, b], rows, stride=k_blocks), :] = in_ref[
             pl.ds(source, rows, stride=k_blocks), :
         ]
 
@@ -462,29 +463,41 @@
                     ]
 
 
-GROUP = 16
-STEP = 32
-PLANES = -(-Q // GROUP)
+STEP = 2 * B
+GROUP = B // 2
+PLANES = -(-2 * Q // STEP)
+
+
+def place_of(i, ch):
+    group, at = divmod(2 * i + ch, GROUP)
+    plane, quarter = divmod(group, 4)
+    return plane, 2 * at + quarter % 2 + B * (quarter // 2)
 
 
 def pack(load, ch_count, k_count, side):
     lane = lax.broadcasted_iota(jnp.int32, (SUB, LANES), 1)
     offset = B - 2 if side == 0 else 0
-    kept = lane % STEP == offset
+    layers = lane % B // 2 == offset // 2
+    kept = (lane % STEP < B) & (lane % 2 == 0)
     k = k_count - 1 if side == 0 else 0
+    slots = [(i, ch) for i in range(Q) for ch in range(ch_count)]
     planes = [None] * PLANES
-    for i in range(Q):
-        for ch in range(ch_count):
+    for first in range(0, len(slots), GROUP):
+        total = None
+        for at, (i, ch) in enumerate(slots[first : first + GROUP]):
             q = ch * k_count + k
-            v = load(i, q, 0) + load(i, q, 1)
-            v = v + pltpu.roll(v, LANES - 1, 1)
-            v = v + pltpu.roll(v, LANES - B, 1)
-            v = jnp.where(kept, v, 0.0)
-            shift = (2 * (i % GROUP) + ch - offset) % LANES
+            v = jnp.where(layers, load(i, q, 0) + load(i, q, 1), 0.0)
+            shift = (2 * at - offset) % LANES
             if shift:
                 v = pltpu.roll(v, shift, 1)
-            n = i // GROUP
-            planes[n] = v if planes[n] is None else planes[n] + v
+            total = v if total is None else total + v
+        total = total + pltpu.roll(total, LANES - 1, 1)
+        total = total + pltpu.roll(total, LANES - B, 1)
+        total = jnp.where(kept, total, 0.0)
+        plane, shift = place_of(*slots[first])
+        if shift:
+            total = pltpu.roll(total, shift, 1)
+        planes[plane] = total if planes[plane] is None else planes[plane] + total
     return planes
 
 
@@ -581,8 +594,9 @@
     per = LANES // STEP
     for i in range(Q):
         for ch in range(ch_count):
+            plane, at = place_of(i, ch)
             ghost[i, pl.ds(ch * per, per), :] = (
-                0.125 * columns[i // GROUP, pl.ds(2 * (i % GROUP) + ch, per, stride=STEP), :]
+                0.125 * columns[plane, pl.ds(at, per, stride=STEP), :]
             )
 
     beyond, entering = rescaled([ghost[i] for i in range(Q)], TO_COARSE, UP + DOWN)
@@ -680,11 +694,11 @@
     regroup = call(
         functools.partial(regroup_body, blocks, k_count, rows),
         f32(total, LANES),
-        [SMEM, VMEM],
+        [VMEM, VMEM],
         moved=8 * total * LANES,
     )
     targets = rows * new_slot - (rows - 1) * (new_slot % k_count)
-    outgoing = regroup(targets, spread.reshape(total, LANES))
+    outgoing = regroup(targets[None], spread.reshape(total, LANES))
     arrived = lax.all_to_all(
         outgoing.reshape(devices, rows, k_count, LANES), axes, 0, 0, tiled=True
     )

time: 65.9 us -> 65.5 us (level)
  no operation moved by 1% of the time
where the time goes in v7:
time: 65.5 us; the launch traced here: 65.2 us
  waiting for transfers between devices  31.1 us (47%)
  starting transfers between devices  21.6 us (33%)
  Pallas kernels  9.57 us (15%)
  local copies, waits for them, and re-layouts  2.07 us (3%)
  between operations  0.81 us (1%)
    all_to_all x1, waiting for transfers between devices, local(): spread = lax.all_to_all(pieces, axes, 0, 0, tiled=True)  18.3 us
    ppermute x3, waiting for transfers between devices, local(): below.append(lax.ppermute(part, axes, slab_pairs(n_grp, n_wide, 1, across)))  9.22 us
    all_to_all x1, starting transfers between devices, local(): spread = lax.all_to_all(pieces, axes, 0, 0, tiled=True)  7.33 us
    ppermute x3, starting transfers between devices, local(): below.append(lax.ppermute(part, axes, slab_pairs(n_grp, n_wide, 1, across)))  4.19 us
    ppermute x2, waiting for transfers between devices, local(): swaps.append(lax.ppermute(values, 'grp', ends + [(j, i) for i, j in ends]))  3.59 us
    pallas_call x1, Pallas kernels, local(): call(functools.partial(coarse_body, planes), [f32(Q, cx, cz, cy), f32(Q,...  2.81 us
    ppermute x1, starting transfers between devices, local(): coarse_right = lax.ppermute(coarse_pop[:, :edge], 'grp', ring(n_grp, -1))  2.62 us
    all_to_all x1, starting transfers between devices, local(): lax.all_to_all(outgoing.reshape(devices, rows, k_count, LANES), axes, 0,...  2.61 us
  transfers between devices with their start and end apart: 10, of which 4 were waited for; matrix products, arithmetic and copies ran while one was open for 3% of the time, Pallas kernels for 10%

profile of v7, /device:TPU:0, one launch (start us, length us, event | category | flops | bytes accessed | tf_op | source)
XLA Modules:
  0.0 65.2 jit_solution(13712929511412570488)
XLA Ops:
  0.6 7.3 %all-to-all-start = ((f32[32,19,2,128]{3,2,1,0:T(2,128)}), f32[32,19,2,128]{3,2,1,0:T(2,128)S(1)}, u32[]{:S(2)}, u32[]{:S(2)}) async-start(f32[32,19,2,128]{3,2,1,0:T(2,128)} %bitcast.30), calls=%async_computation | async-start | bytes 1245184 | tf_op jit(solution)/shard_map/all_to_all | solution.py:685
  8.0 18.3 %all-to-all-done = f32[32,19,2,128]{3,2,1,0:T(2,128)S(1)} async-done(((f32[32,19,2,128]{3,2,1,0:T(2,128)}), f32[32,19,2,128]{3,2,1,0:T(2,128)S(1)}, u32[]{:S(2)}, u32[]{:S(2)}) %all-to-all-start) | async-done | bytes 622624 | tf_op jit(solution)/shard_map/all_to_all | solution.py:685
  26.3 1.0 %shard_map.50 = f32[1216,128]{1,0:T(8,128)} custom-call(s32[1,64]{1,0:T(1,128)S(1)} %fusion.4.target_ref, f32[1216,128]{1,0:T(8,128)S(1)} %bitcast.27), custom_call_target="tpu_custom_call" | custom-call | flops 1000000 | bytes 1245184 | tf_op jit(solution)/shard_map/pallas_call | solution.py:701
  27.3 2.6 %all-to-all-start.1 = ((f32[32,19,2,128]{3,2,1,0:T(2,128)}), f32[32,19,2,128]{3,2,1,0:T(2,128)S(1)}, u32[]{:S(2)}, u32[]{:S(2)}) async-start(f32[32,19,2,128]{3,2,1,0:T(2,128)} %bitcast.5), calls=%async_computation.1 | async-start | bytes 1245184 | tf_op jit(solution)/shard_map/all_to_all | solution.py:702
  30.0 2.6 %collective-permute-start.4 = (f32[19,2,8,128]{3,2,1,0:T(8,128)S(1)}, f32[19,2,8,128]{3,2,1,0:T(8,128)S(1)}, u32[]{:S(2)}, u32[]{:S(2)}) collective-permute-start(f32[19,2,8,128]{3,2,1,0:T(8,128)S(1)} %get-tuple-element.36), channel_id=1, source_target_pairs={{0,24},{8,0},{16,8},{24,16},{1,25},{9,1},{17,9},{25,17},{2,26},{10... | collective-permute-start | bytes 466952 | tf_op jit(solution)/shard_map/ppermute | solution.py:688
  32.6 0.0 collective-permute-start.3
  32.6 0.2 slice.24
  32.9 0.5 copy.11
  33.4 0.0 collective-permute-start.1
  33.4 3.2 %collective-permute-start = (f32[19,2,8]{0,2,1:T(8,128)S(1)}, f32[19,2,8]{0,2,1:T(8,128)S(1)}, u32[]{:S(2)}, u32[]{:S(2)}) collective-permute-start(f32[19,2,8]{0,2,1:T(8,128)S(1)} %get-tuple-element.38), channel_id=1, source_target_pairs={{0,9},{1,10},{2,11},{3,12},{4,13},{5,14},{6,15},{7,8},{8,17},{9,18... | collective-permute-start | bytes 3656 | tf_op jit(solution)/shard_map/ppermute | solution.py:692
  36.7 0.9 %collective-permute-start.2 = (f32[19,2,8]{0,2,1:T(8,128)S(1)}, f32[19,2,8]{0,2,1:T(8,128)S(1)}, u32[]{:S(2)}, u32[]{:S(2)}) collective-permute-start(f32[19,2,8]{0,2,1:T(8,128)S(1)} %get-tuple-element.39), channel_id=1, source_target_pairs={{0,25},{1,26},{2,27},{3,28},{4,29},{5,30},{6,31},{7,24},{8,1},{9,2... | collective-permute-start | bytes 3656 | tf_op jit(solution)/shard_map/ppermute | solution.py:692
  37.6 9.2 %collective-permute-done = f32[19,2,8]{0,2,1:T(8,128)S(1)} collective-permute-done((f32[19,2,8]{0,2,1:T(8,128)S(1)}, f32[19,2,8]{0,2,1:T(8,128)S(1)}, u32[]{:S(2)}, u32[]{:S(2)}) %collective-permute-start) | collective-permute-done | bytes 1248 | tf_op jit(solution)/shard_map/ppermute | solution.py:692
  46.8 0.0 collective-permute-done.2
  46.8 0.0 collective-permute-done.1
  46.8 0.0 collective-permute-done.3
  46.9 0.7 %copy.8 = f32[19,12,8,1]{0,2,3,1:T(8,128)S(1)} copy(f32[19,12,8,1]{3,2,1,0:T(8,128)S(1)} %bitcast.26) | data formatting | bytes 14592 | tf_op jit(solution)/shard_map/slice | solution.py:707
  47.7 0.3 copy.9
  48.0 0.2 broadcast_in_dim.9
  48.2 1.0 %shard_map.51 = (f32[2,6,2,24,128]{4,3,2,1,0:T(8,128)S(1)}, f32[2,6,2,8,128]{4,3,2,1,0:T(8,128)S(1)}, f32[2,6,2,8,128]{4,3,2,1,0:T(8,128)S(1)}) custom-call(f32[2,456,8]{2,1,0:T(8,128)S(1)} %bitcast.28, f32[8,256]{1,0:T(8,128)S(1)} %fusion.spread), custom_call_target="tpu_custom_call" | custom-call | flops 1000000 | bytes 1000000 | tf_op jit(solution)/shard_map/pallas_call | solution.py:711
  49.2 2.8 %shard_map.52 = (f32[19,8,8,128]{3,2,1,0:T(8,128)S(1)}, f32[19,8,128]{2,1,0:T(8,128)S(1)}, f32[8,128]{1,0:T(8,128)S(1)}) custom-call(f32[19,12,8,128]{3,2,1,0:T(8,128)S(1)} %constant_dynamic-update-slice_fusion.state), custom_call_target="tpu_custom_call" | custom-call | flops 10000000 | bytes 1000000 | tf_op jit(solution)/shard_map/pallas_call | solution.py:717
  52.0 0.0 all-to-all-done.1
  52.0 0.3 shard_map.53
  52.3 0.5 shard_map.54
  52.9 0.8 %collective-permute-start.5 = (f32[112,128]{1,0:T(8,128)S(1)}, f32[112,128]{1,0:T(8,128)S(1)}, u32[]{:S(2)}, u32[]{:S(2)}) collective-permute-start(f32[112,128]{1,0:T(8,128)S(1)} %get-tuple-element.29), channel_id=1, source_target_pairs={{0,8},{16,24},{8,0},{24,16},{1,9},{17,25},{9,1},{25,17},{2,10},{18... | collective-permute-start | bytes 172040 | tf_op jit(solution)/shard_map/ppermute | solution.py:753
  53.7 1.5 %collective-permute-start.6 = (f32[112,128]{1,0:T(8,128)S(1)}, f32[112,128]{1,0:T(8,128)S(1)}, u32[]{:S(2)}, u32[]{:S(2)}) collective-permute-start(f32[112,128]{1,0:T(8,128)S(1)} %get-tuple-element.30), channel_id=1, source_target_pairs={{8,16},{24,0},{16,8},{0,24},{9,17},{25,1},{17,9},{1,25},{10,18},{2... | collective-permute-start | bytes 172040 | tf_op jit(solution)/shard_map/ppermute | solution.py:753
  55.1 2.0 %collective-permute-done.5.turn_0 = f32[112,128]{1,0:T(8,128)S(1)} collective-permute-done((f32[112,128]{1,0:T(8,128)S(1)}, f32[112,128]{1,0:T(8,128)S(1)}, u32[]{:S(2)}, u32[]{:S(2)}) %collective-permute-start.5) | collective-permute-done | bytes 57376 | tf_op jit(solution)/shard_map/ppermute | solution.py:753
  57.2 1.6 %collective-permute-done.6.turn_1 = f32[112,128]{1,0:T(8,128)S(1)} collective-permute-done((f32[112,128]{1,0:T(8,128)S(1)}, f32[112,128]{1,0:T(8,128)S(1)}, u32[]{:S(2)}, u32[]{:S(2)}) %collective-permute-start.6) | collective-permute-done | bytes 57376 | tf_op jit(solution)/shard_map/ppermute | solution.py:753
  58.8 2.5 %collective-permute-start.7 = (f32[24,128]{1,0:T(8,128)S(1)}, f32[24,128]{1,0:T(8,128)S(1)}, u32[]{:S(2)}, u32[]{:S(2)}) collective-permute-start(f32[24,128]{1,0:T(8,128)S(1)} %pad_maximum_fusion.1), channel_id=1, source_target_pairs={{0,7},{1,0},{2,1},{3,2},{4,3},{5,4},{6,5},{7,6},{8,15},{9,8},{10,9... | collective-permute-start | bytes 36872 | tf_op jit(solution)/shard_map/ppermute | solution.py:766
  61.3 0.5 shard_map.55.inner
  61.8 2.0 %shard_map.56 = f32[1216,128]{1,0:T(8,128)} custom-call(f32[1216,128]{1,0:T(8,128)S(1)} %bitcast.25, f32[112,128]{1,0:T(8,128)S(1)} %collective-permute-done.5.turn_0, f32[112,128]{1,0:T(8,128)S(1)} %collective-permute-done.6.turn_1, f32[19,4,32,128]{3,2,1,0:T(8,128)S(1)} %shard_map.55.inner, f32[2,6,2,24,128]{4,3,2,1,0:T(8,128)S(1)} %get-tuple-element.31.ghosts, ...), custom_call_target="tpu_custom_call" | custom-call | flops 10000000 | bytes 1000000 | tf_op jit(solution)/shard_map/pallas_call | solution.py:768
  63.8 0.0 collective-permute-done.7.high
  63.8 1.4 %shard_map.57 = f32[19,8,8,128]{3,2,1,0:T(8,128)} custom-call(f32[112,128]{1,0:T(8,128)S(1)} %collective-permute-done.5.turn_0, f32[112,128]{1,0:T(8,128)S(1)} %collective-permute-done.6.turn_1, f32[2,8,128]{2,1,0:T(8,128)S(1)} %get-tuple-element.27.low, f32[24,128]{1,0:T(8,128)S(1)} %collective-permute-done.7.high, ...), custom_call_target="tpu_custom_call" | custom-call | flops 1000000 | bytes 1000000 | tf_op jit(solution)/shard_map/pallas_call | solution.py:785
  (18 shorter events, 0.2 us)
Async XLA Ops:
  0.6 7.4 %copy-start.1 = (s32[64]{0:T(128)S(1)}, s32[64]{0:T(128)}, u32[]{:S(2)}) copy-start(s32[64]{0:T(128)} %param.5) | copy-start | bytes 772
  0.6 25.7 %all-to-all-start = ((f32[32,19,2,128]{3,2,1,0:T(2,128)}), f32[32,19,2,128]{3,2,1,0:T(2,128)S(1)}, u32[]{:S(2)}, u32[]{:S(2)}) async-start(f32[32,19,2,128]{3,2,1,0:T(2,128)} %bitcast.30), calls=%async_computation | async-start | bytes 1245184 | tf_op jit(solution)/shard_map/all_to_all | solution.py:685
  26.3 3.6 %copy-start = (f32[19,8,8,128]{3,2,1,0:T(8,128)S(1)}, f32[19,8,8,128]{3,2,1,0:T(8,128)}, u32[]{:S(2)}) copy-start(f32[19,8,8,128]{3,2,1,0:T(8,128)} %param.4) | copy-start | bytes 1867780
  27.3 24.7 %all-to-all-start.1 = ((f32[32,19,2,128]{3,2,1,0:T(2,128)}), f32[32,19,2,128]{3,2,1,0:T(2,128)S(1)}, u32[]{:S(2)}, u32[]{:S(2)}) async-start(f32[32,19,2,128]{3,2,1,0:T(2,128)} %bitcast.5), calls=%async_computation.1 | async-start | bytes 1245184 | tf_op jit(solution)/shard_map/all_to_all | solution.py:702
  30.0 16.9 %collective-permute-start.4 = (f32[19,2,8,128]{3,2,1,0:T(8,128)S(1)}, f32[19,2,8,128]{3,2,1,0:T(8,128)S(1)}, u32[]{:S(2)}, u32[]{:S(2)}) collective-permute-start(f32[19,2,8,128]{3,2,1,0:T(8,128)S(1)} %get-tuple-element.36), channel_id=1, source_target_pairs={{0,24},{8,0},{16,8},{24,16},{1,25},{9,1},{17,9},{25,17},{2,26},{10... | collective-permute-start | bytes 466952 | tf_op jit(solution)/shard_map/ppermute | solution.py:688
  32.6 14.2 %collective-permute-start.3 = (f32[19,2,8,128]{3,2,1,0:T(8,128)S(1)}, f32[19,2,8,128]{3,2,1,0:T(8,128)S(1)}, u32[]{:S(2)}, u32[]{:S(2)}) collective-permute-start(f32[19,2,8,128]{3,2,1,0:T(8,128)S(1)} %get-tuple-element.37), channel_id=1, source_target_pairs={{0,8},{8,16},{16,24},{24,0},{1,9},{9,17},{17,25},{25,1},{2,10},{10... | collective-permute-start | bytes 466952 | tf_op jit(solution)/shard_map/ppermute | solution.py:687
  33.4 13.4 %collective-permute-start.1 = (f32[19,8,8]{0,2,1:T(8,128)S(1)}, f32[19,8,8]{0,2,1:T(8,128)S(1)}, u32[]{:S(2)}, u32[]{:S(2)}) collective-permute-start(f32[19,8,8]{0,2,1:T(8,128)S(1)} %bitcast.33), channel_id=1, source_target_pairs={{0,1},{1,2},{2,3},{3,4},{4,5},{5,6},{6,7},{7,0},{8,9},{9,10},{10,1... | collective-permute-start | bytes 14600 | tf_op jit(solution)/shard_map/ppermute | solution.py:692
  33.4 13.4 %collective-permute-start = (f32[19,2,8]{0,2,1:T(8,128)S(1)}, f32[19,2,8]{0,2,1:T(8,128)S(1)}, u32[]{:S(2)}, u32[]{:S(2)}) collective-permute-start(f32[19,2,8]{0,2,1:T(8,128)S(1)} %get-tuple-element.38), channel_id=1, source_target_pairs={{0,9},{1,10},{2,11},{3,12},{4,13},{5,14},{6,15},{7,8},{8,17},{9,18... | collective-permute-start | bytes 3656 | tf_op jit(solution)/shard_map/ppermute | solution.py:692
  36.7 10.2 %collective-permute-start.2 = (f32[19,2,8]{0,2,1:T(8,128)S(1)}, f32[19,2,8]{0,2,1:T(8,128)S(1)}, u32[]{:S(2)}, u32[]{:S(2)}) collective-permute-start(f32[19,2,8]{0,2,1:T(8,128)S(1)} %get-tuple-element.39), channel_id=1, source_target_pairs={{0,25},{1,26},{2,27},{3,28},{4,29},{5,30},{6,31},{7,24},{8,1},{9,2... | collective-permute-start | bytes 3656 | tf_op jit(solution)/shard_map/ppermute | solution.py:692
  52.9 4.3 %collective-permute-start.5 = (f32[112,128]{1,0:T(8,128)S(1)}, f32[112,128]{1,0:T(8,128)S(1)}, u32[]{:S(2)}, u32[]{:S(2)}) collective-permute-start(f32[112,128]{1,0:T(8,128)S(1)} %get-tuple-element.29), channel_id=1, source_target_pairs={{0,8},{16,24},{8,0},{24,16},{1,9},{17,25},{9,1},{25,17},{2,10},{18... | collective-permute-start | bytes 172040 | tf_op jit(solution)/shard_map/ppermute | solution.py:753
  53.7 5.1 %collective-permute-start.6 = (f32[112,128]{1,0:T(8,128)S(1)}, f32[112,128]{1,0:T(8,128)S(1)}, u32[]{:S(2)}, u32[]{:S(2)}) collective-permute-start(f32[112,128]{1,0:T(8,128)S(1)} %get-tuple-element.30), channel_id=1, source_target_pairs={{8,16},{24,0},{16,8},{0,24},{9,17},{25,1},{17,9},{1,25},{10,18},{2... | collective-permute-start | bytes 172040 | tf_op jit(solution)/shard_map/ppermute | solution.py:753
  58.8 5.1 %collective-permute-start.7 = (f32[24,128]{1,0:T(8,128)S(1)}, f32[24,128]{1,0:T(8,128)S(1)}, u32[]{:S(2)}, u32[]{:S(2)}) collective-permute-start(f32[24,128]{1,0:T(8,128)S(1)} %pad_maximum_fusion.1), channel_id=1, source_target_pairs={{0,7},{1,0},{2,1},{3,2},{4,3},{5,4},{6,5},{7,6},{8,15},{9,8},{10,9... | collective-permute-start | bytes 36872 | tf_op jit(solution)/shard_map/ppermute | solution.py:766

commit v8 on v5

--- a/solution.py
+++ b/solution.py
@@ -51,7 +51,6 @@
 NG = len(UP) + 1
 
 VMEM = pl.BlockSpec(memory_space=pltpu.VMEM)
-SMEM = pl.BlockSpec(memory_space=pltpu.SMEM)
 HBM = pl.BlockSpec(memory_space=pl.ANY)
 
 
@@ -150,9 +149,10 @@
 
 
 def regroup_body(blocks, k_blocks, rows, target_ref, in_ref, out_ref):
+    targets = target_ref[...]
     for b in range(blocks):
         source = (b // k_blocks) * (rows * k_blocks) + b % k_blocks
-        out_ref[pl.ds(target_ref[b], rows, stride=k_blocks), :] = in_ref[
+        out_ref[pl.ds(targets[0, b], rows, stride=k_blocks), :] = in_ref[
             pl.ds(source, rows, stride=k_blocks), :
         ]
 
@@ -449,29 +449,41 @@
                     ]
 
 
-GROUP = 16
-STEP = 32
-PLANES = -(-Q // GROUP)
+STEP = 2 * B
+GROUP = B // 2
+PLANES = -(-2 * Q // STEP)
+
+
+def place_of(i, ch):
+    group, at = divmod(2 * i + ch, GROUP)
+    plane, quarter = divmod(group, 4)
+    return plane, 2 * at + quarter % 2 + B * (quarter // 2)
 
 
 def pack(load, ch_count, k_count, side):
     lane = lax.broadcasted_iota(jnp.int32, (SUB, LANES), 1)
     offset = B - 2 if side == 0 else 0
-    kept = lane % STEP == offset
+    layers = lane % B // 2 == offset // 2
+    kept = (lane % STEP < B) & (lane % 2 == 0)
     k = k_count - 1 if side == 0 else 0
+    slots = [(i, ch) for i in range(Q) for ch in range(ch_count)]
     planes = [None] * PLANES
-    for i in range(Q):
-        for ch in range(ch_count):
+    for first in range(0, len(slots), GROUP):
+        total = None
+        for at, (i, ch) in enumerate(slots[first : first + GROUP]):
             q = ch * k_count + k
-            v = load(i, q, 0) + load(i, q, 1)
-            v = v + pltpu.roll(v, LANES - 1, 1)
-            v = v + pltpu.roll(v, LANES - B, 1)
-            v = jnp.where(kept, v, 0.0)
-            shift = (2 * (i % GROUP) + ch - offset) % LANES
+            v = jnp.where(layers, load(i, q, 0) + load(i, q, 1), 0.0)
+            shift = (2 * at - offset) % LANES
             if shift:
                 v = pltpu.roll(v, shift, 1)
-            n = i // GROUP
-            planes[n] = v if planes[n] is None else planes[n] + v
+            total = v if total is None else total + v
+        total = total + pltpu.roll(total, LANES - 1, 1)
+        total = total + pltpu.roll(total, LANES - B, 1)
+        total = jnp.where(kept, total, 0.0)
+        plane, shift = place_of(*slots[first])
+        if shift:
+            total = pltpu.roll(total, shift, 1)
+        planes[plane] = total if planes[plane] is None else planes[plane] + total
     return planes
 
 
@@ -563,8 +575,9 @@
     per = LANES // STEP
     for i in range(Q):
         for ch in range(ch_count):
+            plane, at = place_of(i, ch)
             ghost[i, pl.ds(ch * per, per), :] = (
-                0.125 * columns[i // GROUP, pl.ds(2 * (i % GROUP) + ch, per, stride=STEP), :]
+                0.125 * columns[plane, pl.ds(at, per, stride=STEP), :]
             )
 
     beyond, entering = rescaled([ghost[i] for i in range(Q)], TO_COARSE, UP + DOWN)
@@ -662,11 +675,11 @@
     regroup = call(
         functools.partial(regroup_body, blocks, k_count, rows),
         f32(total, LANES),
-        [SMEM, VMEM],
+        [VMEM, VMEM],
         moved=8 * total * LANES,
     )
     targets = rows * new_slot - (rows - 1) * (new_slot % k_count)
-    outgoing = regroup(targets, spread.reshape(total, LANES))
+    outgoing = regroup(targets[None], spread.reshape(total, LANES))
     arrived = lax.all_to_all(
         outgoing.reshape(devices, rows, k_count, LANES), axes, 0, 0, tiled=True
     )

time: 65.5 us -> 65 us (level)
  no operation moved by 1% of the time
where the time goes in v8:
time: 65 us; the launch traced here: 64.7 us
  waiting for transfers between devices  27.6 us (42%)
  starting transfers between devices  24.7 us (38%)
  Pallas kernels  9.54 us (15%)
  local copies, waits for them, and re-layouts  2.06 us (3%)
  between operations  0.84 us (1%)
    all_to_all x1, waiting for transfers between devices, local(): spread = lax.all_to_all(pieces, axes, 0, 0, tiled=True)  18.3 us
    ppermute x3, waiting for transfers between devices, local(): below.append(lax.ppermute(part, axes, slab_pairs(n_grp, n_wide, 1, across)))  9.22 us
    all_to_all x1, starting transfers between devices, local(): spread = lax.all_to_all(pieces, axes, 0, 0, tiled=True)  7.33 us
    ppermute x3, starting transfers between devices, local(): lax.ppermute(first, axes, slab_pairs(n_grp, n_wide, -1, across))  4.92 us
    ppermute x3, starting transfers between devices, local(): below.append(lax.ppermute(part, axes, slab_pairs(n_grp, n_wide, 1, across)))  4.19 us
    pallas_call x1, Pallas kernels, local(): call(functools.partial(coarse_body, planes), [f32(Q, cx, cz, cy), f32(Q,...  2.81 us
    ppermute x1, starting transfers between devices, local(): coarse_right = lax.ppermute(coarse_pop[:, :edge], 'grp', ring(n_grp, -1))  2.62 us
    all_to_all x1, starting transfers between devices, local(): lax.all_to_all(outgoing.reshape(devices, rows, k_count, LANES), axes, 0,...  2.61 us
  transfers between devices with their start and end apart: 12, of which 2 were waited for; matrix products, arithmetic and copies ran while one was open for 3% of the time, Pallas kernels for 10%

profile of v8, /device:TPU:0, one launch (start us, length us, event | category | flops | bytes accessed | tf_op | source)
XLA Modules:
  0.0 64.7 jit_solution(14124439763958724224)
XLA Ops:
  0.6 7.3 %all-to-all-start = ((f32[32,19,2,128]{3,2,1,0:T(2,128)}), f32[32,19,2,128]{3,2,1,0:T(2,128)S(1)}, u32[]{:S(2)}, u32[]{:S(2)}) async-start(f32[32,19,2,128]{3,2,1,0:T(2,128)} %bitcast.28), calls=%async_computation | async-start | bytes 1245184 | tf_op jit(solution)/shard_map/all_to_all | solution.py:666
  8.0 18.3 %all-to-all-done = f32[32,19,2,128]{3,2,1,0:T(2,128)S(1)} async-done(((f32[32,19,2,128]{3,2,1,0:T(2,128)}), f32[32,19,2,128]{3,2,1,0:T(2,128)S(1)}, u32[]{:S(2)}, u32[]{:S(2)}) %all-to-all-start) | async-done | bytes 622624 | tf_op jit(solution)/shard_map/all_to_all | solution.py:666
  26.3 1.0 %shard_map.50 = f32[1216,128]{1,0:T(8,128)} custom-call(s32[1,64]{1,0:T(1,128)S(1)} %fusion.4.target_ref, f32[1216,128]{1,0:T(8,128)S(1)} %bitcast.26), custom_call_target="tpu_custom_call" | custom-call | flops 1000000 | bytes 1245184 | tf_op jit(solution)/shard_map/pallas_call | solution.py:682
  27.3 2.6 %all-to-all-start.1 = ((f32[32,19,2,128]{3,2,1,0:T(2,128)}), f32[32,19,2,128]{3,2,1,0:T(2,128)S(1)}, u32[]{:S(2)}, u32[]{:S(2)}) async-start(f32[32,19,2,128]{3,2,1,0:T(2,128)} %bitcast.5), calls=%async_computation.1 | async-start | bytes 1245184 | tf_op jit(solution)/shard_map/all_to_all | solution.py:683
  30.0 2.6 %collective-permute-start.4 = (f32[19,2,8,128]{3,2,1,0:T(8,128)S(1)}, f32[19,2,8,128]{3,2,1,0:T(8,128)S(1)}, u32[]{:S(2)}, u32[]{:S(2)}) collective-permute-start(f32[19,2,8,128]{3,2,1,0:T(8,128)S(1)} %get-tuple-element.36), channel_id=1, source_target_pairs={{0,24},{8,0},{16,8},{24,16},{1,25},{9,1},{17,9},{25,17},{2,26},{10... | collective-permute-start | bytes 466952 | tf_op jit(solution)/shard_map/ppermute | solution.py:669
  32.6 0.0 collective-permute-start.3
  32.6 0.2 slice.18
  32.9 0.5 copy.11
  33.4 0.0 collective-permute-start.1
  33.4 3.2 %collective-permute-start = (f32[19,2,8]{0,2,1:T(8,128)S(1)}, f32[19,2,8]{0,2,1:T(8,128)S(1)}, u32[]{:S(2)}, u32[]{:S(2)}) collective-permute-start(f32[19,2,8]{0,2,1:T(8,128)S(1)} %get-tuple-element.38), channel_id=1, source_target_pairs={{0,9},{1,10},{2,11},{3,12},{4,13},{5,14},{6,15},{7,8},{8,17},{9,18... | collective-permute-start | bytes 3656 | tf_op jit(solution)/shard_map/ppermute | solution.py:673
  36.7 0.9 %collective-permute-start.2 = (f32[19,2,8]{0,2,1:T(8,128)S(1)}, f32[19,2,8]{0,2,1:T(8,128)S(1)}, u32[]{:S(2)}, u32[]{:S(2)}) collective-permute-start(f32[19,2,8]{0,2,1:T(8,128)S(1)} %get-tuple-element.39), channel_id=1, source_target_pairs={{0,25},{1,26},{2,27},{3,28},{4,29},{5,30},{6,31},{7,24},{8,1},{9,2... | collective-permute-start | bytes 3656 | tf_op jit(solution)/shard_map/ppermute | solution.py:673
  37.6 9.2 %collective-permute-done = f32[19,2,8]{0,2,1:T(8,128)S(1)} collective-permute-done((f32[19,2,8]{0,2,1:T(8,128)S(1)}, f32[19,2,8]{0,2,1:T(8,128)S(1)}, u32[]{:S(2)}, u32[]{:S(2)}) %collective-permute-start) | collective-permute-done | bytes 1248 | tf_op jit(solution)/shard_map/ppermute | solution.py:673
  46.8 0.0 collective-permute-done.2
  46.8 0.0 collective-permute-done.1
  46.9 0.7 %copy.8 = f32[19,12,8,1]{0,2,3,1:T(8,128)S(1)} copy(f32[19,12,8,1]{3,2,1,0:T(8,128)S(1)} %bitcast.25) | data formatting | bytes 14592 | tf_op jit(solution)/shard_map/slice | solution.py:688
  47.7 0.3 copy.9
  48.0 0.2 broadcast_in_dim.9
  48.2 1.0 %shard_map.51 = (f32[2,6,2,24,128]{4,3,2,1,0:T(8,128)S(1)}, f32[2,6,2,8,128]{4,3,2,1,0:T(8,128)S(1)}, f32[2,6,2,8,128]{4,3,2,1,0:T(8,128)S(1)}) custom-call(f32[2,456,8]{2,1,0:T(8,128)S(1)} %bitcast.27, f32[8,256]{1,0:T(8,128)S(1)} %fusion.spread), custom_call_target="tpu_custom_call" | custom-call | flops 1000000 | bytes 1000000 | tf_op jit(solution)/shard_map/pallas_call | solution.py:692
  49.2 2.8 %shard_map.52 = (f32[19,8,8,128]{3,2,1,0:T(8,128)S(1)}, f32[19,8,128]{2,1,0:T(8,128)S(1)}, f32[8,128]{1,0:T(8,128)S(1)}) custom-call(f32[19,12,8,128]{3,2,1,0:T(8,128)S(1)} %constant_dynamic-update-slice_fusion.state), custom_call_target="tpu_custom_call" | custom-call | flops 10000000 | bytes 1000000 | tf_op jit(solution)/shard_map/pallas_call | solution.py:698
  52.0 0.3 shard_map.53
  52.3 0.5 shard_map.54
  52.9 0.8 %collective-permute-start.5 = (f32[112,128]{1,0:T(8,128)S(1)}, f32[112,128]{1,0:T(8,128)S(1)}, u32[]{:S(2)}, u32[]{:S(2)}) collective-permute-start(f32[112,128]{1,0:T(8,128)S(1)} %get-tuple-element.28), channel_id=1, source_target_pairs={{0,8},{8,16},{16,24},{24,0},{1,9},{9,17},{17,25},{25,1},{2,10},{10... | collective-permute-start | bytes 172040 | tf_op jit(solution)/shard_map/ppermute | solution.py:729
  53.6 2.2 %collective-permute-start.6 = (f32[112,128]{1,0:T(8,128)S(1)}, f32[112,128]{1,0:T(8,128)S(1)}, u32[]{:S(2)}, u32[]{:S(2)}) collective-permute-start(f32[112,128]{1,0:T(8,128)S(1)} %get-tuple-element.29), channel_id=1, source_target_pairs={{0,24},{8,0},{16,8},{24,16},{1,25},{9,1},{17,9},{25,17},{2,26},{10... | collective-permute-start | bytes 172040 | tf_op jit(solution)/shard_map/ppermute | solution.py:730
  55.9 2.6 %collective-permute-start.9 = (f32[2,8,128]{2,1,0:T(8,128)S(1)}, f32[2,8,128]{2,1,0:T(8,128)S(1)}, u32[]{:S(2)}, u32[]{:S(2)}) collective-permute-start(f32[2,8,128]{2,1,0:T(8,128)S(1)} %get-tuple-element.32), channel_id=1, source_target_pairs={{0,31},{1,24},{2,25},{3,26},{4,27},{5,28},{6,29},{7,30},{8,7},{9,0... | collective-permute-start | bytes 24584 | tf_op jit(solution)/shard_map/ppermute | solution.py:740
  58.5 2.3 %collective-permute-start.8 = (f32[2,8,128]{2,1,0:T(8,128)S(1)}, f32[2,8,128]{2,1,0:T(8,128)S(1)}, u32[]{:S(2)}, u32[]{:S(2)}) collective-permute-start(f32[2,8,128]{2,1,0:T(8,128)S(1)} %get-tuple-element.32), channel_id=1, source_target_pairs={{0,15},{1,8},{2,9},{3,10},{4,11},{5,12},{6,13},{7,14},{8,23},{9,16... | collective-permute-start | bytes 24584 | tf_op jit(solution)/shard_map/ppermute | solution.py:740
  60.8 0.0 collective-permute-start.7
  60.8 0.5 shard_map.55.inner
  61.3 0.0 collective-permute-done.5.left
  61.3 2.0 %shard_map.56 = f32[1216,128]{1,0:T(8,128)} custom-call(f32[1216,128]{1,0:T(8,128)S(1)} %bitcast.24, f32[112,128]{1,0:T(8,128)S(1)} %collective-permute-done.5.left, f32[112,128]{1,0:T(8,128)S(1)} %collective-permute-done.6.right, f32[19,4,32,128]{3,2,1,0:T(8,128)S(1)} %shard_map.55.inner, f32[2,6,2,24,128]{4,3,2,1,0:T(8,128)S(1)} %get-tuple-element.30.ghosts, ...), custom_call_target="tpu_custom_call" | custom-call | flops 10000000 | bytes 1000000 | tf_op jit(solution)/shard_map/pallas_call | solution.py:742
  63.3 0.0 collective-permute-done.8.high_left
  63.4 0.0 collective-permute-done.7.high
  63.4 1.3 %shard_map.57 = f32[19,8,8,128]{3,2,1,0:T(8,128)} custom-call(f32[112,128]{1,0:T(8,128)S(1)} %collective-permute-done.5.left, f32[112,128]{1,0:T(8,128)S(1)} %collective-permute-done.6.right, f32[2,8,128]{2,1,0:T(8,128)S(1)} %get-tuple-element.27.low, f32[2,8,128]{2,1,0:T(8,128)S(1)} %collective-permute-done.7.high, ...), custom_call_target="tpu_custom_call" | custom-call | flops 1000000 | bytes 1000000 | tf_op jit(solution)/shard_map/pallas_call | solution.py:758
  (19 shorter events, 0.2 us)
Async XLA Ops:
  0.6 7.4 %copy-start.1 = (s32[64]{0:T(128)S(1)}, s32[64]{0:T(128)}, u32[]{:S(2)}) copy-start(s32[64]{0:T(128)} %param.5) | copy-start | bytes 772
  0.6 25.7 %all-to-all-start = ((f32[32,19,2,128]{3,2,1,0:T(2,128)}), f32[32,19,2,128]{3,2,1,0:T(2,128)S(1)}, u32[]{:S(2)}, u32[]{:S(2)}) async-start(f32[32,19,2,128]{3,2,1,0:T(2,128)} %bitcast.28), calls=%async_computation | async-start | bytes 1245184 | tf_op jit(solution)/shard_map/all_to_all | solution.py:666
  26.3 3.6 %copy-start = (f32[19,8,8,128]{3,2,1,0:T(8,128)S(1)}, f32[19,8,8,128]{3,2,1,0:T(8,128)}, u32[]{:S(2)}) copy-start(f32[19,8,8,128]{3,2,1,0:T(8,128)} %param.4) | copy-start | bytes 1867780
  27.3 24.7 %all-to-all-start.1 = ((f32[32,19,2,128]{3,2,1,0:T(2,128)}), f32[32,19,2,128]{3,2,1,0:T(2,128)S(1)}, u32[]{:S(2)}, u32[]{:S(2)}) async-start(f32[32,19,2,128]{3,2,1,0:T(2,128)} %bitcast.5), calls=%async_computation.1 | async-start | bytes 1245184 | tf_op jit(solution)/shard_map/all_to_all | solution.py:683
  30.0 16.9 %collective-permute-start.4 = (f32[19,2,8,128]{3,2,1,0:T(8,128)S(1)}, f32[19,2,8,128]{3,2,1,0:T(8,128)S(1)}, u32[]{:S(2)}, u32[]{:S(2)}) collective-permute-start(f32[19,2,8,128]{3,2,1,0:T(8,128)S(1)} %get-tuple-element.36), channel_id=1, source_target_pairs={{0,24},{8,0},{16,8},{24,16},{1,25},{9,1},{17,9},{25,17},{2,26},{10... | collective-permute-start | bytes 466952 | tf_op jit(solution)/shard_map/ppermute | solution.py:669
  32.6 14.2 %collective-permute-start.3 = (f32[19,2,8,128]{3,2,1,0:T(8,128)S(1)}, f32[19,2,8,128]{3,2,1,0:T(8,128)S(1)}, u32[]{:S(2)}, u32[]{:S(2)}) collective-permute-start(f32[19,2,8,128]{3,2,1,0:T(8,128)S(1)} %get-tuple-element.37), channel_id=1, source_target_pairs={{0,8},{8,16},{16,24},{24,0},{1,9},{9,17},{17,25},{25,1},{2,10},{10... | collective-permute-start | bytes 466952 | tf_op jit(solution)/shard_map/ppermute | solution.py:668
  33.4 13.4 %collective-permute-start.1 = (f32[19,8,8]{0,2,1:T(8,128)S(1)}, f32[19,8,8]{0,2,1:T(8,128)S(1)}, u32[]{:S(2)}, u32[]{:S(2)}) collective-permute-start(f32[19,8,8]{0,2,1:T(8,128)S(1)} %bitcast.31), channel_id=1, source_target_pairs={{0,1},{1,2},{2,3},{3,4},{4,5},{5,6},{6,7},{7,0},{8,9},{9,10},{10,1... | collective-permute-start | bytes 14600 | tf_op jit(solution)/shard_map/ppermute | solution.py:673
  33.4 13.4 %collective-permute-start = (f32[19,2,8]{0,2,1:T(8,128)S(1)}, f32[19,2,8]{0,2,1:T(8,128)S(1)}, u32[]{:S(2)}, u32[]{:S(2)}) collective-permute-start(f32[19,2,8]{0,2,1:T(8,128)S(1)} %get-tuple-element.38), channel_id=1, source_target_pairs={{0,9},{1,10},{2,11},{3,12},{4,13},{5,14},{6,15},{7,8},{8,17},{9,18... | collective-permute-start | bytes 3656 | tf_op jit(solution)/shard_map/ppermute | solution.py:673
  36.7 10.2 %collective-permute-start.2 = (f32[19,2,8]{0,2,1:T(8,128)S(1)}, f32[19,2,8]{0,2,1:T(8,128)S(1)}, u32[]{:S(2)}, u32[]{:S(2)}) collective-permute-start(f32[19,2,8]{0,2,1:T(8,128)S(1)} %get-tuple-element.39), channel_id=1, source_target_pairs={{0,25},{1,26},{2,27},{3,28},{4,29},{5,30},{6,31},{7,24},{8,1},{9,2... | collective-permute-start | bytes 3656 | tf_op jit(solution)/shard_map/ppermute | solution.py:673
  52.9 8.4 %collective-permute-start.5 = (f32[112,128]{1,0:T(8,128)S(1)}, f32[112,128]{1,0:T(8,128)S(1)}, u32[]{:S(2)}, u32[]{:S(2)}) collective-permute-start(f32[112,128]{1,0:T(8,128)S(1)} %get-tuple-element.28), channel_id=1, source_target_pairs={{0,8},{8,16},{16,24},{24,0},{1,9},{9,17},{17,25},{25,1},{2,10},{10... | collective-permute-start | bytes 172040 | tf_op jit(solution)/shard_map/ppermute | solution.py:729
  53.6 7.7 %collective-permute-start.6 = (f32[112,128]{1,0:T(8,128)S(1)}, f32[112,128]{1,0:T(8,128)S(1)}, u32[]{:S(2)}, u32[]{:S(2)}) collective-permute-start(f32[112,128]{1,0:T(8,128)S(1)} %get-tuple-element.29), channel_id=1, source_target_pairs={{0,24},{8,0},{16,8},{24,16},{1,25},{9,1},{17,9},{25,17},{2,26},{10... | collective-permute-start | bytes 172040 | tf_op jit(solution)/shard_map/ppermute | solution.py:730
  55.9 7.5 %collective-permute-start.9 = (f32[2,8,128]{2,1,0:T(8,128)S(1)}, f32[2,8,128]{2,1,0:T(8,128)S(1)}, u32[]{:S(2)}, u32[]{:S(2)}) collective-permute-start(f32[2,8,128]{2,1,0:T(8,128)S(1)} %get-tuple-element.32), channel_id=1, source_target_pairs={{0,31},{1,24},{2,25},{3,26},{4,27},{5,28},{6,29},{7,30},{8,7},{9,0... | collective-permute-start | bytes 24584 | tf_op jit(solution)/shard_map/ppermute | solution.py:740
  58.5 4.9 %collective-permute-start.8 = (f32[2,8,128]{2,1,0:T(8,128)S(1)}, f32[2,8,128]{2,1,0:T(8,128)S(1)}, u32[]{:S(2)}, u32[]{:S(2)}) collective-permute-start(f32[2,8,128]{2,1,0:T(8,128)S(1)} %get-tuple-element.32), channel_id=1, source_target_pairs={{0,15},{1,8},{2,9},{3,10},{4,11},{5,12},{6,13},{7,14},{8,23},{9,16... | collective-permute-start | bytes 24584 | tf_op jit(solution)/shard_map/ppermute | solution.py:740
  60.8 2.6 %collective-permute-start.7 = (f32[2,8,128]{2,1,0:T(8,128)S(1)}, f32[2,8,128]{2,1,0:T(8,128)S(1)}, u32[]{:S(2)}, u32[]{:S(2)}) collective-permute-start(f32[2,8,128]{2,1,0:T(8,128)S(1)} %get-tuple-element.32), channel_id=1, source_target_pairs={{0,7},{1,0},{2,1},{3,2},{4,3},{5,4},{6,5},{7,6},{8,15},{9,8},{10,9... | collective-permute-start | bytes 24584 | tf_op jit(solution)/shard_map/ppermute | solution.py:740

commit v9 on v8

--- a/solution.py
+++ b/solution.py
@@ -288,7 +288,7 @@
             out[n] = plane
 
 
-def send_body(ch_count, k_count, own, ghosts, low, to_left, to_right, rim, moved, parts):
+def send_body(ch_count, k_count, own, ghosts, to_left, to_right, low, high, rim, moved, parts):
     nq = ch_count * k_count
     per = B * nq
     edge = HALO // 2
@@ -307,6 +307,10 @@
         moved[i, q, pl.ds(PAD + cx, SUB), :] = v
 
     substep(load, store, ghosts, 0, parts, ch_count, k_count, 1)
+
+    @pl.loop(0, 1)
+    def _(_):
+        restrict_body(ch_count, k_count, own, low, high)
 
     for c, out, outer in ((1, to_right, B - 1), (-1, to_left, 0)):
         first = PAD + (SUB - 1 if c > 0 else 0)
@@ -711,21 +715,16 @@
     own = arrived.reshape(total, LANES)[: Q * tiles * k_count]
 
     padded = PAD + fine_rows + PAD
-    low, first = call(
-        functools.partial(restrict_body, ch_count, k_count),
-        [f32(PLANES, SUB, LANES)] * 2,
-        [VMEM],
-    )(own)
-    to_left, to_right = call(
+    to_left, to_right, low, first = call(
         functools.partial(send_body, ch_count, k_count),
-        [f32(sent_rows(nq), LANES)] * 2,
-        [VMEM] * 3,
+        [f32(sent_rows(nq), LANES)] * 2 + [f32(PLANES, SUB, LANES)] * 2,
+        [VMEM] * 2,
         [
             pltpu.VMEM((Q, nq, SUB, LANES), jnp.float32),
             pltpu.VMEM((Q, nq, 3 * PAD, LANES), jnp.float32),
             pltpu.VMEM((10, nq, 3 * PAD, LANES), jnp.float32),
         ],
-    )(own, send_ghosts, low)
+    )(own, send_ghosts)
     left = lax.ppermute(to_right, "grp", ring(n_grp, 1))
     right = lax.ppermute(to_left, "grp", ring(n_grp, -1))
     inner = call(

time: 65 us -> 64.7 us (level)
  no operation moved by 1% of the time
where the time goes in v9:
time: 64.7 us; the launch traced here: 64.4 us
  waiting for transfers between devices  27.6 us (43%)
  starting transfers between devices  24.7 us (38%)
  Pallas kernels  9.29 us (14%)
  local copies, waits for them, and re-layouts  2.06 us (3%)
  between operations  0.85 us (1%)
    all_to_all x1, waiting for transfers between devices, local(): spread = lax.all_to_all(pieces, axes, 0, 0, tiled=True)  18.3 us
    ppermute x3, waiting for transfers between devices, local(): below.append(lax.ppermute(part, axes, slab_pairs(n_grp, n_wide, 1, across)))  9.22 us
    all_to_all x1, starting transfers between devices, local(): spread = lax.all_to_all(pieces, axes, 0, 0, tiled=True)  7.33 us
    ppermute x3, starting transfers between devices, local(): lax.ppermute(first, axes, slab_pairs(n_grp, n_wide, -1, across))  4.92 us
    ppermute x3, starting transfers between devices, local(): below.append(lax.ppermute(part, axes, slab_pairs(n_grp, n_wide, 1, across)))  4.19 us
    pallas_call x1, Pallas kernels, local(): call(functools.partial(coarse_body, planes), [f32(Q, cx, cz, cy), f32(Q,...  2.81 us
    ppermute x1, starting transfers between devices, local(): coarse_right = lax.ppermute(coarse_pop[:, :edge], 'grp', ring(n_grp, -1))  2.62 us
    all_to_all x1, starting transfers between devices, local(): lax.all_to_all(outgoing.reshape(devices, rows, k_count, LANES), axes, 0,...  2.61 us
  transfers between devices with their start and end apart: 12, of which 2 were waited for; matrix products, arithmetic and copies ran while one was open for 3% of the time, Pallas kernels for 10%

profile of v9, /device:TPU:0, one launch (start us, length us, event | category | flops | bytes accessed | tf_op | source)
XLA Modules:
  0.0 64.4 jit_solution(14399371246537672480)
XLA Ops:
  0.6 7.3 %all-to-all-start = ((f32[32,19,2,128]{3,2,1,0:T(2,128)}), f32[32,19,2,128]{3,2,1,0:T(2,128)S(1)}, u32[]{:S(2)}, u32[]{:S(2)}) async-start(f32[32,19,2,128]{3,2,1,0:T(2,128)} %bitcast.27), calls=%async_computation | async-start | bytes 1245184 | tf_op jit(solution)/shard_map/all_to_all | solution.py:670
  8.0 18.3 %all-to-all-done = f32[32,19,2,128]{3,2,1,0:T(2,128)S(1)} async-done(((f32[32,19,2,128]{3,2,1,0:T(2,128)}), f32[32,19,2,128]{3,2,1,0:T(2,128)S(1)}, u32[]{:S(2)}, u32[]{:S(2)}) %all-to-all-start) | async-done | bytes 622624 | tf_op jit(solution)/shard_map/all_to_all | solution.py:670
  26.3 1.0 %shard_map.50 = f32[1216,128]{1,0:T(8,128)} custom-call(s32[1,64]{1,0:T(1,128)S(1)} %fusion.4.target_ref, f32[1216,128]{1,0:T(8,128)S(1)} %bitcast.25), custom_call_target="tpu_custom_call" | custom-call | flops 1000000 | bytes 1245184 | tf_op jit(solution)/shard_map/pallas_call | solution.py:686
  27.3 2.6 %all-to-all-start.1 = ((f32[32,19,2,128]{3,2,1,0:T(2,128)}), f32[32,19,2,128]{3,2,1,0:T(2,128)S(1)}, u32[]{:S(2)}, u32[]{:S(2)}) async-start(f32[32,19,2,128]{3,2,1,0:T(2,128)} %bitcast.5), calls=%async_computation.1 | async-start | bytes 1245184 | tf_op jit(solution)/shard_map/all_to_all | solution.py:687
  30.0 2.6 %collective-permute-start.4 = (f32[19,2,8,128]{3,2,1,0:T(8,128)S(1)}, f32[19,2,8,128]{3,2,1,0:T(8,128)S(1)}, u32[]{:S(2)}, u32[]{:S(2)}) collective-permute-start(f32[19,2,8,128]{3,2,1,0:T(8,128)S(1)} %get-tuple-element.36), channel_id=1, source_target_pairs={{0,24},{8,0},{16,8},{24,16},{1,25},{9,1},{17,9},{25,17},{2,26},{10... | collective-permute-start | bytes 466952 | tf_op jit(solution)/shard_map/ppermute | solution.py:673
  32.6 0.0 collective-permute-start.3
  32.6 0.2 slice.18
  32.9 0.5 copy.11
  33.4 0.0 collective-permute-start.1
  33.4 3.2 %collective-permute-start = (f32[19,2,8]{0,2,1:T(8,128)S(1)}, f32[19,2,8]{0,2,1:T(8,128)S(1)}, u32[]{:S(2)}, u32[]{:S(2)}) collective-permute-start(f32[19,2,8]{0,2,1:T(8,128)S(1)} %get-tuple-element.38), channel_id=1, source_target_pairs={{0,9},{1,10},{2,11},{3,12},{4,13},{5,14},{6,15},{7,8},{8,17},{9,18... | collective-permute-start | bytes 3656 | tf_op jit(solution)/shard_map/ppermute | solution.py:677
  36.7 0.9 %collective-permute-start.2 = (f32[19,2,8]{0,2,1:T(8,128)S(1)}, f32[19,2,8]{0,2,1:T(8,128)S(1)}, u32[]{:S(2)}, u32[]{:S(2)}) collective-permute-start(f32[19,2,8]{0,2,1:T(8,128)S(1)} %get-tuple-element.39), channel_id=1, source_target_pairs={{0,25},{1,26},{2,27},{3,28},{4,29},{5,30},{6,31},{7,24},{8,1},{9,2... | collective-permute-start | bytes 3656 | tf_op jit(solution)/shard_map/ppermute | solution.py:677
  37.6 9.2 %collective-permute-done = f32[19,2,8]{0,2,1:T(8,128)S(1)} collective-permute-done((f32[19,2,8]{0,2,1:T(8,128)S(1)}, f32[19,2,8]{0,2,1:T(8,128)S(1)}, u32[]{:S(2)}, u32[]{:S(2)}) %collective-permute-start) | collective-permute-done | bytes 1248 | tf_op jit(solution)/shard_map/ppermute | solution.py:677
  46.8 0.0 collective-permute-done.2
  46.8 0.0 collective-permute-done.1
  46.8 0.0 collective-permute-done.3
  46.9 0.7 %copy.8 = f32[19,12,8,1]{0,2,3,1:T(8,128)S(1)} copy(f32[19,12,8,1]{3,2,1,0:T(8,128)S(1)} %bitcast.24) | data formatting | bytes 14592 | tf_op jit(solution)/shard_map/slice | solution.py:692
  47.7 0.3 copy.9
  48.0 0.2 broadcast_in_dim.9
  48.2 1.0 %shard_map.51 = (f32[2,6,2,24,128]{4,3,2,1,0:T(8,128)S(1)}, f32[2,6,2,8,128]{4,3,2,1,0:T(8,128)S(1)}, f32[2,6,2,8,128]{4,3,2,1,0:T(8,128)S(1)}) custom-call(f32[2,456,8]{2,1,0:T(8,128)S(1)} %bitcast.26, f32[8,256]{1,0:T(8,128)S(1)} %fusion.spread), custom_call_target="tpu_custom_call" | custom-call | flops 1000000 | bytes 1000000 | tf_op jit(solution)/shard_map/pallas_call | solution.py:696
  49.2 2.8 %shard_map.52 = (f32[19,8,8,128]{3,2,1,0:T(8,128)S(1)}, f32[19,8,128]{2,1,0:T(8,128)S(1)}, f32[8,128]{1,0:T(8,128)S(1)}) custom-call(f32[19,12,8,128]{3,2,1,0:T(8,128)S(1)} %constant_dynamic-update-slice_fusion.state), custom_call_target="tpu_custom_call" | custom-call | flops 10000000 | bytes 1000000 | tf_op jit(solution)/shard_map/pallas_call | solution.py:702
  52.0 0.6 shard_map.53
  52.6 0.8 %collective-permute-start.5 = (f32[112,128]{1,0:T(8,128)S(1)}, f32[112,128]{1,0:T(8,128)S(1)}, u32[]{:S(2)}, u32[]{:S(2)}) collective-permute-start(f32[112,128]{1,0:T(8,128)S(1)} %get-tuple-element.27), channel_id=1, source_target_pairs={{0,8},{8,16},{16,24},{24,0},{1,9},{9,17},{17,25},{25,1},{2,10},{10... | collective-permute-start | bytes 172040 | tf_op jit(solution)/shard_map/ppermute | solution.py:728
  53.4 2.2 %collective-permute-start.6 = (f32[112,128]{1,0:T(8,128)S(1)}, f32[112,128]{1,0:T(8,128)S(1)}, u32[]{:S(2)}, u32[]{:S(2)}) collective-permute-start(f32[112,128]{1,0:T(8,128)S(1)} %get-tuple-element.28), channel_id=1, source_target_pairs={{0,24},{8,0},{16,8},{24,16},{1,25},{9,1},{17,9},{25,17},{2,26},{10... | collective-permute-start | bytes 172040 | tf_op jit(solution)/shard_map/ppermute | solution.py:729
  55.6 2.6 %collective-permute-start.9 = (f32[2,8,128]{2,1,0:T(8,128)S(1)}, f32[2,8,128]{2,1,0:T(8,128)S(1)}, u32[]{:S(2)}, u32[]{:S(2)}) collective-permute-start(f32[2,8,128]{2,1,0:T(8,128)S(1)} %get-tuple-element.32), channel_id=1, source_target_pairs={{0,31},{1,24},{2,25},{3,26},{4,27},{5,28},{6,29},{7,30},{8,7},{9,0... | collective-permute-start | bytes 24584 | tf_op jit(solution)/shard_map/ppermute | solution.py:739
  58.2 2.3 %collective-permute-start.8 = (f32[2,8,128]{2,1,0:T(8,128)S(1)}, f32[2,8,128]{2,1,0:T(8,128)S(1)}, u32[]{:S(2)}, u32[]{:S(2)}) collective-permute-start(f32[2,8,128]{2,1,0:T(8,128)S(1)} %get-tuple-element.32), channel_id=1, source_target_pairs={{0,15},{1,8},{2,9},{3,10},{4,11},{5,12},{6,13},{7,14},{8,23},{9,16... | collective-permute-start | bytes 24584 | tf_op jit(solution)/shard_map/ppermute | solution.py:739
  60.5 0.0 collective-permute-start.7
  60.5 0.5 shard_map.54.inner
  61.1 0.0 collective-permute-done.6.right
  61.1 2.0 %shard_map.55 = f32[1216,128]{1,0:T(8,128)} custom-call(f32[1216,128]{1,0:T(8,128)S(1)} %bitcast.23, f32[112,128]{1,0:T(8,128)S(1)} %collective-permute-done.5.left, f32[112,128]{1,0:T(8,128)S(1)} %collective-permute-done.6.right, f32[19,4,32,128]{3,2,1,0:T(8,128)S(1)} %shard_map.54.inner, f32[2,6,2,24,128]{4,3,2,1,0:T(8,128)S(1)} %get-tuple-element.29.ghosts, ...), custom_call_target="tpu_custom_call" | custom-call | flops 10000000 | bytes 1000000 | tf_op jit(solution)/shard_map/pallas_call | solution.py:741
  63.1 0.0 collective-permute-done.9.high_right
  63.1 0.0 collective-permute-done.7.high
  63.1 1.3 %shard_map.56 = f32[19,8,8,128]{3,2,1,0:T(8,128)} custom-call(f32[112,128]{1,0:T(8,128)S(1)} %collective-permute-done.5.left, f32[112,128]{1,0:T(8,128)S(1)} %collective-permute-done.6.right, f32[2,8,128]{2,1,0:T(8,128)S(1)} %get-tuple-element.31.low, f32[2,8,128]{2,1,0:T(8,128)S(1)} %collective-permute-done.7.high, ...), custom_call_target="tpu_custom_call" | custom-call | flops 1000000 | bytes 1000000 | tf_op jit(solution)/shard_map/pallas_call | solution.py:757
  (18 shorter events, 0.2 us)
Async XLA Ops:
  0.6 7.4 %copy-start.1 = (s32[64]{0:T(128)S(1)}, s32[64]{0:T(128)}, u32[]{:S(2)}) copy-start(s32[64]{0:T(128)} %param.5) | copy-start | bytes 772
  0.6 25.7 %all-to-all-start = ((f32[32,19,2,128]{3,2,1,0:T(2,128)}), f32[32,19,2,128]{3,2,1,0:T(2,128)S(1)}, u32[]{:S(2)}, u32[]{:S(2)}) async-start(f32[32,19,2,128]{3,2,1,0:T(2,128)} %bitcast.27), calls=%async_computation | async-start | bytes 1245184 | tf_op jit(solution)/shard_map/all_to_all | solution.py:670
  26.3 3.6 %copy-start = (f32[19,8,8,128]{3,2,1,0:T(8,128)S(1)}, f32[19,8,8,128]{3,2,1,0:T(8,128)}, u32[]{:S(2)}) copy-start(f32[19,8,8,128]{3,2,1,0:T(8,128)} %param.4) | copy-start | bytes 1867780
  27.3 24.7 %all-to-all-start.1 = ((f32[32,19,2,128]{3,2,1,0:T(2,128)}), f32[32,19,2,128]{3,2,1,0:T(2,128)S(1)}, u32[]{:S(2)}, u32[]{:S(2)}) async-start(f32[32,19,2,128]{3,2,1,0:T(2,128)} %bitcast.5), calls=%async_computation.1 | async-start | bytes 1245184 | tf_op jit(solution)/shard_map/all_to_all | solution.py:687
  30.0 16.9 %collective-permute-start.4 = (f32[19,2,8,128]{3,2,1,0:T(8,128)S(1)}, f32[19,2,8,128]{3,2,1,0:T(8,128)S(1)}, u32[]{:S(2)}, u32[]{:S(2)}) collective-permute-start(f32[19,2,8,128]{3,2,1,0:T(8,128)S(1)} %get-tuple-element.36), channel_id=1, source_target_pairs={{0,24},{8,0},{16,8},{24,16},{1,25},{9,1},{17,9},{25,17},{2,26},{10... | collective-permute-start | bytes 466952 | tf_op jit(solution)/shard_map/ppermute | solution.py:673
  32.6 14.2 %collective-permute-start.3 = (f32[19,2,8,128]{3,2,1,0:T(8,128)S(1)}, f32[19,2,8,128]{3,2,1,0:T(8,128)S(1)}, u32[]{:S(2)}, u32[]{:S(2)}) collective-permute-start(f32[19,2,8,128]{3,2,1,0:T(8,128)S(1)} %get-tuple-element.37), channel_id=1, source_target_pairs={{0,8},{8,16},{16,24},{24,0},{1,9},{9,17},{17,25},{25,1},{2,10},{10... | collective-permute-start | bytes 466952 | tf_op jit(solution)/shard_map/ppermute | solution.py:672
  33.4 13.4 %collective-permute-start.1 = (f32[19,8,8]{0,2,1:T(8,128)S(1)}, f32[19,8,8]{0,2,1:T(8,128)S(1)}, u32[]{:S(2)}, u32[]{:S(2)}) collective-permute-start(f32[19,8,8]{0,2,1:T(8,128)S(1)} %bitcast.30), channel_id=1, source_target_pairs={{0,1},{1,2},{2,3},{3,4},{4,5},{5,6},{6,7},{7,0},{8,9},{9,10},{10,1... | collective-permute-start | bytes 14600 | tf_op jit(solution)/shard_map/ppermute | solution.py:677
  33.4 13.4 %collective-permute-start = (f32[19,2,8]{0,2,1:T(8,128)S(1)}, f32[19,2,8]{0,2,1:T(8,128)S(1)}, u32[]{:S(2)}, u32[]{:S(2)}) collective-permute-start(f32[19,2,8]{0,2,1:T(8,128)S(1)} %get-tuple-element.38), channel_id=1, source_target_pairs={{0,9},{1,10},{2,11},{3,12},{4,13},{5,14},{6,15},{7,8},{8,17},{9,18... | collective-permute-start | bytes 3656 | tf_op jit(solution)/shard_map/ppermute | solution.py:677
  36.7 10.2 %collective-permute-start.2 = (f32[19,2,8]{0,2,1:T(8,128)S(1)}, f32[19,2,8]{0,2,1:T(8,128)S(1)}, u32[]{:S(2)}, u32[]{:S(2)}) collective-permute-start(f32[19,2,8]{0,2,1:T(8,128)S(1)} %get-tuple-element.39), channel_id=1, source_target_pairs={{0,25},{1,26},{2,27},{3,28},{4,29},{5,30},{6,31},{7,24},{8,1},{9,2... | collective-permute-start | bytes 3656 | tf_op jit(solution)/shard_map/ppermute | solution.py:677
  52.6 8.4 %collective-permute-start.5 = (f32[112,128]{1,0:T(8,128)S(1)}, f32[112,128]{1,0:T(8,128)S(1)}, u32[]{:S(2)}, u32[]{:S(2)}) collective-permute-start(f32[112,128]{1,0:T(8,128)S(1)} %get-tuple-element.27), channel_id=1, source_target_pairs={{0,8},{8,16},{16,24},{24,0},{1,9},{9,17},{17,25},{25,1},{2,10},{10... | collective-permute-start | bytes 172040 | tf_op jit(solution)/shard_map/ppermute | solution.py:728
  53.4 7.7 %collective-permute-start.6 = (f32[112,128]{1,0:T(8,128)S(1)}, f32[112,128]{1,0:T(8,128)S(1)}, u32[]{:S(2)}, u32[]{:S(2)}) collective-permute-start(f32[112,128]{1,0:T(8,128)S(1)} %get-tuple-element.28), channel_id=1, source_target_pairs={{0,24},{8,0},{16,8},{24,16},{1,25},{9,1},{17,9},{25,17},{2,26},{10... | collective-permute-start | bytes 172040 | tf_op jit(solution)/shard_map/ppermute | solution.py:729
  55.6 7.5 %collective-permute-start.9 = (f32[2,8,128]{2,1,0:T(8,128)S(1)}, f32[2,8,128]{2,1,0:T(8,128)S(1)}, u32[]{:S(2)}, u32[]{:S(2)}) collective-permute-start(f32[2,8,128]{2,1,0:T(8,128)S(1)} %get-tuple-element.32), channel_id=1, source_target_pairs={{0,31},{1,24},{2,25},{3,26},{4,27},{5,28},{6,29},{7,30},{8,7},{9,0... | collective-permute-start | bytes 24584 | tf_op jit(solution)/shard_map/ppermute | solution.py:739
  58.2 4.9 %collective-permute-start.8 = (f32[2,8,128]{2,1,0:T(8,128)S(1)}, f32[2,8,128]{2,1,0:T(8,128)S(1)}, u32[]{:S(2)}, u32[]{:S(2)}) collective-permute-start(f32[2,8,128]{2,1,0:T(8,128)S(1)} %get-tuple-element.32), channel_id=1, source_target_pairs={{0,15},{1,8},{2,9},{3,10},{4,11},{5,12},{6,13},{7,14},{8,23},{9,16... | collective-permute-start | bytes 24584 | tf_op jit(solution)/shard_map/ppermute | solution.py:739
  60.5 2.6 %collective-permute-start.7 = (f32[2,8,128]{2,1,0:T(8,128)S(1)}, f32[2,8,128]{2,1,0:T(8,128)S(1)}, u32[]{:S(2)}, u32[]{:S(2)}) collective-permute-start(f32[2,8,128]{2,1,0:T(8,128)S(1)} %get-tuple-element.32), channel_id=1, source_target_pairs={{0,7},{1,0},{2,1},{3,2},{4,3},{5,4},{6,5},{7,6},{8,15},{9,8},{10,9... | collective-permute-start | bytes 24584 | tf_op jit(solution)/shard_map/ppermute | solution.py:739

commit v10 on v9

--- a/solution.py
+++ b/solution.py
@@ -199,7 +199,27 @@
                 out.append(jnp.where(edge, rolled[other * k_count + k], rolled[q]))
         return out
 
-    return shift_y, shift_z
+    def shift_both(v, cy, cz, which):
+        edge_y = first_y if cy > 0 else last_y
+        edge_z = first_z if cz > 0 else last_z
+        turn = B * cz
+        moved = []
+        for ch in range(ch_count):
+            for k in range(k_count):
+                q = ch * k_count + k
+                own = pltpu.roll(v[q], (turn + cy) % LANES, 1)
+                if k == (0 if cy > 0 else k_count - 1):
+                    carry = pltpu.roll(ghost(0 if cy > 0 else 1, which, ch), turn % LANES, 1)
+                else:
+                    carry = pltpu.roll(v[q - cy], (turn - cy * (B - 1)) % LANES, 1)
+                moved.append(jnp.where(edge_y, carry, own))
+        return [
+            jnp.where(edge_z, moved[(ch - cz) % ch_count * k_count + k], moved[ch * k_count + k])
+            for ch in range(ch_count)
+            for k in range(k_count)
+        ]
+
+    return shift_y, shift_z, shift_both
 
 
 def substep(load, store, ghosts, start, parts, ch_count, k_count, chunks, density_of=None):
@@ -215,7 +235,7 @@
         if density_of is not None:
             density = [density_of(q, r, density[q]) for q in qs]
         p = [1.0 - jnp.exp(-density[q]) for q in qs]
-        shift_y, shift_z = fine_shifts(ch_count, k_count, ghost)
+        shift_y, shift_z, shift_both = fine_shifts(ch_count, k_count, ghost)
         tx, dy, dz, gy, gz = gradient_parts(p, shift_y, shift_z)
         for q in qs:
             values = (tx[q], dy[q], dz[q], gy[q], gz[q], p[q], density[q], *moved[q][1])
@@ -228,7 +248,7 @@
             place = (UP if side == 0 else DOWN).index(which)
             return ghosts[side, place, ch, pl.ds(start + r, SUB), :]
 
-        shift_y, shift_z = fine_shifts(ch_count, k_count, ghost)
+        shift_y, shift_z, shift_both = fine_shifts(ch_count, k_count, ghost)
         streams = []
         for q in qs:
             low = [parts[n, q, pl.ds(PAD + r - 1, SUB), :] for n in range(3)]
@@ -245,9 +265,11 @@
             for q in qs:
                 _, balance = next(streams[q])
                 post.append(load(i, q, r) * (1.0 - 1.0 / FINE_TAU) + balance)
-            if cy:
+            if cy and cz:
+                post = shift_both(post, cy, cz, i)
+            elif cy:
                 post = shift_y(post, cy, i)
-            if cz:
+            elif cz:
                 post = shift_z(post, cz)
             for q in qs:
                 store(i, q, r, cx, post[q])

time: 64.7 us -> 64.6 us (level)
  no operation moved by 1% of the time
where the time goes in v10:
time: 64.6 us; the launch traced here: 64.3 us
  waiting for transfers between devices  27.6 us (43%)
  starting transfers between devices  24.7 us (38%)
  Pallas kernels  9.14 us (14%)
  local copies, waits for them, and re-layouts  2.06 us (3%)
  between operations  0.85 us (1%)
    all_to_all x1, waiting for transfers between devices, local(): spread = lax.all_to_all(pieces, axes, 0, 0, tiled=True)  18.3 us
    ppermute x3, waiting for transfers between devices, local(): below.append(lax.ppermute(part, axes, slab_pairs(n_grp, n_wide, 1, across)))  9.22 us
    all_to_all x1, starting transfers between devices, local(): spread = lax.all_to_all(pieces, axes, 0, 0, tiled=True)  7.33 us
    ppermute x3, starting transfers between devices, local(): lax.ppermute(first, axes, slab_pairs(n_grp, n_wide, -1, across))  4.92 us
    ppermute x3, starting transfers between devices, local(): below.append(lax.ppermute(part, axes, slab_pairs(n_grp, n_wide, 1, across)))  4.19 us
    pallas_call x1, Pallas kernels, local(): call(functools.partial(coarse_body, planes), [f32(Q, cx, cz, cy), f32(Q,...  2.81 us
    ppermute x1, starting transfers between devices, local(): coarse_right = lax.ppermute(coarse_pop[:, :edge], 'grp', ring(n_grp, -1))  2.62 us
    all_to_all x1, starting transfers between devices, local(): lax.all_to_all(outgoing.reshape(devices, rows, k_count, LANES), axes, 0,...  2.61 us
  transfers between devices with their start and end apart: 12, of which 2 were waited for; matrix products, arithmetic and copies ran while one was open for 3% of the time, Pallas kernels for 10%

profile of v10, /device:TPU:0, one launch (start us, length us, event | category | flops | bytes accessed | tf_op | source)
XLA Modules:
  0.0 64.3 jit_solution(14867378632790728835)
XLA Ops:
  0.6 7.3 %all-to-all-start = ((f32[32,19,2,128]{3,2,1,0:T(2,128)}), f32[32,19,2,128]{3,2,1,0:T(2,128)S(1)}, u32[]{:S(2)}, u32[]{:S(2)}) async-start(f32[32,19,2,128]{3,2,1,0:T(2,128)} %bitcast.27), calls=%async_computation | async-start | bytes 1245184 | tf_op jit(solution)/shard_map/all_to_all | solution.py:692
  8.0 18.3 %all-to-all-done = f32[32,19,2,128]{3,2,1,0:T(2,128)S(1)} async-done(((f32[32,19,2,128]{3,2,1,0:T(2,128)}), f32[32,19,2,128]{3,2,1,0:T(2,128)S(1)}, u32[]{:S(2)}, u32[]{:S(2)}) %all-to-all-start) | async-done | bytes 622624 | tf_op jit(solution)/shard_map/all_to_all | solution.py:692
  26.3 1.0 %shard_map.50 = f32[1216,128]{1,0:T(8,128)} custom-call(s32[1,64]{1,0:T(1,128)S(1)} %fusion.4.target_ref, f32[1216,128]{1,0:T(8,128)S(1)} %bitcast.25), custom_call_target="tpu_custom_call" | custom-call | flops 1000000 | bytes 1245184 | tf_op jit(solution)/shard_map/pallas_call | solution.py:708
  27.3 2.6 %all-to-all-start.1 = ((f32[32,19,2,128]{3,2,1,0:T(2,128)}), f32[32,19,2,128]{3,2,1,0:T(2,128)S(1)}, u32[]{:S(2)}, u32[]{:S(2)}) async-start(f32[32,19,2,128]{3,2,1,0:T(2,128)} %bitcast.5), calls=%async_computation.1 | async-start | bytes 1245184 | tf_op jit(solution)/shard_map/all_to_all | solution.py:709
  30.0 2.6 %collective-permute-start.4 = (f32[19,2,8,128]{3,2,1,0:T(8,128)S(1)}, f32[19,2,8,128]{3,2,1,0:T(8,128)S(1)}, u32[]{:S(2)}, u32[]{:S(2)}) collective-permute-start(f32[19,2,8,128]{3,2,1,0:T(8,128)S(1)} %get-tuple-element.36), channel_id=1, source_target_pairs={{0,24},{8,0},{16,8},{24,16},{1,25},{9,1},{17,9},{25,17},{2,26},{10... | collective-permute-start | bytes 466952 | tf_op jit(solution)/shard_map/ppermute | solution.py:695
  32.6 0.0 collective-permute-start.3
  32.6 0.2 slice.18
  32.9 0.5 copy.11
  33.4 0.0 collective-permute-start.1
  33.4 3.2 %collective-permute-start = (f32[19,2,8]{0,2,1:T(8,128)S(1)}, f32[19,2,8]{0,2,1:T(8,128)S(1)}, u32[]{:S(2)}, u32[]{:S(2)}) collective-permute-start(f32[19,2,8]{0,2,1:T(8,128)S(1)} %get-tuple-element.38), channel_id=1, source_target_pairs={{0,9},{1,10},{2,11},{3,12},{4,13},{5,14},{6,15},{7,8},{8,17},{9,18... | collective-permute-start | bytes 3656 | tf_op jit(solution)/shard_map/ppermute | solution.py:699
  36.7 0.9 %collective-permute-start.2 = (f32[19,2,8]{0,2,1:T(8,128)S(1)}, f32[19,2,8]{0,2,1:T(8,128)S(1)}, u32[]{:S(2)}, u32[]{:S(2)}) collective-permute-start(f32[19,2,8]{0,2,1:T(8,128)S(1)} %get-tuple-element.39), channel_id=1, source_target_pairs={{0,25},{1,26},{2,27},{3,28},{4,29},{5,30},{6,31},{7,24},{8,1},{9,2... | collective-permute-start | bytes 3656 | tf_op jit(solution)/shard_map/ppermute | solution.py:699
  37.6 9.2 %collective-permute-done = f32[19,2,8]{0,2,1:T(8,128)S(1)} collective-permute-done((f32[19,2,8]{0,2,1:T(8,128)S(1)}, f32[19,2,8]{0,2,1:T(8,128)S(1)}, u32[]{:S(2)}, u32[]{:S(2)}) %collective-permute-start) | collective-permute-done | bytes 1248 | tf_op jit(solution)/shard_map/ppermute | solution.py:699
  46.8 0.0 collective-permute-done.2
  46.8 0.0 collective-permute-done.1
  46.8 0.0 collective-permute-done.3
  46.9 0.7 %copy.8 = f32[19,12,8,1]{0,2,3,1:T(8,128)S(1)} copy(f32[19,12,8,1]{3,2,1,0:T(8,128)S(1)} %bitcast.24) | data formatting | bytes 14592 | tf_op jit(solution)/shard_map/slice | solution.py:714
  47.7 0.3 copy.9
  48.0 0.2 broadcast_in_dim.9
  48.2 1.0 %shard_map.51 = (f32[2,6,2,24,128]{4,3,2,1,0:T(8,128)S(1)}, f32[2,6,2,8,128]{4,3,2,1,0:T(8,128)S(1)}, f32[2,6,2,8,128]{4,3,2,1,0:T(8,128)S(1)}) custom-call(f32[2,456,8]{2,1,0:T(8,128)S(1)} %bitcast.26, f32[8,256]{1,0:T(8,128)S(1)} %fusion.spread), custom_call_target="tpu_custom_call" | custom-call | flops 1000000 | bytes 1000000 | tf_op jit(solution)/shard_map/pallas_call | solution.py:718
  49.2 2.8 %shard_map.52 = (f32[19,8,8,128]{3,2,1,0:T(8,128)S(1)}, f32[19,8,128]{2,1,0:T(8,128)S(1)}, f32[8,128]{1,0:T(8,128)S(1)}) custom-call(f32[19,12,8,128]{3,2,1,0:T(8,128)S(1)} %constant_dynamic-update-slice_fusion.state), custom_call_target="tpu_custom_call" | custom-call | flops 10000000 | bytes 1000000 | tf_op jit(solution)/shard_map/pallas_call | solution.py:724
  52.0 0.6 shard_map.53
  52.6 0.8 %collective-permute-start.5 = (f32[112,128]{1,0:T(8,128)S(1)}, f32[112,128]{1,0:T(8,128)S(1)}, u32[]{:S(2)}, u32[]{:S(2)}) collective-permute-start(f32[112,128]{1,0:T(8,128)S(1)} %get-tuple-element.27), channel_id=1, source_target_pairs={{0,8},{8,16},{16,24},{24,0},{1,9},{9,17},{17,25},{25,1},{2,10},{10... | collective-permute-start | bytes 172040 | tf_op jit(solution)/shard_map/ppermute | solution.py:750
  53.3 2.2 %collective-permute-start.6 = (f32[112,128]{1,0:T(8,128)S(1)}, f32[112,128]{1,0:T(8,128)S(1)}, u32[]{:S(2)}, u32[]{:S(2)}) collective-permute-start(f32[112,128]{1,0:T(8,128)S(1)} %get-tuple-element.28), channel_id=1, source_target_pairs={{0,24},{8,0},{16,8},{24,16},{1,25},{9,1},{17,9},{25,17},{2,26},{10... | collective-permute-start | bytes 172040 | tf_op jit(solution)/shard_map/ppermute | solution.py:751
  55.5 2.6 %collective-permute-start.9 = (f32[2,8,128]{2,1,0:T(8,128)S(1)}, f32[2,8,128]{2,1,0:T(8,128)S(1)}, u32[]{:S(2)}, u32[]{:S(2)}) collective-permute-start(f32[2,8,128]{2,1,0:T(8,128)S(1)} %get-tuple-element.32), channel_id=1, source_target_pairs={{0,31},{1,24},{2,25},{3,26},{4,27},{5,28},{6,29},{7,30},{8,7},{9,0... | collective-permute-start | bytes 24584 | tf_op jit(solution)/shard_map/ppermute | solution.py:761
  58.1 2.3 %collective-permute-start.8 = (f32[2,8,128]{2,1,0:T(8,128)S(1)}, f32[2,8,128]{2,1,0:T(8,128)S(1)}, u32[]{:S(2)}, u32[]{:S(2)}) collective-permute-start(f32[2,8,128]{2,1,0:T(8,128)S(1)} %get-tuple-element.32), channel_id=1, source_target_pairs={{0,15},{1,8},{2,9},{3,10},{4,11},{5,12},{6,13},{7,14},{8,23},{9,16... | collective-permute-start | bytes 24584 | tf_op jit(solution)/shard_map/ppermute | solution.py:761
  60.5 0.0 collective-permute-start.7
  60.5 0.5 shard_map.54.inner
  61.0 0.0 collective-permute-done.6.right
  61.0 1.9 %shard_map.55 = f32[1216,128]{1,0:T(8,128)} custom-call(f32[1216,128]{1,0:T(8,128)S(1)} %bitcast.23, f32[112,128]{1,0:T(8,128)S(1)} %collective-permute-done.5.left, f32[112,128]{1,0:T(8,128)S(1)} %collective-permute-done.6.right, f32[19,4,32,128]{3,2,1,0:T(8,128)S(1)} %shard_map.54.inner, f32[2,6,2,24,128]{4,3,2,1,0:T(8,128)S(1)} %get-tuple-element.29.ghosts, ...), custom_call_target="tpu_custom_call" | custom-call | flops 10000000 | bytes 1000000 | tf_op jit(solution)/shard_map/pallas_call | solution.py:763
  62.9 0.0 collective-permute-done.9.high_right
  62.9 0.0 collective-permute-done.8.high_left
  63.0 1.3 %shard_map.56 = f32[19,8,8,128]{3,2,1,0:T(8,128)} custom-call(f32[112,128]{1,0:T(8,128)S(1)} %collective-permute-done.5.left, f32[112,128]{1,0:T(8,128)S(1)} %collective-permute-done.6.right, f32[2,8,128]{2,1,0:T(8,128)S(1)} %get-tuple-element.31.low, f32[2,8,128]{2,1,0:T(8,128)S(1)} %collective-permute-done.7.high, ...), custom_call_target="tpu_custom_call" | custom-call | flops 1000000 | bytes 1000000 | tf_op jit(solution)/shard_map/pallas_call | solution.py:779
  (18 shorter events, 0.2 us)
Async XLA Ops:
  0.6 7.4 %copy-start.1 = (s32[64]{0:T(128)S(1)}, s32[64]{0:T(128)}, u32[]{:S(2)}) copy-start(s32[64]{0:T(128)} %param.5) | copy-start | bytes 772
  0.6 25.7 %all-to-all-start = ((f32[32,19,2,128]{3,2,1,0:T(2,128)}), f32[32,19,2,128]{3,2,1,0:T(2,128)S(1)}, u32[]{:S(2)}, u32[]{:S(2)}) async-start(f32[32,19,2,128]{3,2,1,0:T(2,128)} %bitcast.27), calls=%async_computation | async-start | bytes 1245184 | tf_op jit(solution)/shard_map/all_to_all | solution.py:692
  26.3 3.6 %copy-start = (f32[19,8,8,128]{3,2,1,0:T(8,128)S(1)}, f32[19,8,8,128]{3,2,1,0:T(8,128)}, u32[]{:S(2)}) copy-start(f32[19,8,8,128]{3,2,1,0:T(8,128)} %param.4) | copy-start | bytes 1867780
  27.3 24.7 %all-to-all-start.1 = ((f32[32,19,2,128]{3,2,1,0:T(2,128)}), f32[32,19,2,128]{3,2,1,0:T(2,128)S(1)}, u32[]{:S(2)}, u32[]{:S(2)}) async-start(f32[32,19,2,128]{3,2,1,0:T(2,128)} %bitcast.5), calls=%async_computation.1 | async-start | bytes 1245184 | tf_op jit(solution)/shard_map/all_to_all | solution.py:709
  30.0 16.9 %collective-permute-start.4 = (f32[19,2,8,128]{3,2,1,0:T(8,128)S(1)}, f32[19,2,8,128]{3,2,1,0:T(8,128)S(1)}, u32[]{:S(2)}, u32[]{:S(2)}) collective-permute-start(f32[19,2,8,128]{3,2,1,0:T(8,128)S(1)} %get-tuple-element.36), channel_id=1, source_target_pairs={{0,24},{8,0},{16,8},{24,16},{1,25},{9,1},{17,9},{25,17},{2,26},{10... | collective-permute-start | bytes 466952 | tf_op jit(solution)/shard_map/ppermute | solution.py:695
  32.6 14.2 %collective-permute-start.3 = (f32[19,2,8,128]{3,2,1,0:T(8,128)S(1)}, f32[19,2,8,128]{3,2,1,0:T(8,128)S(1)}, u32[]{:S(2)}, u32[]{:S(2)}) collective-permute-start(f32[19,2,8,128]{3,2,1,0:T(8,128)S(1)} %get-tuple-element.37), channel_id=1, source_target_pairs={{0,8},{8,16},{16,24},{24,0},{1,9},{9,17},{17,25},{25,1},{2,10},{10... | collective-permute-start | bytes 466952 | tf_op jit(solution)/shard_map/ppermute | solution.py:694
  33.4 13.4 %collective-permute-start.1 = (f32[19,8,8]{0,2,1:T(8,128)S(1)}, f32[19,8,8]{0,2,1:T(8,128)S(1)}, u32[]{:S(2)}, u32[]{:S(2)}) collective-permute-start(f32[19,8,8]{0,2,1:T(8,128)S(1)} %bitcast.30), channel_id=1, source_target_pairs={{0,1},{1,2},{2,3},{3,4},{4,5},{5,6},{6,7},{7,0},{8,9},{9,10},{10,1... | collective-permute-start | bytes 14600 | tf_op jit(solution)/shard_map/ppermute | solution.py:699
  33.4 13.4 %collective-permute-start = (f32[19,2,8]{0,2,1:T(8,128)S(1)}, f32[19,2,8]{0,2,1:T(8,128)S(1)}, u32[]{:S(2)}, u32[]{:S(2)}) collective-permute-start(f32[19,2,8]{0,2,1:T(8,128)S(1)} %get-tuple-element.38), channel_id=1, source_target_pairs={{0,9},{1,10},{2,11},{3,12},{4,13},{5,14},{6,15},{7,8},{8,17},{9,18... | collective-permute-start | bytes 3656 | tf_op jit(solution)/shard_map/ppermute | solution.py:699
  36.7 10.2 %collective-permute-start.2 = (f32[19,2,8]{0,2,1:T(8,128)S(1)}, f32[19,2,8]{0,2,1:T(8,128)S(1)}, u32[]{:S(2)}, u32[]{:S(2)}) collective-permute-start(f32[19,2,8]{0,2,1:T(8,128)S(1)} %get-tuple-element.39), channel_id=1, source_target_pairs={{0,25},{1,26},{2,27},{3,28},{4,29},{5,30},{6,31},{7,24},{8,1},{9,2... | collective-permute-start | bytes 3656 | tf_op jit(solution)/shard_map/ppermute | solution.py:699
  52.6 8.4 %collective-permute-start.5 = (f32[112,128]{1,0:T(8,128)S(1)}, f32[112,128]{1,0:T(8,128)S(1)}, u32[]{:S(2)}, u32[]{:S(2)}) collective-permute-start(f32[112,128]{1,0:T(8,128)S(1)} %get-tuple-element.27), channel_id=1, source_target_pairs={{0,8},{8,16},{16,24},{24,0},{1,9},{9,17},{17,25},{25,1},{2,10},{10... | collective-permute-start | bytes 172040 | tf_op jit(solution)/shard_map/ppermute | solution.py:750
  53.3 7.7 %collective-permute-start.6 = (f32[112,128]{1,0:T(8,128)S(1)}, f32[112,128]{1,0:T(8,128)S(1)}, u32[]{:S(2)}, u32[]{:S(2)}) collective-permute-start(f32[112,128]{1,0:T(8,128)S(1)} %get-tuple-element.28), channel_id=1, source_target_pairs={{0,24},{8,0},{16,8},{24,16},{1,25},{9,1},{17,9},{25,17},{2,26},{10... | collective-permute-start | bytes 172040 | tf_op jit(solution)/shard_map/ppermute | solution.py:751
  55.5 7.4 %collective-permute-start.9 = (f32[2,8,128]{2,1,0:T(8,128)S(1)}, f32[2,8,128]{2,1,0:T(8,128)S(1)}, u32[]{:S(2)}, u32[]{:S(2)}) collective-permute-start(f32[2,8,128]{2,1,0:T(8,128)S(1)} %get-tuple-element.32), channel_id=1, source_target_pairs={{0,31},{1,24},{2,25},{3,26},{4,27},{5,28},{6,29},{7,30},{8,7},{9,0... | collective-permute-start | bytes 24584 | tf_op jit(solution)/shard_map/ppermute | solution.py:761
  58.1 4.8 %collective-permute-start.8 = (f32[2,8,128]{2,1,0:T(8,128)S(1)}, f32[2,8,128]{2,1,0:T(8,128)S(1)}, u32[]{:S(2)}, u32[]{:S(2)}) collective-permute-start(f32[2,8,128]{2,1,0:T(8,128)S(1)} %get-tuple-element.32), channel_id=1, source_target_pairs={{0,15},{1,8},{2,9},{3,10},{4,11},{5,12},{6,13},{7,14},{8,23},{9,16... | collective-permute-start | bytes 24584 | tf_op jit(solution)/shard_map/ppermute | solution.py:761
  60.5 2.5 %collective-permute-start.7 = (f32[2,8,128]{2,1,0:T(8,128)S(1)}, f32[2,8,128]{2,1,0:T(8,128)S(1)}, u32[]{:S(2)}, u32[]{:S(2)}) collective-permute-start(f32[2,8,128]{2,1,0:T(8,128)S(1)} %get-tuple-element.32), channel_id=1, source_target_pairs={{0,7},{1,0},{2,1},{3,2},{4,3},{5,4},{6,5},{7,6},{8,15},{9,8},{10,9... | collective-permute-start | bytes 24584 | tf_op jit(solution)/shard_map/ppermute | solution.py:761

commit v11 on v10

--- a/solution.py
+++ b/solution.py
@@ -15,7 +15,7 @@
 HALO = 4
 PAD = 8
 GRANT = 24 << 20
-PIECES = 8
+PIECES = 4
 
 VELOCITIES = (
     (0, 0, 0),
@@ -209,7 +209,7 @@
                 q = ch * k_count + k
                 own = pltpu.roll(v[q], (turn + cy) % LANES, 1)
                 if k == (0 if cy > 0 else k_count - 1):
-                    carry = pltpu.roll(ghost(0 if cy > 0 else 1, which, ch), turn % LANES, 1)
+                    carry = ghost(0 if cy > 0 else 1, which, ch)
                 else:
                     carry = pltpu.roll(v[q - cy], (turn - cy * (B - 1)) % LANES, 1)
                 moved.append(jnp.where(edge_y, carry, own))
@@ -462,7 +462,10 @@
                 ]
                 potential, found = rescaled(f, TO_FINE, wanted)
                 for n, i in enumerate(wanted):
-                    out[side, n, ch, pl.ds(r, SUB), :] = found[i]
+                    v, cz = found[i], VELOCITIES[i][2]
+                    if cz:
+                        v = pltpu.roll(v, B * cz % LANES, 1)
+                    out[side, n, ch, pl.ds(r, SUB), :] = v
                 out[side, NG - 1, ch, pl.ds(r, SUB), :] = potential
             for n in range(NG):
                 for ref, lower, upper in (

time: 64.6 us -> 64.6 us (level)
  no operation moved by 1% of the time
where the time goes in v11:
time: 64.6 us; the launch traced here: 64.3 us
  waiting for transfers between devices  27.6 us (43%)
  starting transfers between devices  24.7 us (38%)
  Pallas kernels  9.15 us (14%)
  local copies, waits for them, and re-layouts  2.06 us (3%)
  between operations  0.85 us (1%)
    all_to_all x1, waiting for transfers between devices, local(): spread = lax.all_to_all(pieces, axes, 0, 0, tiled=True)  18.3 us
    ppermute x3, waiting for transfers between devices, local(): below.append(lax.ppermute(part, axes, slab_pairs(n_grp, n_wide, 1, across)))  9.22 us
    all_to_all x1, starting transfers between devices, local(): spread = lax.all_to_all(pieces, axes, 0, 0, tiled=True)  7.33 us
    ppermute x3, starting transfers between devices, local(): lax.ppermute(first, axes, slab_pairs(n_grp, n_wide, -1, across))  4.92 us
    ppermute x3, starting transfers between devices, local(): below.append(lax.ppermute(part, axes, slab_pairs(n_grp, n_wide, 1, across)))  4.19 us
    pallas_call x1, Pallas kernels, local(): call(functools.partial(coarse_body, planes), [f32(Q, cx, cz, cy), f32(Q,...  2.81 us
    ppermute x1, starting transfers between devices, local(): coarse_right = lax.ppermute(coarse_pop[:, :edge], 'grp', ring(n_grp, -1))  2.62 us
    all_to_all x1, starting transfers between devices, local(): lax.all_to_all(outgoing.reshape(devices, rows, k_count, LANES), axes, 0,...  2.61 us
  transfers between devices with their start and end apart: 12, of which 2 were waited for; matrix products, arithmetic and copies ran while one was open for 3% of the time, Pallas kernels for 10%

profile of v11, /device:TPU:0, one launch (start us, length us, event | category | flops | bytes accessed | tf_op | source)
XLA Modules:
  0.0 64.3 jit_solution(8043954040108026316)
XLA Ops:
  0.6 7.3 %all-to-all-start = ((f32[32,19,2,128]{3,2,1,0:T(2,128)}), f32[32,19,2,128]{3,2,1,0:T(2,128)S(1)}, u32[]{:S(2)}, u32[]{:S(2)}) async-start(f32[32,19,2,128]{3,2,1,0:T(2,128)} %bitcast.27), calls=%async_computation | async-start | bytes 1245184 | tf_op jit(solution)/shard_map/all_to_all | solution.py:695
  8.0 18.3 %all-to-all-done = f32[32,19,2,128]{3,2,1,0:T(2,128)S(1)} async-done(((f32[32,19,2,128]{3,2,1,0:T(2,128)}), f32[32,19,2,128]{3,2,1,0:T(2,128)S(1)}, u32[]{:S(2)}, u32[]{:S(2)}) %all-to-all-start) | async-done | bytes 622624 | tf_op jit(solution)/shard_map/all_to_all | solution.py:695
  26.3 1.0 %shard_map.50 = f32[1216,128]{1,0:T(8,128)} custom-call(s32[1,64]{1,0:T(1,128)S(1)} %fusion.4.target_ref, f32[1216,128]{1,0:T(8,128)S(1)} %bitcast.25), custom_call_target="tpu_custom_call" | custom-call | flops 1000000 | bytes 1245184 | tf_op jit(solution)/shard_map/pallas_call | solution.py:711
  27.3 2.6 %all-to-all-start.1 = ((f32[32,19,2,128]{3,2,1,0:T(2,128)}), f32[32,19,2,128]{3,2,1,0:T(2,128)S(1)}, u32[]{:S(2)}, u32[]{:S(2)}) async-start(f32[32,19,2,128]{3,2,1,0:T(2,128)} %bitcast.5), calls=%async_computation.1 | async-start | bytes 1245184 | tf_op jit(solution)/shard_map/all_to_all | solution.py:712
  30.0 2.6 %collective-permute-start.4 = (f32[19,2,8,128]{3,2,1,0:T(8,128)S(1)}, f32[19,2,8,128]{3,2,1,0:T(8,128)S(1)}, u32[]{:S(2)}, u32[]{:S(2)}) collective-permute-start(f32[19,2,8,128]{3,2,1,0:T(8,128)S(1)} %get-tuple-element.36), channel_id=1, source_target_pairs={{0,24},{8,0},{16,8},{24,16},{1,25},{9,1},{17,9},{25,17},{2,26},{10... | collective-permute-start | bytes 466952 | tf_op jit(solution)/shard_map/ppermute | solution.py:698
  32.6 0.0 collective-permute-start.3
  32.6 0.2 slice.18
  32.9 0.5 copy.11
  33.4 0.0 collective-permute-start.1
  33.4 3.2 %collective-permute-start = (f32[19,2,8]{0,2,1:T(8,128)S(1)}, f32[19,2,8]{0,2,1:T(8,128)S(1)}, u32[]{:S(2)}, u32[]{:S(2)}) collective-permute-start(f32[19,2,8]{0,2,1:T(8,128)S(1)} %get-tuple-element.38), channel_id=1, source_target_pairs={{0,9},{1,10},{2,11},{3,12},{4,13},{5,14},{6,15},{7,8},{8,17},{9,18... | collective-permute-start | bytes 3656 | tf_op jit(solution)/shard_map/ppermute | solution.py:702
  36.7 0.9 %collective-permute-start.2 = (f32[19,2,8]{0,2,1:T(8,128)S(1)}, f32[19,2,8]{0,2,1:T(8,128)S(1)}, u32[]{:S(2)}, u32[]{:S(2)}) collective-permute-start(f32[19,2,8]{0,2,1:T(8,128)S(1)} %get-tuple-element.39), channel_id=1, source_target_pairs={{0,25},{1,26},{2,27},{3,28},{4,29},{5,30},{6,31},{7,24},{8,1},{9,2... | collective-permute-start | bytes 3656 | tf_op jit(solution)/shard_map/ppermute | solution.py:702
  37.6 9.2 %collective-permute-done = f32[19,2,8]{0,2,1:T(8,128)S(1)} collective-permute-done((f32[19,2,8]{0,2,1:T(8,128)S(1)}, f32[19,2,8]{0,2,1:T(8,128)S(1)}, u32[]{:S(2)}, u32[]{:S(2)}) %collective-permute-start) | collective-permute-done | bytes 1248 | tf_op jit(solution)/shard_map/ppermute | solution.py:702
  46.8 0.0 collective-permute-done.2
  46.8 0.0 collective-permute-done.1
  46.9 0.7 %copy.8 = f32[19,12,8,1]{0,2,3,1:T(8,128)S(1)} copy(f32[19,12,8,1]{3,2,1,0:T(8,128)S(1)} %bitcast.24) | data formatting | bytes 14592 | tf_op jit(solution)/shard_map/slice | solution.py:717
  47.7 0.3 copy.9
  48.0 0.2 broadcast_in_dim.9
  48.2 1.1 %shard_map.51 = (f32[2,6,2,24,128]{4,3,2,1,0:T(8,128)S(1)}, f32[2,6,2,8,128]{4,3,2,1,0:T(8,128)S(1)}, f32[2,6,2,8,128]{4,3,2,1,0:T(8,128)S(1)}) custom-call(f32[2,456,8]{2,1,0:T(8,128)S(1)} %bitcast.26, f32[8,256]{1,0:T(8,128)S(1)} %fusion.spread), custom_call_target="tpu_custom_call" | custom-call | flops 1000000 | bytes 1000000 | tf_op jit(solution)/shard_map/pallas_call | solution.py:721
  49.3 2.8 %shard_map.52 = (f32[19,8,8,128]{3,2,1,0:T(8,128)S(1)}, f32[19,8,128]{2,1,0:T(8,128)S(1)}, f32[8,128]{1,0:T(8,128)S(1)}) custom-call(f32[19,12,8,128]{3,2,1,0:T(8,128)S(1)} %constant_dynamic-update-slice_fusion.state), custom_call_target="tpu_custom_call" | custom-call | flops 10000000 | bytes 1000000 | tf_op jit(solution)/shard_map/pallas_call | solution.py:727
  52.1 0.0 all-to-all-done.1
  52.1 0.5 shard_map.53
  52.6 0.8 %collective-permute-start.5 = (f32[112,128]{1,0:T(8,128)S(1)}, f32[112,128]{1,0:T(8,128)S(1)}, u32[]{:S(2)}, u32[]{:S(2)}) collective-permute-start(f32[112,128]{1,0:T(8,128)S(1)} %get-tuple-element.27), channel_id=1, source_target_pairs={{0,8},{8,16},{16,24},{24,0},{1,9},{9,17},{17,25},{25,1},{2,10},{10... | collective-permute-start | bytes 172040 | tf_op jit(solution)/shard_map/ppermute | solution.py:753
  53.4 2.2 %collective-permute-start.6 = (f32[112,128]{1,0:T(8,128)S(1)}, f32[112,128]{1,0:T(8,128)S(1)}, u32[]{:S(2)}, u32[]{:S(2)}) collective-permute-start(f32[112,128]{1,0:T(8,128)S(1)} %get-tuple-element.28), channel_id=1, source_target_pairs={{0,24},{8,0},{16,8},{24,16},{1,25},{9,1},{17,9},{25,17},{2,26},{10... | collective-permute-start | bytes 172040 | tf_op jit(solution)/shard_map/ppermute | solution.py:754
  55.6 2.6 %collective-permute-start.9 = (f32[2,8,128]{2,1,0:T(8,128)S(1)}, f32[2,8,128]{2,1,0:T(8,128)S(1)}, u32[]{:S(2)}, u32[]{:S(2)}) collective-permute-start(f32[2,8,128]{2,1,0:T(8,128)S(1)} %get-tuple-element.32), channel_id=1, source_target_pairs={{0,31},{1,24},{2,25},{3,26},{4,27},{5,28},{6,29},{7,30},{8,7},{9,0... | collective-permute-start | bytes 24584 | tf_op jit(solution)/shard_map/ppermute | solution.py:764
  58.2 2.3 %collective-permute-start.8 = (f32[2,8,128]{2,1,0:T(8,128)S(1)}, f32[2,8,128]{2,1,0:T(8,128)S(1)}, u32[]{:S(2)}, u32[]{:S(2)}) collective-permute-start(f32[2,8,128]{2,1,0:T(8,128)S(1)} %get-tuple-element.32), channel_id=1, source_target_pairs={{0,15},{1,8},{2,9},{3,10},{4,11},{5,12},{6,13},{7,14},{8,23},{9,16... | collective-permute-start | bytes 24584 | tf_op jit(solution)/shard_map/ppermute | solution.py:764
  60.5 0.0 collective-permute-start.7
  60.5 0.5 shard_map.54.inner
  61.0 0.0 collective-permute-done.6.right
  61.0 1.9 %shard_map.55 = f32[1216,128]{1,0:T(8,128)} custom-call(f32[1216,128]{1,0:T(8,128)S(1)} %bitcast.23, f32[112,128]{1,0:T(8,128)S(1)} %collective-permute-done.5.left, f32[112,128]{1,0:T(8,128)S(1)} %collective-permute-done.6.right, f32[19,4,32,128]{3,2,1,0:T(8,128)S(1)} %shard_map.54.inner, f32[2,6,2,24,128]{4,3,2,1,0:T(8,128)S(1)} %get-tuple-element.29.ghosts, ...), custom_call_target="tpu_custom_call" | custom-call | flops 10000000 | bytes 1000000 | tf_op jit(solution)/shard_map/pallas_call | solution.py:766
  62.9 0.0 collective-permute-done.9.high_right
  63.0 0.0 collective-permute-done.7.high
  63.0 1.3 %shard_map.56 = f32[19,8,8,128]{3,2,1,0:T(8,128)} custom-call(f32[112,128]{1,0:T(8,128)S(1)} %collective-permute-done.5.left, f32[112,128]{1,0:T(8,128)S(1)} %collective-permute-done.6.right, f32[2,8,128]{2,1,0:T(8,128)S(1)} %get-tuple-element.31.low, f32[2,8,128]{2,1,0:T(8,128)S(1)} %collective-permute-done.7.high, ...), custom_call_target="tpu_custom_call" | custom-call | flops 1000000 | bytes 1000000 | tf_op jit(solution)/shard_map/pallas_call | solution.py:782
  (18 shorter events, 0.2 us)
Async XLA Ops:
  0.6 7.4 %copy-start.1 = (s32[64]{0:T(128)S(1)}, s32[64]{0:T(128)}, u32[]{:S(2)}) copy-start(s32[64]{0:T(128)} %param.5) | copy-start | bytes 772
  0.6 25.7 %all-to-all-start = ((f32[32,19,2,128]{3,2,1,0:T(2,128)}), f32[32,19,2,128]{3,2,1,0:T(2,128)S(1)}, u32[]{:S(2)}, u32[]{:S(2)}) async-start(f32[32,19,2,128]{3,2,1,0:T(2,128)} %bitcast.27), calls=%async_computation | async-start | bytes 1245184 | tf_op jit(solution)/shard_map/all_to_all | solution.py:695
  26.3 3.6 %copy-start = (f32[19,8,8,128]{3,2,1,0:T(8,128)S(1)}, f32[19,8,8,128]{3,2,1,0:T(8,128)}, u32[]{:S(2)}) copy-start(f32[19,8,8,128]{3,2,1,0:T(8,128)} %param.4) | copy-start | bytes 1867780
  27.3 24.7 %all-to-all-start.1 = ((f32[32,19,2,128]{3,2,1,0:T(2,128)}), f32[32,19,2,128]{3,2,1,0:T(2,128)S(1)}, u32[]{:S(2)}, u32[]{:S(2)}) async-start(f32[32,19,2,128]{3,2,1,0:T(2,128)} %bitcast.5), calls=%async_computation.1 | async-start | bytes 1245184 | tf_op jit(solution)/shard_map/all_to_all | solution.py:712
  30.0 16.9 %collective-permute-start.4 = (f32[19,2,8,128]{3,2,1,0:T(8,128)S(1)}, f32[19,2,8,128]{3,2,1,0:T(8,128)S(1)}, u32[]{:S(2)}, u32[]{:S(2)}) collective-permute-start(f32[19,2,8,128]{3,2,1,0:T(8,128)S(1)} %get-tuple-element.36), channel_id=1, source_target_pairs={{0,24},{8,0},{16,8},{24,16},{1,25},{9,1},{17,9},{25,17},{2,26},{10... | collective-permute-start | bytes 466952 | tf_op jit(solution)/shard_map/ppermute | solution.py:698
  32.6 14.2 %collective-permute-start.3 = (f32[19,2,8,128]{3,2,1,0:T(8,128)S(1)}, f32[19,2,8,128]{3,2,1,0:T(8,128)S(1)}, u32[]{:S(2)}, u32[]{:S(2)}) collective-permute-start(f32[19,2,8,128]{3,2,1,0:T(8,128)S(1)} %get-tuple-element.37), channel_id=1, source_target_pairs={{0,8},{8,16},{16,24},{24,0},{1,9},{9,17},{17,25},{25,1},{2,10},{10... | collective-permute-start | bytes 466952 | tf_op jit(solution)/shard_map/ppermute | solution.py:697
  33.4 13.4 %collective-permute-start.1 = (f32[19,8,8]{0,2,1:T(8,128)S(1)}, f32[19,8,8]{0,2,1:T(8,128)S(1)}, u32[]{:S(2)}, u32[]{:S(2)}) collective-permute-start(f32[19,8,8]{0,2,1:T(8,128)S(1)} %bitcast.30), channel_id=1, source_target_pairs={{0,1},{1,2},{2,3},{3,4},{4,5},{5,6},{6,7},{7,0},{8,9},{9,10},{10,1... | collective-permute-start | bytes 14600 | tf_op jit(solution)/shard_map/ppermute | solution.py:702
  33.4 13.4 %collective-permute-start = (f32[19,2,8]{0,2,1:T(8,128)S(1)}, f32[19,2,8]{0,2,1:T(8,128)S(1)}, u32[]{:S(2)}, u32[]{:S(2)}) collective-permute-start(f32[19,2,8]{0,2,1:T(8,128)S(1)} %get-tuple-element.38), channel_id=1, source_target_pairs={{0,9},{1,10},{2,11},{3,12},{4,13},{5,14},{6,15},{7,8},{8,17},{9,18... | collective-permute-start | bytes 3656 | tf_op jit(solution)/shard_map/ppermute | solution.py:702
  36.7 10.2 %collective-permute-start.2 = (f32[19,2,8]{0,2,1:T(8,128)S(1)}, f32[19,2,8]{0,2,1:T(8,128)S(1)}, u32[]{:S(2)}, u32[]{:S(2)}) collective-permute-start(f32[19,2,8]{0,2,1:T(8,128)S(1)} %get-tuple-element.39), channel_id=1, source_target_pairs={{0,25},{1,26},{2,27},{3,28},{4,29},{5,30},{6,31},{7,24},{8,1},{9,2... | collective-permute-start | bytes 3656 | tf_op jit(solution)/shard_map/ppermute | solution.py:702
  52.6 8.4 %collective-permute-start.5 = (f32[112,128]{1,0:T(8,128)S(1)}, f32[112,128]{1,0:T(8,128)S(1)}, u32[]{:S(2)}, u32[]{:S(2)}) collective-permute-start(f32[112,128]{1,0:T(8,128)S(1)} %get-tuple-element.27), channel_id=1, source_target_pairs={{0,8},{8,16},{16,24},{24,0},{1,9},{9,17},{17,25},{25,1},{2,10},{10... | collective-permute-start | bytes 172040 | tf_op jit(solution)/shard_map/ppermute | solution.py:753
  53.4 7.6 %collective-permute-start.6 = (f32[112,128]{1,0:T(8,128)S(1)}, f32[112,128]{1,0:T(8,128)S(1)}, u32[]{:S(2)}, u32[]{:S(2)}) collective-permute-start(f32[112,128]{1,0:T(8,128)S(1)} %get-tuple-element.28), channel_id=1, source_target_pairs={{0,24},{8,0},{16,8},{24,16},{1,25},{9,1},{17,9},{25,17},{2,26},{10... | collective-permute-start | bytes 172040 | tf_op jit(solution)/shard_map/ppermute | solution.py:754
  55.6 7.3 %collective-permute-start.9 = (f32[2,8,128]{2,1,0:T(8,128)S(1)}, f32[2,8,128]{2,1,0:T(8,128)S(1)}, u32[]{:S(2)}, u32[]{:S(2)}) collective-permute-start(f32[2,8,128]{2,1,0:T(8,128)S(1)} %get-tuple-element.32), channel_id=1, source_target_pairs={{0,31},{1,24},{2,25},{3,26},{4,27},{5,28},{6,29},{7,30},{8,7},{9,0... | collective-permute-start | bytes 24584 | tf_op jit(solution)/shard_map/ppermute | solution.py:764
  58.2 4.7 %collective-permute-start.8 = (f32[2,8,128]{2,1,0:T(8,128)S(1)}, f32[2,8,128]{2,1,0:T(8,128)S(1)}, u32[]{:S(2)}, u32[]{:S(2)}) collective-permute-start(f32[2,8,128]{2,1,0:T(8,128)S(1)} %get-tuple-element.32), channel_id=1, source_target_pairs={{0,15},{1,8},{2,9},{3,10},{4,11},{5,12},{6,13},{7,14},{8,23},{9,16... | collective-permute-start | bytes 24584 | tf_op jit(solution)/shard_map/ppermute | solution.py:764
  60.5 2.4 %collective-permute-start.7 = (f32[2,8,128]{2,1,0:T(8,128)S(1)}, f32[2,8,128]{2,1,0:T(8,128)S(1)}, u32[]{:S(2)}, u32[]{:S(2)}) collective-permute-start(f32[2,8,128]{2,1,0:T(8,128)S(1)} %get-tuple-element.32), channel_id=1, source_target_pairs={{0,7},{1,0},{2,1},{3,2},{4,3},{5,4},{6,5},{7,6},{8,15},{9,8},{10,9... | collective-permute-start | bytes 24584 | tf_op jit(solution)/shard_map/ppermute | solution.py:764
